TPU v7x, 32 devices: a whole 2x2x4 slice. The times are simulated.
32 devices in a mesh: grp: 2 (over y), seq: 4 (over z), ch: 4 (over x, core).
Axes of the slice: x: 2, y: 2, z: 4, core: 2. Of those that a mesh axis runs over, the one named last changes fastest.
Arguments:
- activations: bfloat16 [4096, 1024], P('ch', ('grp', 'seq')), parts along dimension 1, may hold values from -6 to 6
- projection: bfloat16 [4096, 2048], P('seq', 'ch'), may hold values from -0.09375 to 0.09375
- medium_taps: float32 [2048, 128], P('ch'), may hold values from -0.5 to 0.5
- long_filters: bfloat16 [2048, 512], P('ch', 'seq'), may hold values from -0.25 to 0.25
- cotangent: bfloat16 [2048, 1024], P('ch', ('grp', 'seq')), parts along dimension 1, may hold values from -6 to 6
Outputs:
- conv_out: bfloat16 [2048, 1024], P('ch', ('grp', 'seq')), parts along dimension 1
- input_grad: bfloat16 [4096, 1024], P('ch', ('grp', 'seq')), parts along dimension 1
There are 2 independent parts, one for each index of `grp`. A program takes and returns all parts, laid end to end along the dimension named above; an argument that names none is the same for every part. Nothing has to cross between parts.
All inputs are finite; a program needn't handle non-finite values.
Results may differ from a plain program's by a relative error of at most 0.012.
Values may be sent and summed in bfloat16 or wider, within the bound.
No kernel may reach another device: no remote copies, remote signals or barrier semaphores. Data moves between devices by JAX's collectives and lax.ppermute only.
A program may use at most 64 MiB of HBM per device.

v0:
```python
import math

import jax
import jax.numpy as jnp
from jax import lax
from jax.sharding import PartitionSpec as P

exact_mode = lax.Precision.HIGH


def medium_forward(padded, tap_weights, length):
    tap_count = tap_weights.shape[1]
    summed = jnp.zeros((padded.shape[0], length), jnp.float32)
    for offset in range(tap_count):
        begin_col = tap_count - 1 - offset
        summed = (
            summed + tap_weights[:, offset : offset + 1] * padded[:, begin_col : begin_col + length]
        )
    return summed


def medium_backward(padded, tap_weights, length):
    tap_count = tap_weights.shape[1]
    summed = jnp.zeros((padded.shape[0], length), jnp.float32)
    for offset in range(tap_count):
        summed = summed + tap_weights[:, offset : offset + 1] * padded[:, offset : offset + length]
    return summed


def dft_tables(length):
    points = 2 * length
    columns = 128
    row_count = points // columns
    half_rows = row_count // 2
    freq_rows = jnp.arange(row_count, dtype=jnp.int32)
    time_rows = jnp.arange(half_rows, dtype=jnp.int32)
    lane_index = jnp.arange(columns, dtype=jnp.int32)
    angle_first = (
        2.0
        * math.pi
        / row_count
        * (freq_rows[:, None] * time_rows[None, :] % row_count).astype(jnp.float32)
    )
    angle_twist = (
        2.0
        * math.pi
        / points
        * (freq_rows[:, None] * lane_index[None, :] % points).astype(jnp.float32)
    )
    angle_last = (
        2.0
        * math.pi
        / columns
        * (lane_index[:, None] * lane_index[None, :] % columns).astype(jnp.float32)
    )
    return (
        jnp.cos(angle_first),
        jnp.sin(angle_first),
        jnp.cos(angle_twist),
        jnp.sin(angle_twist),
        jnp.cos(angle_last),
        jnp.sin(angle_last),
    )


def forward_dft(signal, tables):
    cos_first, sin_first, cos_twist, sin_twist, cos_last, sin_last = tables
    channels = signal.shape[0]
    shaped = signal.reshape(channels, cos_first.shape[1], 128)
    section_re = jnp.einsum("kn,cnq->ckq", cos_first, shaped, precision=exact_mode)
    section_im = -jnp.einsum("kn,cnq->ckq", sin_first, shaped, precision=exact_mode)
    twist_re = section_re * cos_twist + section_im * sin_twist
    twist_im = section_im * cos_twist - section_re * sin_twist
    spec_re = jnp.einsum("ckq,qm->ckm", twist_re, cos_last, precision=exact_mode) + jnp.einsum(
        "ckq,qm->ckm", twist_im, sin_last, precision=exact_mode
    )
    spec_im = jnp.einsum("ckq,qm->ckm", twist_im, cos_last, precision=exact_mode) - jnp.einsum(
        "ckq,qm->ckm", twist_re, sin_last, precision=exact_mode
    )
    return (spec_re, spec_im)


def inverse_dft(spec_re, spec_im, tables):
    cos_first, sin_first, cos_twist, sin_twist, cos_last, sin_last = tables
    channels = spec_re.shape[0]
    half_rows = cos_first.shape[1]
    inner_re = jnp.einsum("ckq,qm->ckm", spec_re, cos_last, precision=exact_mode) - jnp.einsum(
        "ckq,qm->ckm", spec_im, sin_last, precision=exact_mode
    )
    inner_im = jnp.einsum("ckq,qm->ckm", spec_im, cos_last, precision=exact_mode) + jnp.einsum(
        "ckq,qm->ckm", spec_re, sin_last, precision=exact_mode
    )
    turned_re = inner_re * cos_twist - inner_im * sin_twist
    turned_im = inner_im * cos_twist + inner_re * sin_twist
    output = jnp.einsum("kn,ckq->cnq", cos_first, turned_re, precision=exact_mode) - jnp.einsum(
        "kn,ckq->cnq", sin_first, turned_im, precision=exact_mode
    )
    points = 2 * half_rows * 128
    return (output / points).reshape(channels, half_rows * 128)


def causal_apply(signal, filt_re, filt_im, tables, conjugate):
    sig_re, sig_im = forward_dft(signal, tables)
    if conjugate:
        prod_re = sig_re * filt_re + sig_im * filt_im
        prod_im = sig_im * filt_re - sig_re * filt_im
    else:
        prod_re = sig_re * filt_re - sig_im * filt_im
        prod_im = sig_im * filt_re + sig_re * filt_im
    return inverse_dft(prod_re, prod_im, tables)


def on_device(activations, projection, medium_taps, long_filters, cotangent):
    tap_count = medium_taps.shape[1]
    whole_in = lax.all_gather(activations, "ch", axis=0, tiled=True)
    mixed_sum = lax.dot_general(
        lax.all_gather(projection, "seq", axis=0, tiled=True),
        whole_in,
        (((0,), (0,)), ((), ())),
        preferred_element_type=jnp.float32,
    )
    values = mixed_sum.astype(jnp.bfloat16)
    channel_count = values.shape[0] // lax.axis_size("seq")
    own_taps = lax.dynamic_slice_in_dim(
        medium_taps, lax.axis_index("seq") * channel_count, channel_count, 0
    )
    arrived, filters_ch = (
        lax.all_to_all(values, "seq", split_axis=0, concat_axis=1, tiled=True),
        lax.all_to_all(long_filters, "seq", split_axis=0, concat_axis=1, tiled=True),
    )
    tables = dft_tables(arrived.shape[1])
    filt_re, filt_im = forward_dft(filters_ch.astype(jnp.float32), tables)
    values_ch = arrived.astype(jnp.float32)
    padded_ch = jnp.pad(values_ch, ((0, 0), (tap_count - 1, 0)))
    conv_ch = medium_forward(padded_ch, own_taps, arrived.shape[1])
    gate_ch = jax.nn.sigmoid(values_ch)
    signal = lax.optimization_barrier((conv_ch * gate_ch).astype(jnp.bfloat16)).astype(jnp.float32)
    kept_state = (conv_ch, gate_ch)
    output_ch = causal_apply(signal, filt_re, filt_im, tables, False).astype(jnp.bfloat16)
    output_ch, context = (output_ch, (filt_re, filt_im, tables, kept_state))
    conv_out = lax.all_to_all(output_ch, "seq", split_axis=1, concat_axis=0, tiled=True)
    grad_ch = lax.all_to_all(cotangent, "seq", split_axis=0, concat_axis=1, tiled=True)
    filt_re, filt_im, tables, kept_state = context
    back_grad = lax.optimization_barrier(
        causal_apply(grad_ch.astype(jnp.float32), filt_re, filt_im, tables, True).astype(
            jnp.bfloat16
        )
    )
    conv_ch, gate_ch = kept_state
    grad_wide = back_grad.astype(jnp.float32)
    conv_grad = lax.optimization_barrier((grad_wide * gate_ch).astype(jnp.bfloat16)).astype(
        jnp.float32
    )
    padded_grad = jnp.pad(conv_grad, ((0, 0), (0, tap_count - 1)))
    through = medium_backward(padded_grad, own_taps, conv_grad.shape[1])
    gate_grad = grad_wide * conv_ch * gate_ch * (1.0 - gate_ch)
    back_ch = (through + gate_grad).astype(jnp.bfloat16)
    returned = lax.all_to_all(back_ch, "seq", split_axis=1, concat_axis=0, tiled=True)
    partial_grad = jnp.dot(
        lax.all_gather(projection, "seq", axis=0, tiled=True),
        returned,
        preferred_element_type=jnp.float32,
    )
    input_grad = lax.psum_scatter(
        partial_grad.astype(jnp.bfloat16), "ch", scatter_dimension=0, tiled=True
    )
    return (conv_out, input_grad)


def solution(mesh):
    return jax.shard_map(
        on_device,
        mesh=mesh,
        in_specs=(
            P("ch", ("grp", "seq")),
            P("seq", "ch"),
            P("ch", None),
            P("ch", "seq"),
            P("ch", ("grp", "seq")),
        ),
        out_specs=(P("ch", ("grp", "seq")), P("ch", ("grp", "seq"))),
        check_vma=False,
    )
```

profile of v0, /device:TPU:0, one launch (start us, length us, event | category | flops | bytes accessed | tf_op | source)
XLA Modules:
  0.0 196.6 jit_solution(1277242276180059869)
XLA Ops:
  8.7 6.4 %all-to-all-start.3 = ((bf16[4,128,128]{2,1,0:T(8,128)(2,1)}), bf16[4,128,128]{2,1,0:T(8,128)(2,1)S(1)}, u32[]{:S(2)}, u32[]{:S(2)}) async-start(bf16[4,128,128]{2,1,0:T(8,128)(2,1)} %bitcast.137), calls=%async_computation.3 | async-start | bytes 262144 | tf_op jit(solution)/shard_map/all_to_all | solution.py:142
  15.0 3.3 %dynamic-slice_reduce_fusion.121 = (f32[128]{0:T(128)S(1)}, f32[128]{0:T(128)S(1)}, f32[128]{0:T(128)}, f32[128]{0:T(128)}, f32[128]{0:T(128)}, /*index=5*/f32[1...) fusion(f32[512,128]{1,0:T(8,128)} %param.7, ...), kind=kLoop, calls=%fused_computation.996 | loop fusion | bytes 17480 | tf_op jit(solution)/shard_map/slice | solution.py:17
  18.3 2.2 %dynamic-slice_reduce_fusion.120 = (f32[128]{0:T(128)}, f32[128]{0:T(128)}, f32[128]{0:T(128)}, f32[128]{0:T(128)}, f32[128]{0:T(128)}, /*index=5*/f32[128]{0:T(128)}, f32[128]{0:T(128)}, f32[128]{0:T(128)}) fusion(f32[512,128]{1,0:T(8,128)} %param.7, s32[]{:T(128)S(6)} %select_n.123, s32[]{:T(128)S(6)} %add.1346, s32[]{:T(128)S(6)} %add.1352, ...), kind=kLoop, calls=%fused_computation.995 | loop fusion | bytes 8228 | tf_op jit(solution)/shard_map/slice | solution.py:17
  20.5 1.3 dynamic-slice_reduce_fusion.122
  21.8 1.3 dynamic-slice_reduce_fusion.123
  23.1 1.3 dynamic-slice_reduce_fusion.124
  24.3 1.3 dynamic-slice_reduce_fusion.125
  25.6 1.3 dynamic-slice_reduce_fusion.126
  26.9 1.3 dynamic-slice_reduce_fusion.127
  28.3 5.1 %all-to-all-start.1 = ((bf16[4,128,128]{2,1,0:T(8,128)(2,1)}), bf16[4,128,128]{2,1,0:T(8,128)(2,1)S(1)}, u32[]{:S(2)}, u32[]{:S(2)}) async-start(bf16[4,128,128]{2,1,0:T(8,128)(2,1)} %bitcast.11), calls=%async_computation.1 | async-start | bytes 262144 | tf_op jit(solution)/shard_map/all_to_all | solution.py:129
  34.1 5.1 %all-to-all-done.1 = bf16[4,128,128]{2,1,0:T(8,128)(2,1)S(1)} async-done(((bf16[4,128,128]{2,1,0:T(8,128)(2,1)}), bf16[4,128,128]{2,1,0:T(8,128)(2,1)S(1)}, u32[]{:S(2)}, u32[]{:S(2)}) %all-to-all-start.1) | async-done | bytes 131104 | tf_op jit(solution)/shard_map/all_to_all | solution.py:129
  44.4 67.0 %all-gather.3.cloned.1.call-done = bf16[4096,512]{1,0:T(8,128)(2,1)} async-done(((bf16[1024,512]{1,0:T(8,128)(2,1)}), bf16[4096,512]{1,0:T(8,128)(2,1)}) %all-gather.3.cloned.1.call-update) | async-done | bytes 4194320 | tf_op jit(solution)/shard_map/all_gather | solution.py:117
  111.3 3.8 %convolution_convert_fusion.1 = bf16[512,128]{1,0:T(8,128)(2,1)S(1)} fusion(bf16[4096,512]{1,0:T(8,128)(2,1)} %all-gather.3.cloned.1.call-done, bf16[4096,128]{1,0:T(8,128)(2,1)} %all-gather.5.cloned.1.call-done), kind=kOutput, calls=%fused_computation.275 | convolution fusion | flops 536936448 | bytes 5373952 | tf_op jit(solution)/shard_map/dot_general | solution.py:116
  115.9 3.3 %all-to-all-start = ((bf16[4,128,128]{1,2,0:T(8,128)(2,1)}), bf16[4,128,128]{1,2,0:T(8,128)(2,1)S(1)}, u32[]{:S(2)}, u32[]{:S(2)}) async-start(bf16[4,128,128]{1,2,0:T(8,128)(2,1)} %copy.57), calls=%async_computation | async-start | bytes 262144 | tf_op jit(solution)/shard_map/all_to_all | solution.py:128
  119.3 1.4 fusion.33
  120.7 4.6 %all-to-all-done = bf16[4,128,128]{1,2,0:T(8,128)(2,1)S(1)} async-done(((bf16[4,128,128]{1,2,0:T(8,128)(2,1)}), bf16[4,128,128]{1,2,0:T(8,128)(2,1)S(1)}, u32[]{:S(2)}, u32[]{:S(2)}) %all-to-all-start) | async-done | bytes 131104 | tf_op jit(solution)/shard_map/all_to_all | solution.py:128
  125.7 7.3 %multiply_convert_fusion = (bf16[128,512]{0,1:T(8,128)(2,1)S(1)}, f32[128,512]{0,1:T(8,128)S(1)}) fusion(bf16[4,128,128]{1,2,0:T(8,128)(2,1)S(1)} %all-to-all-done, f32[128]{0:T(128)S(1)} %copy-done.23, f32[128]{0:T(128)} %get-tuple-element.9, f32[128]{0:T(128)} %get-tuple-element.10, f32[128]{0:T(128)} %get-tuple-element.11, f32[128]{0:T(128)} %get-tuple-element.12, ...), kind=kLoop, calls=%fused_computation.856 | loop fusion | flops 17104896 | bytes 851968 | tf_op jit(solution)/shard_map/convert_element_type | solution.py:137
  136.6 1.8 multiply_add_fusion
  138.4 0.8 fusion.25
  139.2 0.8 fusion.21
  140.1 0.8 convolution_subtract_fusion
  140.9 0.8 convolution_add_fusion
  142.8 7.5 %fusion.55 = bf16[128,512]{0,1:T(8,128)(2,1)S(1)} fusion(f32[128,512]{0,1:T(8,128)S(1)} %get-tuple-element.137, bf16[128,512]{0,1:T(8,128)(2,1)S(1)} %copy.83, f32[128,512]{0,1:T(8,128)S(1)} %convert_element_type.181, f32[128]{0:T(128)} %get-tuple-element.135, f32[128]{0:T(128)} %get-tuple-element.9, f32[128]{0:T(128)} %get-tuple-element.10, ...), kind=kLoop, calls=%fused_computation.339 | loop fusion | flops 17432576 | bytes 983040 | tf_op jit(solution)/shard_map/convert_element_type | solution.py:157
  150.4 8.6 %all_to_all.80 = bf16[128,4,128]{2,0,1:T(8,128)(2,1)S(1)} all-to-all(bf16[128,4,128]{2,0,1:T(8,128)(2,1)S(1)} %copy.84), channel_id=1, replica_groups=mesh['grp'=2,'seq'=4,'ch'=4] {'seq'}, dimensions={1} | all-to-all | bytes 262144 | tf_op jit(solution)/shard_map/all_to_all | solution.py:158
  159.0 4.7 %fusion = bf16[4096,128]{0,1:T(8,128)(2,1)} fusion(bf16[512,128]{1,0:T(8,128)(2,1)S(1)} %bitcast.136, bf16[4096,512]{1,0:T(8,128)(2,1)} %all-gather.3.cloned.1.call-done), kind=kOutput, calls=%fused_computation.1 | convolution fusion | flops 537395200 | bytes 5373952 | tf_op jit(solution)/shard_map/dot_general | solution.py:159
  163.7 0.8 fusion.27
  164.5 0.8 fusion.31
  165.4 0.8 convolution_add_fusion.2
  166.2 0.8 convolution_subtract_fusion.2
  167.9 8.4 %all_to_all.81 = bf16[128,4,128]{2,0,1:T(8,128)(2,1)S(1)} all-to-all(bf16[128,4,128]{2,0,1:T(8,128)(2,1)S(1)} %copy.73), channel_id=1, replica_groups=mesh['grp'=2,'seq'=4,'ch'=4] {'seq'}, dimensions={1} | all-to-all | bytes 262144 | tf_op jit(solution)/shard_map/all_to_all | solution.py:141
  176.3 11.3 %reduce-scatter.2.cloned.1.call-done = bf16[1024,128]{0,1:T(8,128)(2,1)} async-done(((bf16[4096,128]{0,1:T(8,128)(2,1)}), bf16[1024,128]{0,1:T(8,128)(2,1)}) %reduce-scatter.2.cloned.1.call-update) | async-done | bytes 262160 | tf_op jit(solution)/shard_map/reduce_scatter | solution.py:164
  187.6 1.8 copy.85
  (121 shorter events, 14.2 us)
Async XLA Ops:
  7.2 37.2 %all-gather.5.cloned.1.call-start = ((), (), s32[]{:S(2)}) async-start(), calls=%async_computation.7 | async-start | bytes 1310720 | tf_op jit(solution)/shard_map/all_gather | solution.py:115
  7.9 103.4 %all-gather.3.cloned.1.call-start = ((), (), s32[]{:S(2)}) async-start(), calls=%async_computation.6 | async-start | bytes 5242880 | tf_op jit(solution)/shard_map/all_gather | solution.py:117
  8.7 19.6 %all-to-all-start.3 = ((bf16[4,128,128]{2,1,0:T(8,128)(2,1)}), bf16[4,128,128]{2,1,0:T(8,128)(2,1)S(1)}, u32[]{:S(2)}, u32[]{:S(2)}) async-start(bf16[4,128,128]{2,1,0:T(8,128)(2,1)} %bitcast.137), calls=%async_computation.3 | async-start | bytes 262144 | tf_op jit(solution)/shard_map/all_to_all | solution.py:142
  28.3 11.0 %all-to-all-start.1 = ((bf16[4,128,128]{2,1,0:T(8,128)(2,1)}), bf16[4,128,128]{2,1,0:T(8,128)(2,1)S(1)}, u32[]{:S(2)}, u32[]{:S(2)}) async-start(bf16[4,128,128]{2,1,0:T(8,128)(2,1)} %bitcast.11), calls=%async_computation.1 | async-start | bytes 262144 | tf_op jit(solution)/shard_map/all_to_all | solution.py:129
  43.9 81.4 %copy-start.1 = (f32[128]{0:T(128)S(1)}, f32[128]{0:T(128)}, u32[]{:S(2)}) copy-start(f32[128]{0:T(128)} %get-tuple-element.113) | copy-start | bytes 1540
  43.9 81.4 %copy-start.2 = (f32[128]{0:T(128)S(1)}, f32[128]{0:T(128)}, u32[]{:S(2)}) copy-start(f32[128]{0:T(128)} %get-tuple-element.114) | copy-start | bytes 1540
  44.0 81.4 %copy-start.3 = (f32[128]{0:T(128)S(1)}, f32[128]{0:T(128)}, u32[]{:S(2)}) copy-start(f32[128]{0:T(128)} %get-tuple-element.115) | copy-start | bytes 1540
  44.0 81.4 %copy-start.4 = (f32[128]{0:T(128)S(1)}, f32[128]{0:T(128)}, u32[]{:S(2)}) copy-start(f32[128]{0:T(128)} %get-tuple-element.116) | copy-start | bytes 1540
  44.0 81.4 %copy-start.5 = (f32[128]{0:T(128)S(1)}, f32[128]{0:T(128)}, u32[]{:S(2)}) copy-start(f32[128]{0:T(128)} %get-tuple-element.117) | copy-start | bytes 1540
  44.0 81.4 %copy-start.6 = (f32[128]{0:T(128)S(1)}, f32[128]{0:T(128)}, u32[]{:S(2)}) copy-start(f32[128]{0:T(128)} %get-tuple-element.118) | copy-start | bytes 1540
  44.0 81.4 %copy-start.7 = (f32[128]{0:T(128)S(1)}, f32[128]{0:T(128)}, u32[]{:S(2)}) copy-start(f32[128]{0:T(128)} %get-tuple-element.119) | copy-start | bytes 1540
  44.0 81.4 %copy-start.8 = (f32[128]{0:T(128)S(1)}, f32[128]{0:T(128)}, u32[]{:S(2)}) copy-start(f32[128]{0:T(128)} %get-tuple-element.120) | copy-start | bytes 1540
  44.0 81.4 %copy-start.9 = (f32[128]{0:T(128)S(1)}, f32[128]{0:T(128)}, u32[]{:S(2)}) copy-start(f32[128]{0:T(128)} %get-tuple-element.121) | copy-start | bytes 1540
  44.0 81.4 %copy-start.10 = (f32[128]{0:T(128)S(1)}, f32[128]{0:T(128)}, u32[]{:S(2)}) copy-start(f32[128]{0:T(128)} %get-tuple-element.122) | copy-start | bytes 1540
  44.0 81.4 %copy-start.11 = (f32[128]{0:T(128)S(1)}, f32[128]{0:T(128)}, u32[]{:S(2)}) copy-start(f32[128]{0:T(128)} %get-tuple-element.123) | copy-start | bytes 1540
  44.0 81.4 %copy-start.12 = (f32[128]{0:T(128)S(1)}, f32[128]{0:T(128)}, u32[]{:S(2)}) copy-start(f32[128]{0:T(128)} %get-tuple-element.124) | copy-start | bytes 1540
  44.1 81.4 %copy-start.13 = (f32[128]{0:T(128)S(1)}, f32[128]{0:T(128)}, u32[]{:S(2)}) copy-start(f32[128]{0:T(128)} %get-tuple-element.125) | copy-start | bytes 1540
  44.1 81.4 %copy-start.14 = (f32[128]{0:T(128)S(1)}, f32[128]{0:T(128)}, u32[]{:S(2)}) copy-start(f32[128]{0:T(128)} %get-tuple-element.126) | copy-start | bytes 1540
  44.1 81.4 %copy-start.15 = (f32[128]{0:T(128)S(1)}, f32[128]{0:T(128)}, u32[]{:S(2)}) copy-start(f32[128]{0:T(128)} %get-tuple-element.127) | copy-start | bytes 1540
  44.1 81.4 %copy-start.16 = (f32[128]{0:T(128)S(1)}, f32[128]{0:T(128)}, u32[]{:S(2)}) copy-start(f32[128]{0:T(128)} %get-tuple-element.128) | copy-start | bytes 1540
  44.1 81.4 %copy-start.17 = (f32[128]{0:T(128)S(1)}, f32[128]{0:T(128)}, u32[]{:S(2)}) copy-start(f32[128]{0:T(128)} %get-tuple-element.129) | copy-start | bytes 1540
  44.1 81.4 %copy-start.18 = (f32[128]{0:T(128)S(1)}, f32[128]{0:T(128)}, u32[]{:S(2)}) copy-start(f32[128]{0:T(128)} %get-tuple-element.130) | copy-start | bytes 1540
  44.1 81.4 %copy-start.19 = (f32[128]{0:T(128)S(1)}, f32[128]{0:T(128)}, u32[]{:S(2)}) copy-start(f32[128]{0:T(128)} %get-tuple-element.131) | copy-start | bytes 1540
  44.1 81.4 %copy-start.20 = (f32[128]{0:T(128)S(1)}, f32[128]{0:T(128)}, u32[]{:S(2)}) copy-start(f32[128]{0:T(128)} %get-tuple-element.132) | copy-start | bytes 1540
  44.1 81.4 %copy-start.21 = (f32[128]{0:T(128)S(1)}, f32[128]{0:T(128)}, u32[]{:S(2)}) copy-start(f32[128]{0:T(128)} %get-tuple-element.133) | copy-start | bytes 1540
  44.2 81.4 %copy-start.22 = (f32[128]{0:T(128)S(1)}, f32[128]{0:T(128)}, u32[]{:S(2)}) copy-start(f32[128]{0:T(128)} %get-tuple-element.134) | copy-start | bytes 1540
  44.2 81.4 %copy-start.23 = (f32[128]{0:T(128)S(1)}, f32[128]{0:T(128)}, u32[]{:S(2)}) copy-start(f32[128]{0:T(128)} %get-tuple-element.135) | copy-start | bytes 1540
  44.2 81.4 %copy-start.24 = (f32[128]{0:T(128)S(1)}, f32[128]{0:T(128)}, u32[]{:S(2)}) copy-start(f32[128]{0:T(128)} %get-tuple-element.94) | copy-start | bytes 1540
  44.2 81.4 %copy-start.25 = (f32[128]{0:T(128)S(1)}, f32[128]{0:T(128)}, u32[]{:S(2)}) copy-start(f32[128]{0:T(128)} %get-tuple-element.95) | copy-start | bytes 1540
  44.2 81.4 %copy-start.26 = (f32[128]{0:T(128)S(1)}, f32[128]{0:T(128)}, u32[]{:S(2)}) copy-start(f32[128]{0:T(128)} %get-tuple-element.96) | copy-start | bytes 1540
  115.9 9.4 %all-to-all-start = ((bf16[4,128,128]{1,2,0:T(8,128)(2,1)}), bf16[4,128,128]{1,2,0:T(8,128)(2,1)S(1)}, u32[]{:S(2)}, u32[]{:S(2)}) async-start(bf16[4,128,128]{1,2,0:T(8,128)(2,1)} %copy.57), calls=%async_computation | async-start | bytes 262144 | tf_op jit(solution)/shard_map/all_to_all | solution.py:128
  119.2 68.4 %reduce-scatter.2.cloned.1.call-start = ((), (), s32[]{:S(2)}) async-start(), calls=%async_computation.8 | async-start | bytes 1310720 | tf_op jit(solution)/shard_map/reduce_scatter | solution.py:164
  (15 other events, 1152.3 us)
Sparse Core Ops, SparseCore 0:
  9.5 19.4 all-gather.4
  30.6 80.7 all-gather.2
  163.8 23.7 reduce-scatter.1
where the time goes:
time: 197 us
  waiting for transfers between devices  89.4 us (45%)
  matrix products  28.7 us (15%)
  local copies, waits for them, and re-layouts  17 us (9%)
  blocking collectives  17 us (9%)
  other arithmetic  15 us (8%)
  starting transfers between devices  14.9 us (8%)
  between operations  14.7 us (7%)
    all_gather x1, waiting for transfers between devices, on_device(): lax.all_gather(projection, 'seq', axis=0, tiled=True)  67 us
    slice x8, local copies, waits for them, and re-layouts, medium_forward(): tap_weights[:, offset:offset + 1] * padded[:, begin_col:begin_col + length]  13.2 us
    reduce_scatter x1, waiting for transfers between devices, on_device(): lax.psum_scatter(partial_grad.astype(jnp.bfloat16), 'ch', scatter_dimensi...  11.3 us
    all_to_all x1, blocking collectives, on_device(): lax.all_to_all(back_ch, 'seq', split_axis=1, concat_axis=0, tiled=True)  8.57 us
    all_to_all x1, blocking collectives, on_device(): lax.all_to_all(output_ch, 'seq', split_axis=1, concat_axis=0, tiled=True)  8.41 us
    convert_element_type x1, other arithmetic, on_device(): back_ch = (through + gate_grad).astype(jnp.bfloat16)  7.47 us
    convert_element_type x1, other arithmetic, on_device(): (conv_ch * gate_ch).astype(jnp.bfloat16)  7.34 us
    all_to_all x1, starting transfers between devices, on_device(): lax.all_to_all(cotangent, 'seq', split_axis=0, concat_axis=1, tiled=True)  6.36 us
  transfers between devices with their start and end apart: 6, of which 4 were waited for; matrix products, arithmetic and copies ran while one was open for 12% of the time, Pallas kernels for 0%

commit v1 on v0

--- a/solution.py
+++ b/solution.py
@@ -1,11 +1,345 @@
+import functools
 import math
 
 import jax
 import jax.numpy as jnp
 from jax import lax
+from jax.experimental import pallas as pl
+from jax.experimental.pallas import tpu as pltpu
 from jax.sharding import PartitionSpec as P
 
 exact_mode = lax.Precision.HIGH
+F32 = jnp.float32
+BF16 = jnp.bfloat16
+
+
+def reverse_bits(value, count):
+    out = 0
+    for bit in range(count):
+        out = out | (((value >> bit) & 1) << (count - 1 - bit))
+    return out
+
+
+def block_tables(size):
+    steps = jnp.arange(size, dtype=jnp.int32)
+    turns = (4 * steps[None, :] + 1) * steps[:, None] % (4 * size)
+    angle = (2.0 * math.pi / (4 * size)) * turns.astype(F32)
+    cos, sin = jnp.cos(angle), jnp.sin(angle)
+
+    def parts(table):
+        high = table.astype(BF16)
+        return high, (table - high.astype(F32)).astype(BF16)
+
+    forward = jnp.concatenate([cos, -sin], axis=1)
+    inverse = jnp.concatenate([cos.T, -sin.T], axis=0) / size
+    return (
+        jnp.concatenate(parts(forward), axis=0),
+        jnp.concatenate(parts(inverse), axis=1),
+    )
+
+
+def matmul(left, right):
+    return jnp.dot(left, right, preferred_element_type=F32)
+
+
+def to_spectrum(rows, table):
+    size = rows.shape[1]
+    out = matmul(jnp.concatenate([rows, rows], axis=1), table)
+    return out[:, :size], out[:, size:]
+
+
+def from_spectrum(real, imag, table):
+    size = real.shape[1]
+    both = jnp.concatenate([real, imag], axis=1)
+    high = both.astype(BF16)
+    low = (both - high.astype(F32)).astype(BF16)
+    out = matmul(high, table)
+    return out[:, :size] + out[:, size:] + matmul(low, table[:, :size])
+
+
+def split_rows(array, count):
+    step = array.shape[0] // count
+    return [array[i * step : (i + 1) * step] for i in range(count)]
+
+
+def prepare_kernel(n, index_ref, *refs):
+    given, (taps_ref, table_ref, inverse_ref) = refs[:n], refs[n : n + 3]
+    grad_ref, filt_ref, tap_ref, filters, cotangents = refs[n + 3 :]
+    s = index_ref[0]
+    size = taps_ref.shape[1]
+    for r in range(n):
+        filters[s ^ r] = given[r][0]
+        cotangents[s ^ r] = given[r][1]
+    table = table_ref[...]
+    filt_re, filt_im = to_spectrum(filters[...].reshape(n * size, size), table)
+    cot_re, cot_im = to_spectrum(cotangents[...].reshape(n * size, size), table)
+    filt_ref[:, :size] = filt_re
+    filt_ref[:, size:] = filt_im
+    taps = taps_ref[pl.ds(pl.multiple_of(s * size, size), size), :]
+    taps_high = taps.astype(BF16)
+    taps_low = (taps - taps_high.astype(F32)).astype(BF16)
+    tap_re, tap_im = to_spectrum(taps_high, table)
+    rest = matmul(taps_low, table[:size])
+    tap_ref[:, :size] = tap_re + rest[:, :size]
+    tap_ref[:, size:] = tap_im + rest[:, size:]
+    fr, fi = split_rows(filt_re, n), split_rows(filt_im, n)
+    cr, ci = split_rows(cot_re, n), split_rows(cot_im, n)
+    turned = []
+    for b in range(n):
+        if b + 1 < n:
+            turned.append((cr[b] + ci[b + 1], ci[b] - cr[b + 1]))
+        else:
+            turned.append((cr[b], ci[b]))
+    real, imag = [], []
+    for b in range(n):
+        re, im = 0.0, 0.0
+        for d in range(n - b):
+            vr, vi = turned[b + d]
+            re = re + fr[d] * vr + fi[d] * vi
+            im = im + fr[d] * vi - fi[d] * vr
+        real.append(re)
+        imag.append(im)
+    out = from_spectrum(jnp.concatenate(real), jnp.concatenate(imag), inverse_ref[...])
+    grad_ref[...] = out.astype(BF16).reshape(n, size, size)
+
+
+def gate_kernel(n, index_ref, *refs):
+    sums = refs[: 2 * n]
+    grad_in_ref, tap_ref, table_ref, inverse_ref = refs[2 * n : 2 * n + 4]
+    far_ref, near_ref, gated_ref, held = refs[2 * n + 4 :]
+    c = index_ref[1]
+    half, size = n // 2, tap_ref.shape[0]
+    bits = n.bit_length() - 1
+    for part in range(2):
+        total = sums[part * n][...].astype(F32)
+        for r in range(1, n):
+            total = total + sums[part * n + r][...].astype(F32)
+        for j in range(half):
+            held[c ^ (part * half + j)] = total[j].astype(BF16)
+    values = held[...].reshape(n * size, size)
+    table, inverse = table_ref[...], inverse_ref[...]
+    tr, ti = tap_ref[:, :size], tap_ref[:, size:]
+    wide = values.astype(F32)
+    gate = 1.0 / (1.0 + jnp.exp(-wide))
+    grad = grad_in_ref[...].reshape(n * size, size).astype(F32)
+    grad_medium = (grad * gate).astype(BF16)
+    re, im = to_spectrum(values, table)
+    gr, gi = to_spectrum(grad_medium, table)
+    re, im, gr, gi = (split_rows(x, n) for x in (re, im, gr, gi))
+    real, imag, back_real, back_imag = [], [], [], []
+    for b in range(n):
+        ur, ui = (re[b] - im[b - 1], im[b] + re[b - 1]) if b else (re[b], im[b])
+        real.append(tr * ur - ti * ui)
+        imag.append(tr * ui + ti * ur)
+        vr, vi = (gr[b] + gi[b + 1], gi[b] - gr[b + 1]) if b + 1 < n else (gr[b], gi[b])
+        back_real.append(tr * vr + ti * vi)
+        back_imag.append(tr * vi - ti * vr)
+    medium = from_spectrum(jnp.concatenate(real), jnp.concatenate(imag), inverse)
+    through = from_spectrum(jnp.concatenate(back_real), jnp.concatenate(back_imag), inverse)
+    gated_ref[...] = (medium * gate).astype(BF16).reshape(n, size, size)
+    back = (through + grad * medium * gate * (1.0 - gate)).astype(BF16)
+    held[...] = back.reshape(n, size, size)
+    for j in range(half):
+        near_ref[j] = held[reverse_bits(c ^ j, bits)]
+        far_ref[j] = held[reverse_bits(c ^ (half + j), bits)]
+
+
+def long_kernel(n, index_ref, gated_ref, filt_ref, table_ref, inverse_ref, *refs):
+    outs, held = refs[:n], refs[n]
+    s = index_ref[0]
+    size = gated_ref.shape[2]
+    re, im = to_spectrum(gated_ref[...].reshape(n * size, size), table_ref[...])
+    re, im = split_rows(re, n), split_rows(im, n)
+    fr, fi = split_rows(filt_ref[:, :size], n), split_rows(filt_ref[:, size:], n)
+    turned = [(re[0], im[0])]
+    for b in range(1, n):
+        turned.append((re[b] - im[b - 1], im[b] + re[b - 1]))
+    real, imag = [], []
+    for b in range(n):
+        zr, zi = 0.0, 0.0
+        for d in range(b + 1):
+            ur, ui = turned[b - d]
+            zr = zr + fr[d] * ur - fi[d] * ui
+            zi = zi + fr[d] * ui + fi[d] * ur
+        real.append(zr)
+        imag.append(zi)
+    out = from_spectrum(jnp.concatenate(real), jnp.concatenate(imag), inverse_ref[...])
+    held[...] = out.astype(BF16).reshape(n, size, size)
+    for r in range(n):
+        outs[r][...] = held[s ^ r]
+
+
+def place_kernel(n, index_ref, *refs):
+    given, out_ref = refs[:n], refs[n]
+    s = index_ref[0]
+    size = given[0].shape[0]
+    for r in range(n):
+        out_ref[pl.ds(pl.multiple_of((s ^ r) * size, size), size), :] = given[r][...]
+
+
+def values_kernel(n, weight_ref, *refs):
+    acts, outs = refs[: n // 2], refs[n // 2 :]
+    size = acts[0].shape[1]
+    right = jnp.concatenate([ref[...] for ref in acts], axis=1)
+    step = weight_ref.shape[0] // n
+    for r in range(n):
+        out = matmul(weight_ref[r * step : (r + 1) * step, :], right).astype(BF16)
+        for j in range(n // 2):
+            outs[r][j] = out[:, j * size : (j + 1) * size]
+
+
+def input_kernel(n, weight_ref, *refs):
+    grads, outs = refs[:n], refs[n:]
+    half = n // 2
+    size = grads[0].shape[2]
+    right = jnp.concatenate(
+        [jnp.concatenate([ref[j] for j in range(half)], axis=1) for ref in grads], axis=0
+    )
+    out = matmul(weight_ref[...], right)
+    for j in range(half):
+        outs[j][...] = out[:, j * size : (j + 1) * size].astype(outs[j].dtype)
+
+
+def call(kernel, outs, scratch, index, args, flops):
+    sizes = sum(math.prod(a.shape) * a.dtype.itemsize for a in (*args, *outs))
+    specs = [pl.BlockSpec(memory_space=pltpu.VMEM)] * len(args)
+    if index is not None:
+        specs = [pl.BlockSpec(memory_space=pltpu.SMEM)] + specs
+        args = (index, *args)
+    return pl.pallas_call(
+        kernel,
+        out_shape=tuple(outs),
+        in_specs=specs,
+        out_specs=tuple(pl.BlockSpec(memory_space=pltpu.VMEM) for _ in outs),
+        scratch_shapes=scratch,
+        cost_estimate=pl.CostEstimate(flops=flops, bytes_accessed=sizes, transcendentals=0),
+    )(*args)
+
+
+def square_plan(n, activations, projection, medium_taps, long_filters, cotangent):
+    bits = n.bit_length() - 1
+    half = n // 2
+    depth, size = activations.shape
+    own = projection.shape[1] // n
+    s, c = lax.axis_index("seq"), lax.axis_index("ch")
+    index = jnp.stack([s, c]).astype(jnp.int32)
+    shape = jax.ShapeDtypeStruct
+
+    def move(array, target):
+        pairs = [
+            (i * n + j, (lambda t: t[0] * n + t[1])(target(i, j)))
+            for i in range(n)
+            for j in range(n)
+        ]
+        return lax.ppermute(array, ("seq", "ch"), pairs)
+
+    def across_seq(array, r):
+        return move(array, lambda i, j: (i ^ r, j))
+
+    def across_ch(array, r):
+        return move(array, lambda i, j: (i, j ^ r))
+
+    def gather_low(block):
+        held = [block]
+        while len(held) < half:
+            step = len(held)
+            held = held + [across_ch(x, step) for x in held]
+        return held
+
+    own_act = move(activations, lambda i, j: (j, i))
+
+    both = jnp.stack([long_filters, cotangent]).reshape(2, n, own, size)
+    blocks = [lax.dynamic_index_in_dim(both, s ^ r, 1, False) for r in range(n)]
+    blocks = [blocks[0]] + [across_seq(blocks[r], r) for r in range(1, n)]
+
+    columns = [
+        lax.dynamic_slice_in_dim(projection, (s ^ r) * own, own, 1) for r in range(n)
+    ]
+    weight = jnp.concatenate(columns, axis=1)
+    weight, weight_t = lax.optimization_barrier((weight, weight.T))
+    table, inverse = lax.optimization_barrier(block_tables(size))
+
+    def values_of(acts):
+        outs = [shape((half, own, size), BF16)] * n
+        parts = call(
+            functools.partial(values_kernel, n),
+            outs,
+            [],
+            None,
+            (weight_t, *acts),
+            2 * depth * n * own * half * size,
+        )
+        return [parts[0]] + [across_seq(parts[r], r) for r in range(1, n)]
+
+    far_act = across_ch(own_act, half)
+    near_sums = values_of(gather_low(own_act))
+    far_sums = values_of(gather_low(far_act))
+
+    spectrum = 4 * n * size * 2 * size * own
+    grad_gated, filt, tap = call(
+        functools.partial(prepare_kernel, n),
+        [shape((n, own, size), BF16), shape((n * own, 2 * size), F32), shape((own, 2 * size), F32)],
+        [pltpu.VMEM((n, own, size), BF16), pltpu.VMEM((n, own, size), BF16)],
+        index,
+        (*blocks, medium_taps, table, inverse),
+        6 * spectrum,
+    )
+    far, near, gated = call(
+        functools.partial(gate_kernel, n),
+        [shape((half, own, size), BF16), shape((half, own, size), BF16), shape((n, own, size), BF16)],
+        [pltpu.VMEM((n, own, size), BF16)],
+        index,
+        (*near_sums, *far_sums, grad_gated, tap, table, inverse),
+        8 * spectrum,
+    )
+
+    def gathered(part):
+        return [part] + [across_seq(part, r) for r in range(1, n)]
+
+    far_parts = gathered(far)
+    near_parts = gathered(near)
+
+    out_blocks = call(
+        functools.partial(long_kernel, n),
+        [shape((own, size), BF16)] * n,
+        [pltpu.VMEM((n, own, size), BF16)],
+        index,
+        (gated, filt, table, inverse),
+        4 * spectrum,
+    )
+    out_blocks = [out_blocks[0]] + [across_seq(out_blocks[r], r) for r in range(1, n)]
+
+    def input_of(parts):
+        outs = [shape((depth, size), F32 if j < max(half // 2, 1) else BF16) for j in range(half)]
+        return call(
+            functools.partial(input_kernel, n),
+            outs,
+            [],
+            None,
+            (weight, *parts),
+            2 * depth * n * own * half * size,
+        )
+
+    def scatter_low(sums):
+        while len(sums) > 1:
+            step = len(sums) // 2
+            kept = sums[:step]
+            sent = [across_ch(x.astype(BF16), step) for x in sums[step:]]
+            sums = [a.astype(F32) + b.astype(F32) for a, b in zip(kept, sent)]
+        return sums[0]
+
+    far_total = across_ch(scatter_low(list(input_of(far_parts))).astype(BF16), half)
+    total = scatter_low(list(input_of(near_parts))) + far_total.astype(F32)
+    input_grad = move(total.astype(BF16), lambda i, j: (reverse_bits(j, bits), i))
+    (conv_out,) = call(
+        functools.partial(place_kernel, n),
+        [shape((n * own, size), BF16)],
+        [],
+        index,
+        tuple(out_blocks),
+        0,
+    )
+    return conv_out, input_grad
 
 
 def medium_forward(padded, tap_weights, length):
@@ -168,8 +502,24 @@
 
 
 def solution(mesh):
+    seq, ch = mesh.shape["seq"], mesh.shape["ch"]
+
+    def step(*args):
+        activations, projection, medium_taps = args[:3]
+        size = activations.shape[1]
+        square = (
+            seq == ch
+            and seq > 1
+            and seq & (seq - 1) == 0
+            and medium_taps.shape[1] == size
+            and projection.shape[0] == activations.shape[0]
+            and projection.shape[1] == seq * size
+            and size % 128 == 0
+        )
+        return square_plan(seq, *args) if square else on_device(*args)
+
     return jax.shard_map(
-        on_device,
+        step,
         mesh=mesh,
         in_specs=(
             P("ch", ("grp", "seq")),

time: 197 us -> 109 us (0.55)
  waiting for transfers between devices: 89.4 us -> 30.1 us
  starting transfers between devices: 14.9 us -> 45.6 us
  matrix products: 28.7 us -> 0 us
  Pallas kernels: 0 us -> 19.1 us
  blocking collectives: 17 us -> 0 us
  between operations: 14.7 us -> 0.88 us
  other arithmetic: 15 us -> 4.83 us
  local copies, waits for them, and re-layouts: 17 us -> 7.77 us
    all_gather x2 -> x0, waiting for transfers between devices: 67 us -> none  [the longest x1 67 us: on_device(): lax.all_gather(projection, 'seq', axis=0, tiled=True)]
    ppermute x0 -> x26, starting transfers between devices: none -> 45.6 us  [move(): return lax.ppermute(array, ('seq', 'ch'), pairs)]
    ppermute x0 -> x26, waiting for transfers between devices: none -> 30.1 us  [move(): return lax.ppermute(array, ('seq', 'ch'), pairs)]
    dot_general x32 -> x0, matrix products: 28.7 us -> none  [the longest x1 4.65 us: on_device(): jnp.dot(lax.all_gather(projection, 'seq', axis=0, tiled=True), returned,...]
    pallas_call x0 -> x8, Pallas kernels: none -> 19.1 us  [call(): pl.pallas_call(kernel, out_shape=tuple(outs), in_specs=specs, out_specs=t...]
    all_to_all x2 -> x0, blocking collectives: 17 us -> none  [the longest x1 8.57 us: on_device(): lax.all_to_all(back_ch, 'seq', split_axis=1, concat_axis=0, tiled=True)]
    convert_element_type x5, other arithmetic: 14.9 us -> 0.18 us  [the longest x1 0.09 us: square_plan(): total.astype(BF16)]
    all_to_all x3 -> x0, starting transfers between devices: 14.7 us -> none  [the longest x1 6.36 us: on_device(): lax.all_to_all(cotangent, 'seq', split_axis=0, concat_axis=1, tiled=True)]
  transfers between devices with their start and end apart: 6 -> 26, of which waited for: 4 -> 9; matrix products, arithmetic and copies ran while one was open for 12% -> 7% of each run, Pallas kernels for 0% -> 13%
where the time goes in v1:
time: 109 us; the launch traced here: 108 us
  starting transfers between devices  45.6 us (42%)
  waiting for transfers between devices  30.1 us (28%)
  Pallas kernels  19.1 us (18%)
  local copies, waits for them, and re-layouts  7.77 us (7%)
  other arithmetic  4.83 us (4%)
    ppermute x26, starting transfers between devices, move(): return lax.ppermute(array, ('seq', 'ch'), pairs)  45.6 us
    ppermute x26, waiting for transfers between devices, move(): return lax.ppermute(array, ('seq', 'ch'), pairs)  30.1 us
    pallas_call x8, Pallas kernels, call(): pl.pallas_call(kernel, out_shape=tuple(outs), in_specs=specs, out_specs=t...  19.1 us
    unnamed x53, local copies, waits for them, and re-layouts  5.16 us
  transfers between devices with their start and end apart: 26, of which 9 were waited for; matrix products, arithmetic and copies ran while one was open for 7% of the time, Pallas kernels for 13%

profile of v1, /device:TPU:0, one launch (start us, length us, event | category | flops | bytes accessed | tf_op | source)
XLA Modules:
  0.0 108.3 jit_solution(18385462897822729989)
XLA Ops:
  0.6 1.6 %collective-permute-start = (bf16[1024,128]{1,0:T(8,128)(2,1)}, bf16[1024,128]{1,0:T(8,128)(2,1)S(1)}, u32[]{:S(2)}, u32[]{:S(2)}) collective-permute-start(bf16[1024,128]{1,0:T(8,128)(2,1)} %param.5), channel_id=1, source_target_pairs={{0,0},{1,4},{2,8},{3,12},{4,1},{5,5},{6,9},{7,13},{8,2},{9,6},{10,... | collective-permute-start | bytes 786440 | tf_op jit(solution)/shard_map/ppermute | solution.py:234
  2.2 1.5 %fusion.9 = (bf16[2,128,128]{2,1,0:T(8,128)(2,1)S(1)}, bf16[2,128,128]{2,1,0:T(8,128)(2,1)}, bf16[2,128,128]{2,1,0:T(8,128)(2,1)S(1)}, bf16[2,128,128]{2,1,0:T(8,128)(2,1)S(1)}) fusion(s32[]{:T(128)S(6)} %select_n.47, bf16[1,4,128,128]{3,2,0,1:T(8,128)(2,1)} %bitcast.18, bf16[1,4,128,128]{3,2,0,1:T(8,128)(2,1)} %bitcast.19, s32[]{:T(128)S(6)} %select_n.44, ...), kind=kLoop, calls=%fused_computation.32 | loop fusion | flops 131072 | bytes 524304 | tf_op jit(solution)/shard_map/jit(dynamic_index_in_dim)/squeeze | solution.py:252
  3.8 3.4 %collective-permute-start.10 = (bf16[2,128,128]{2,1,0:T(8,128)(2,1)S(1)}, bf16[2,128,128]{2,1,0:T(8,128)(2,1)S(1)}, u32[]{:S(2)}, u32[]{:S(2)}) collective-permute-start(bf16[2,128,128]{2,1,0:T(8,128)(2,1)S(1)} %get-tuple-element.62), channel_id=1, source_target_pairs={{0,4},{1,5},{2,6},{3,7},{4,0},{5,1},{6,2},{7,3},{8,12},{9,13},{10,... | collective-permute-start | bytes 196616 | tf_op jit(solution)/shard_map/ppermute | solution.py:234
  7.2 3.2 %collective-permute-start.11 = (bf16[2,128,128]{2,1,0:T(8,128)(2,1)S(1)}, bf16[2,128,128]{2,1,0:T(8,128)(2,1)S(1)}, u32[]{:S(2)}, u32[]{:S(2)}) collective-permute-start(bf16[2,128,128]{2,1,0:T(8,128)(2,1)S(1)} %get-tuple-element.63), channel_id=1, source_target_pairs={{0,8},{1,9},{2,10},{3,11},{4,12},{5,13},{6,14},{7,15},{8,0},{9,1},... | collective-permute-start | bytes 196616 | tf_op jit(solution)/shard_map/ppermute | solution.py:234
  10.9 1.3 %constant_dynamic-slice_fusion.3 = (bf16[1024,128]{1,0:T(8,128)(2,1)S(1)}, bf16[1024,128]{1,0:T(8,128)(2,1)S(1)}, bf16[1024,128]{1,0:T(8,128)(2,1)S(1)}, bf16[1024,128]{1,0:T(8,128)(2,1)S(1)}) fusion(bf16[1024,512]{1,0:T(8,128)(2,1)} %param.6, s32[]{:T(128)S(6)} %select_n.40, s32[]{:T(128)S(6)} %select_n.41, s32[]{:T(128)S(6)} %select_n.43, s32[]{:T(128)S(6)} %select_n.42), kind=kLoop, calls=%fused_computation.52 | loop fusion | bytes 2097168 | tf_op jit(solution)/shard_map/dynamic_slice | solution.py:256
  12.8 12.3 %collective-permute-start.5 = (bf16[1024,128]{1,0:T(8,128)(2,1)S(1)}, bf16[1024,128]{1,0:T(8,128)(2,1)S(1)}, u32[]{:S(2)}, u32[]{:S(2)}) collective-permute-start(bf16[1024,128]{1,0:T(8,128)(2,1)S(1)} %collective-permute-done.refs_0_), channel_id=1, source_target_pairs={{0,2},{1,3},{2,0},{3,1},{4,6},{5,7},{6,4},{7,5},{8,10},{9,11},{10,... | collective-permute-start | bytes 786440 | tf_op jit(solution)/shard_map/ppermute | solution.py:234
  25.1 1.2 %fusion.24 = (bf16[512,1024]{0,1:T(8,128)(2,1)S(1)}, bf16[1024,512]{1,0:T(8,128)(2,1)}) fusion(bf16[1024,128]{1,0:T(8,128)(2,1)S(1)} %get-tuple-element.58, bf16[1024,128]{1,0:T(8,128)(2,1)S(1)} %get-tuple-element.59, bf16[1024,128]{1,0:T(8,128)(2,1)S(1)} %get-tuple-element.57, bf16[1024,128]{1,0:T(8,128)(2,1)S(1)} %get-tuple-element.56), kind=kLoop, calls=%fused_computation.55 | loop fusion | flops 4194304 | bytes 3145728 | tf_op jit(solution)/shard_map/transpose | solution.py:259
  26.3 3.2 %collective-permute-done.5.refs_0_ = bf16[1024,128]{1,0:T(8,128)(2,1)S(1)} collective-permute-done((bf16[1024,128]{1,0:T(8,128)(2,1)S(1)}, bf16[1024,128]{1,0:T(8,128)(2,1)S(1)}, u32[]{:S(2)}, u32[]{:S(2)}) %collective-permute-start.5) | collective-permute-done | bytes 262176 | tf_op jit(solution)/shard_map/ppermute | solution.py:234
  29.4 1.3 %copy.7.weight_ref = bf16[512,1024]{1,0:T(8,128)(2,1)} copy(bf16[512,1024]{0,1:T(8,128)(2,1)S(1)} %get-tuple-element.28) | data formatting | bytes 2097152 | tf_op jit(solution)/shard_map/optimization_barrier | solution.py:259
  31.5 2.4 %shard_map.68 = (bf16[2,128,128]{2,1,0:T(8,128)(2,1)}, bf16[2,128,128]{2,1,0:T(8,128)(2,1)}, bf16[2,128,128]{2,1,0:T(8,128)(2,1)}, bf16[2,128,128]{2,1,0:T(8,128)(2,1)}) custom-call(bf16[512,1024]{1,0:T(8,128)(2,1)} %copy.7.weight_ref, bf16[1024,128]{1,0:T(8,128)(2,1)} %copy-done.2, bf16[1024,128]{1,0:T(8,128)(2,1)} %copy-done.5), custom_call_target="tpu_custom_call" | custom-call | flops 268435456 | bytes 1835008 | tf_op jit(solution)/shard_map/pallas_call | solution.py:209
  35.8 1.8 %collective-permute-start.3 = (bf16[2,128,128]{2,1,0:T(8,128)(2,1)}, bf16[2,128,128]{2,1,0:T(8,128)(2,1)S(1)}, u32[]{:S(2)}, u32[]{:S(2)}) collective-permute-start(bf16[2,128,128]{2,1,0:T(8,128)(2,1)} %get-tuple-element.31), channel_id=1, source_target_pairs={{0,8},{1,9},{2,10},{3,11},{4,12},{5,13},{6,14},{7,15},{8,0},{9,1},... | collective-permute-start | bytes 196616 | tf_op jit(solution)/shard_map/ppermute | solution.py:234
  37.6 2.4 %shard_map.69 = (bf16[2,128,128]{2,1,0:T(8,128)(2,1)}, bf16[2,128,128]{2,1,0:T(8,128)(2,1)}, bf16[2,128,128]{2,1,0:T(8,128)(2,1)}, bf16[2,128,128]{2,1,0:T(8,128)(2,1)}) custom-call(bf16[512,1024]{1,0:T(8,128)(2,1)} %copy.7.weight_ref, bf16[1024,128]{1,0:T(8,128)(2,1)} %copy-done.3, bf16[1024,128]{1,0:T(8,128)(2,1)} %copy-done.4), custom_call_target="tpu_custom_call" | custom-call | flops 268435456 | bytes 1835008 | tf_op jit(solution)/shard_map/pallas_call | solution.py:209
  40.1 2.2 %collective-permute-start.4 = (bf16[2,128,128]{2,1,0:T(8,128)(2,1)S(1)}, bf16[2,128,128]{2,1,0:T(8,128)(2,1)S(1)}, u32[]{:S(2)}, u32[]{:S(2)}) collective-permute-start(bf16[2,128,128]{2,1,0:T(8,128)(2,1)S(1)} %copy-done.20), channel_id=1, source_target_pairs={{0,12},{1,13},{2,14},{3,15},{4,8},{5,9},{6,10},{7,11},{8,4},{9,5},... | collective-permute-start | bytes 196616 | tf_op jit(solution)/shard_map/ppermute | solution.py:234
  42.3 2.2 %collective-permute-start.8 = (bf16[2,128,128]{2,1,0:T(8,128)(2,1)}, bf16[2,128,128]{2,1,0:T(8,128)(2,1)S(1)}, u32[]{:S(2)}, u32[]{:S(2)}) collective-permute-start(bf16[2,128,128]{2,1,0:T(8,128)(2,1)} %get-tuple-element.35), channel_id=1, source_target_pairs={{0,8},{1,9},{2,10},{3,11},{4,12},{5,13},{6,14},{7,15},{8,0},{9,1},... | collective-permute-start | bytes 196616 | tf_op jit(solution)/shard_map/ppermute | solution.py:234
  44.5 2.2 %collective-permute-start.9 = (bf16[2,128,128]{2,1,0:T(8,128)(2,1)}, bf16[2,128,128]{2,1,0:T(8,128)(2,1)S(1)}, u32[]{:S(2)}, u32[]{:S(2)}) collective-permute-start(bf16[2,128,128]{2,1,0:T(8,128)(2,1)} %get-tuple-element.36), channel_id=1, source_target_pairs={{0,12},{1,13},{2,14},{3,15},{4,8},{5,9},{6,10},{7,11},{8,4},{9,5},... | collective-permute-start | bytes 196616 | tf_op jit(solution)/shard_map/ppermute | solution.py:234
  47.4 2.5 %shard_map.70 = (bf16[4,128,128]{2,1,0:T(8,128)(2,1)}, f32[512,256]{1,0:T(8,128)}, f32[128,256]{1,0:T(8,128)}) custom-call(s32[2]{0:T(128)} %pad_add_fusion.index_ref, bf16[2,128,128]{2,1,0:T(8,128)(2,1)} %get-tuple-element.61.refs_0_, bf16[2,128,128]{2,1,0:T(8,128)(2,1)} %copy-done.16, bf16[2,128,128]{2,1,0:T(8,128)(2,1)} %copy-done.17, ...), custom_call_target="tpu_custom_call" | custom-call | flops 402653184 | bytes 1572864 | tf_op jit(solution)/shard_map/pallas_call | solution.py:209
  49.9 1.7 %collective-permute-done.8.refs_6_ = bf16[2,128,128]{2,1,0:T(8,128)(2,1)S(1)} collective-permute-done((bf16[2,128,128]{2,1,0:T(8,128)(2,1)}, bf16[2,128,128]{2,1,0:T(8,128)(2,1)S(1)}, u32[]{:S(2)}, u32[]{:S(2)}) %collective-permute-start.8) | collective-permute-done | bytes 65568 | tf_op jit(solution)/shard_map/ppermute | solution.py:234
  52.3 2.7 %shard_map.71 = (bf16[2,128,128]{2,1,0:T(8,128)(2,1)}, bf16[2,128,128]{2,1,0:T(8,128)(2,1)}, bf16[4,128,128]{2,1,0:T(8,128)(2,1)}) custom-call(s32[2]{0:T(128)} %pad_add_fusion.index_ref, bf16[2,128,128]{2,1,0:T(8,128)(2,1)} %get-tuple-element.29.refs_0_, bf16[2,128,128]{2,1,0:T(8,128)(2,1)} %copy-done.19, bf16[2,128,128]{2,1,0:T(8,128)(2,1)} %copy-done.21, ...), custom_call_target="tpu_custom_call" | custom-call | flops 536870912 | bytes 1310720 | tf_op jit(solution)/shard_map/pallas_call | solution.py:209
  55.0 1.5 %collective-permute-start.20 = (bf16[2,128,128]{2,1,0:T(8,128)(2,1)}, bf16[2,128,128]{2,1,0:T(8,128)(2,1)S(1)}, u32[]{:S(2)}, u32[]{:S(2)}) collective-permute-start(bf16[2,128,128]{2,1,0:T(8,128)(2,1)} %get-tuple-element.51.refs_0_), channel_id=1, source_target_pairs={{0,4},{1,5},{2,6},{3,7},{4,0},{5,1},{6,2},{7,3},{8,12},{9,13},{10,... | collective-permute-start | bytes 196616 | tf_op jit(solution)/shard_map/ppermute | solution.py:234
  57.6 1.9 %collective-permute-start.22 = (bf16[2,128,128]{2,1,0:T(8,128)(2,1)}, bf16[2,128,128]{2,1,0:T(8,128)(2,1)S(1)}, u32[]{:S(2)}, u32[]{:S(2)}) collective-permute-start(bf16[2,128,128]{2,1,0:T(8,128)(2,1)} %get-tuple-element.51.refs_0_), channel_id=1, source_target_pairs={{0,12},{1,13},{2,14},{3,15},{4,8},{5,9},{6,10},{7,11},{8,4},{9,5},... | collective-permute-start | bytes 196616 | tf_op jit(solution)/shard_map/ppermute | solution.py:234
  59.6 4.7 %collective-permute-done.21.refs_2_ = bf16[2,128,128]{2,1,0:T(8,128)(2,1)S(1)} collective-permute-done((bf16[2,128,128]{2,1,0:T(8,128)(2,1)}, bf16[2,128,128]{2,1,0:T(8,128)(2,1)S(1)}, u32[]{:S(2)}, u32[]{:S(2)}) %collective-permute-start.21) | collective-permute-done | bytes 65568 | tf_op jit(solution)/shard_map/ppermute | solution.py:234
  65.5 2.6 %shard_map.75 = (f32[1024,128]{1,0:T(8,128)}, bf16[1024,128]{1,0:T(8,128)(2,1)}) custom-call(bf16[1024,512]{1,0:T(8,128)(2,1)} %get-tuple-element.47.weight_ref, bf16[2,128,128]{2,1,0:T(8,128)(2,1)} %get-tuple-element.51.refs_0_, bf16[2,128,128]{2,1,0:T(8,128)(2,1)} %copy-done.8, bf16[2,128,128]{2,1,0:T(8,128)(2,1)} %copy-done.10, ...), custom_call_target="tpu_custom_call" | custom-call | flops 268435456 | bytes 2097152 | tf_op jit(solution)/shard_map/pallas_call | solution.py:209
  69.7 2.9 %collective-permute-start.18 = (bf16[2,128,128]{2,1,0:T(8,128)(2,1)S(1)}, bf16[2,128,128]{2,1,0:T(8,128)(2,1)S(1)}, u32[]{:S(2)}, u32[]{:S(2)}) collective-permute-start(bf16[2,128,128]{2,1,0:T(8,128)(2,1)S(1)} %copy-done.6), channel_id=1, source_target_pairs={{0,12},{1,13},{2,14},{3,15},{4,8},{5,9},{6,10},{7,11},{8,4},{9,5},... | collective-permute-start | bytes 196616 | tf_op jit(solution)/shard_map/ppermute | solution.py:234
  73.4 4.1 %collective-permute-done.17.refs_2_ = bf16[2,128,128]{2,1,0:T(8,128)(2,1)S(1)} collective-permute-done((bf16[2,128,128]{2,1,0:T(8,128)(2,1)S(1)}, bf16[2,128,128]{2,1,0:T(8,128)(2,1)S(1)}, u32[]{:S(2)}, u32[]{:S(2)}) %collective-permute-start.17) | collective-permute-done | bytes 65568 | tf_op jit(solution)/shard_map/ppermute | solution.py:234
  78.7 2.6 %shard_map.74 = (f32[1024,128]{1,0:T(8,128)}, bf16[1024,128]{1,0:T(8,128)(2,1)}) custom-call(bf16[1024,512]{1,0:T(8,128)(2,1)} %get-tuple-element.47.weight_ref, bf16[2,128,128]{2,1,0:T(8,128)(2,1)} %get-tuple-element.48.refs_0_, bf16[2,128,128]{2,1,0:T(8,128)(2,1)} %copy-done.7, bf16[2,128,128]{2,1,0:T(8,128)(2,1)} %copy-done.9, bf16[2,128,128]{2,1,0:T(8,128)(2,1)} %copy-done.11), custom_call_target="tpu_custom_call" | custom-call | flops 268435456 | bytes 2097152 | tf_op jit(solution)/shard_map/pallas_call | solution.py:209
  81.5 1.6 %collective-permute-done.19 = bf16[1024,128]{1,0:T(8,128)(2,1)S(1)} collective-permute-done((bf16[1024,128]{1,0:T(8,128)(2,1)}, bf16[1024,128]{1,0:T(8,128)(2,1)S(1)}, u32[]{:S(2)}, u32[]{:S(2)}) %collective-permute-start.19) | collective-permute-done | bytes 262176 | tf_op jit(solution)/shard_map/ppermute | solution.py:234
  83.1 7.1 %collective-permute-done.24 = bf16[1024,128]{1,0:T(8,128)(2,1)S(1)} collective-permute-done((bf16[1024,128]{1,0:T(8,128)(2,1)S(1)}, bf16[1024,128]{1,0:T(8,128)(2,1)S(1)}, u32[]{:S(2)}, u32[]{:S(2)}) %collective-permute-start.24) | collective-permute-done | bytes 262176 | tf_op jit(solution)/shard_map/ppermute | solution.py:234
  91.0 2.3 %shard_map.72 = (bf16[128,128]{1,0:T(8,128)(2,1)}, bf16[128,128]{1,0:T(8,128)(2,1)}, bf16[128,128]{1,0:T(8,128)(2,1)}, bf16[128,128]{1,0:T(8,128)(2,1)}) custom-call(s32[2]{0:T(128)} %pad_add_fusion.index_ref, bf16[4,128,128]{2,1,0:T(8,128)(2,1)} %get-tuple-element.41.gated_ref, f32[512,256]{1,0:T(8,128)} %get-tuple-element.42.filt_ref, ...), custom_call_target="tpu_custom_call" | custom-call | flops 268435456 | bytes 1048576 | tf_op jit(solution)/shard_map/pallas_call | solution.py:209
  93.3 2.5 %collective-permute-start.13 = (bf16[128,128]{1,0:T(8,128)(2,1)}, bf16[128,128]{1,0:T(8,128)(2,1)S(1)}, u32[]{:S(2)}, u32[]{:S(2)}) collective-permute-start(bf16[128,128]{1,0:T(8,128)(2,1)} %get-tuple-element.44), channel_id=1, source_target_pairs={{0,4},{1,5},{2,6},{3,7},{4,0},{5,1},{6,2},{7,3},{8,12},{9,13},{10,... | collective-permute-start | bytes 98312 | tf_op jit(solution)/shard_map/ppermute | solution.py:234
  95.8 2.4 %collective-permute-start.14 = (bf16[128,128]{1,0:T(8,128)(2,1)}, bf16[128,128]{1,0:T(8,128)(2,1)S(1)}, u32[]{:S(2)}, u32[]{:S(2)}) collective-permute-start(bf16[128,128]{1,0:T(8,128)(2,1)} %get-tuple-element.45), channel_id=1, source_target_pairs={{0,8},{1,9},{2,10},{3,11},{4,12},{5,13},{6,14},{7,15},{8,0},{9,1},... | collective-permute-start | bytes 98312 | tf_op jit(solution)/shard_map/ppermute | solution.py:234
  98.6 6.9 %collective-permute-done.13.refs_1_ = bf16[128,128]{1,0:T(8,128)(2,1)S(1)} collective-permute-done((bf16[128,128]{1,0:T(8,128)(2,1)}, bf16[128,128]{1,0:T(8,128)(2,1)S(1)}, u32[]{:S(2)}, u32[]{:S(2)}) %collective-permute-start.13) | collective-permute-done | bytes 32800 | tf_op jit(solution)/shard_map/ppermute | solution.py:234
  106.1 1.5 %shard_map.73 = bf16[512,128]{1,0:T(8,128)(2,1)} custom-call(s32[2]{0:T(128)} %pad_add_fusion.index_ref, bf16[128,128]{1,0:T(8,128)(2,1)} %get-tuple-element.43.refs_0_, bf16[128,128]{1,0:T(8,128)(2,1)} %copy-done.13, bf16[128,128]{1,0:T(8,128)(2,1)} %copy-done.14, bf16[128,128]{1,0:T(8,128)(2,1)} %copy-done.15), custom_call_target="tpu_custom_call" | custom-call | bytes 262144 | tf_op jit(solution)/shard_map/pallas_call | solution.py:209
  (94 shorter events, 13.7 us)
Async XLA Ops:
  0.6 12.1 %collective-permute-start = (bf16[1024,128]{1,0:T(8,128)(2,1)}, bf16[1024,128]{1,0:T(8,128)(2,1)S(1)}, u32[]{:S(2)}, u32[]{:S(2)}) collective-permute-start(bf16[1024,128]{1,0:T(8,128)(2,1)} %param.5), channel_id=1, source_target_pairs={{0,0},{1,4},{2,8},{3,12},{4,1},{5,5},{6,9},{7,13},{8,2},{9,6},{10,... | collective-permute-start | bytes 786440 | tf_op jit(solution)/shard_map/ppermute | solution.py:234
  3.8 36.3 %collective-permute-start.10 = (bf16[2,128,128]{2,1,0:T(8,128)(2,1)S(1)}, bf16[2,128,128]{2,1,0:T(8,128)(2,1)S(1)}, u32[]{:S(2)}, u32[]{:S(2)}) collective-permute-start(bf16[2,128,128]{2,1,0:T(8,128)(2,1)S(1)} %get-tuple-element.62), channel_id=1, source_target_pairs={{0,4},{1,5},{2,6},{3,7},{4,0},{5,1},{6,2},{7,3},{8,12},{9,13},{10,... | collective-permute-start | bytes 196616 | tf_op jit(solution)/shard_map/ppermute | solution.py:234
  7.2 35.1 %collective-permute-start.11 = (bf16[2,128,128]{2,1,0:T(8,128)(2,1)S(1)}, bf16[2,128,128]{2,1,0:T(8,128)(2,1)S(1)}, u32[]{:S(2)}, u32[]{:S(2)}) collective-permute-start(bf16[2,128,128]{2,1,0:T(8,128)(2,1)S(1)} %get-tuple-element.63), channel_id=1, source_target_pairs={{0,8},{1,9},{2,10},{3,11},{4,12},{5,13},{6,14},{7,15},{8,0},{9,1},... | collective-permute-start | bytes 196616 | tf_op jit(solution)/shard_map/ppermute | solution.py:234
  10.3 32.0 %collective-permute-start.12 = (bf16[2,128,128]{2,1,0:T(8,128)(2,1)S(1)}, bf16[2,128,128]{2,1,0:T(8,128)(2,1)S(1)}, u32[]{:S(2)}, u32[]{:S(2)}) collective-permute-start(bf16[2,128,128]{2,1,0:T(8,128)(2,1)S(1)} %get-tuple-element.60), channel_id=1, source_target_pairs={{0,12},{1,13},{2,14},{3,15},{4,8},{5,9},{6,10},{7,11},{8,4},{9,5},... | collective-permute-start | bytes 196616 | tf_op jit(solution)/shard_map/ppermute | solution.py:234
  12.8 13.5 %copy-start.2 = (bf16[1024,128]{1,0:T(8,128)(2,1)}, bf16[1024,128]{1,0:T(8,128)(2,1)S(1)}, u32[]{:S(2)}) copy-start(bf16[1024,128]{1,0:T(8,128)(2,1)S(1)} %collective-permute-done.refs_0_) | copy-start | bytes 786436
  12.8 16.7 %collective-permute-start.5 = (bf16[1024,128]{1,0:T(8,128)(2,1)S(1)}, bf16[1024,128]{1,0:T(8,128)(2,1)S(1)}, u32[]{:S(2)}, u32[]{:S(2)}) collective-permute-start(bf16[1024,128]{1,0:T(8,128)(2,1)S(1)} %collective-permute-done.refs_0_), channel_id=1, source_target_pairs={{0,2},{1,3},{2,0},{3,1},{4,6},{5,7},{6,4},{7,5},{8,10},{9,11},{10,... | collective-permute-start | bytes 786440 | tf_op jit(solution)/shard_map/ppermute | solution.py:234
  26.3 4.5 %collective-permute-start.1 = (bf16[1024,128]{1,0:T(8,128)(2,1)S(1)}, bf16[1024,128]{1,0:T(8,128)(2,1)S(1)}, u32[]{:S(2)}, u32[]{:S(2)}) collective-permute-start(bf16[1024,128]{1,0:T(8,128)(2,1)S(1)} %collective-permute-done.refs_0_), channel_id=1, source_target_pairs={{0,1},{1,0},{2,3},{3,2},{4,5},{5,4},{6,7},{7,6},{8,9},{9,8},{10,11... | collective-permute-start | bytes 786440 | tf_op jit(solution)/shard_map/ppermute | solution.py:234
  29.4 6.4 %collective-permute-start.6 = (bf16[1024,128]{1,0:T(8,128)(2,1)S(1)}, bf16[1024,128]{1,0:T(8,128)(2,1)S(1)}, u32[]{:S(2)}, u32[]{:S(2)}) collective-permute-start(bf16[1024,128]{1,0:T(8,128)(2,1)S(1)} %collective-permute-done.5.refs_0_), channel_id=1, source_target_pairs={{0,1},{1,0},{2,3},{3,2},{4,5},{5,4},{6,7},{7,6},{8,9},{9,8},{10,11... | collective-permute-start | bytes 786440 | tf_op jit(solution)/shard_map/ppermute | solution.py:234
  34.0 10.6 %collective-permute-start.2 = (bf16[2,128,128]{2,1,0:T(8,128)(2,1)}, bf16[2,128,128]{2,1,0:T(8,128)(2,1)S(1)}, u32[]{:S(2)}, u32[]{:S(2)}) collective-permute-start(bf16[2,128,128]{2,1,0:T(8,128)(2,1)} %get-tuple-element.30), channel_id=1, source_target_pairs={{0,4},{1,5},{2,6},{3,7},{4,0},{5,1},{6,2},{7,3},{8,12},{9,13},{10,... | collective-permute-start | bytes 196616 | tf_op jit(solution)/shard_map/ppermute | solution.py:234
  35.8 14.1 %collective-permute-start.3 = (bf16[2,128,128]{2,1,0:T(8,128)(2,1)}, bf16[2,128,128]{2,1,0:T(8,128)(2,1)S(1)}, u32[]{:S(2)}, u32[]{:S(2)}) collective-permute-start(bf16[2,128,128]{2,1,0:T(8,128)(2,1)} %get-tuple-element.31), channel_id=1, source_target_pairs={{0,8},{1,9},{2,10},{3,11},{4,12},{5,13},{6,14},{7,15},{8,0},{9,1},... | collective-permute-start | bytes 196616 | tf_op jit(solution)/shard_map/ppermute | solution.py:234
  40.1 7.3 %copy-start.16 = (bf16[2,128,128]{2,1,0:T(8,128)(2,1)}, bf16[2,128,128]{2,1,0:T(8,128)(2,1)S(1)}, u32[]{:S(2)}) copy-start(bf16[2,128,128]{2,1,0:T(8,128)(2,1)S(1)} %collective-permute-done.10.refs_1_) | copy-start | bytes 196612
  40.1 9.8 %collective-permute-start.4 = (bf16[2,128,128]{2,1,0:T(8,128)(2,1)S(1)}, bf16[2,128,128]{2,1,0:T(8,128)(2,1)S(1)}, u32[]{:S(2)}, u32[]{:S(2)}) collective-permute-start(bf16[2,128,128]{2,1,0:T(8,128)(2,1)S(1)} %copy-done.20), channel_id=1, source_target_pairs={{0,12},{1,13},{2,14},{3,15},{4,8},{5,9},{6,10},{7,11},{8,4},{9,5},... | collective-permute-start | bytes 196616 | tf_op jit(solution)/shard_map/ppermute | solution.py:234
  42.3 7.6 %collective-permute-start.7 = (bf16[2,128,128]{2,1,0:T(8,128)(2,1)}, bf16[2,128,128]{2,1,0:T(8,128)(2,1)S(1)}, u32[]{:S(2)}, u32[]{:S(2)}) collective-permute-start(bf16[2,128,128]{2,1,0:T(8,128)(2,1)} %get-tuple-element.34), channel_id=1, source_target_pairs={{0,4},{1,5},{2,6},{3,7},{4,0},{5,1},{6,2},{7,3},{8,12},{9,13},{10,... | collective-permute-start | bytes 196616 | tf_op jit(solution)/shard_map/ppermute | solution.py:234
  42.3 9.3 %collective-permute-start.8 = (bf16[2,128,128]{2,1,0:T(8,128)(2,1)}, bf16[2,128,128]{2,1,0:T(8,128)(2,1)S(1)}, u32[]{:S(2)}, u32[]{:S(2)}) collective-permute-start(bf16[2,128,128]{2,1,0:T(8,128)(2,1)} %get-tuple-element.35), channel_id=1, source_target_pairs={{0,8},{1,9},{2,10},{3,11},{4,12},{5,13},{6,14},{7,15},{8,0},{9,1},... | collective-permute-start | bytes 196616 | tf_op jit(solution)/shard_map/ppermute | solution.py:234
  44.5 7.1 %copy-start.19 = (bf16[2,128,128]{2,1,0:T(8,128)(2,1)}, bf16[2,128,128]{2,1,0:T(8,128)(2,1)S(1)}, u32[]{:S(2)}) copy-start(bf16[2,128,128]{2,1,0:T(8,128)(2,1)S(1)} %collective-permute-done.2.refs_1_) | copy-start | bytes 196612
  44.5 7.1 %collective-permute-start.9 = (bf16[2,128,128]{2,1,0:T(8,128)(2,1)}, bf16[2,128,128]{2,1,0:T(8,128)(2,1)S(1)}, u32[]{:S(2)}, u32[]{:S(2)}) collective-permute-start(bf16[2,128,128]{2,1,0:T(8,128)(2,1)} %get-tuple-element.36), channel_id=1, source_target_pairs={{0,12},{1,13},{2,14},{3,15},{4,8},{5,9},{6,10},{7,11},{8,4},{9,5},... | collective-permute-start | bytes 196616 | tf_op jit(solution)/shard_map/ppermute | solution.py:234
  55.0 13.1 %copy-start.6 = (bf16[2,128,128]{2,1,0:T(8,128)(2,1)S(1)}, bf16[2,128,128]{2,1,0:T(8,128)(2,1)}, u32[]{:S(2)}) copy-start(bf16[2,128,128]{2,1,0:T(8,128)(2,1)} %get-tuple-element.48.refs_0_) | copy-start | bytes 196612
  55.0 4.5 %collective-permute-start.20 = (bf16[2,128,128]{2,1,0:T(8,128)(2,1)}, bf16[2,128,128]{2,1,0:T(8,128)(2,1)S(1)}, u32[]{:S(2)}, u32[]{:S(2)}) collective-permute-start(bf16[2,128,128]{2,1,0:T(8,128)(2,1)} %get-tuple-element.51.refs_0_), channel_id=1, source_target_pairs={{0,4},{1,5},{2,6},{3,7},{4,0},{5,1},{6,2},{7,3},{8,12},{9,13},{10,... | collective-permute-start | bytes 196616 | tf_op jit(solution)/shard_map/ppermute | solution.py:234
  56.5 7.8 %collective-permute-start.21 = (bf16[2,128,128]{2,1,0:T(8,128)(2,1)}, bf16[2,128,128]{2,1,0:T(8,128)(2,1)S(1)}, u32[]{:S(2)}, u32[]{:S(2)}) collective-permute-start(bf16[2,128,128]{2,1,0:T(8,128)(2,1)} %get-tuple-element.51.refs_0_), channel_id=1, source_target_pairs={{0,8},{1,9},{2,10},{3,11},{4,12},{5,13},{6,14},{7,15},{8,0},{9,1},... | collective-permute-start | bytes 196616 | tf_op jit(solution)/shard_map/ppermute | solution.py:234
  57.6 6.7 %collective-permute-start.22 = (bf16[2,128,128]{2,1,0:T(8,128)(2,1)}, bf16[2,128,128]{2,1,0:T(8,128)(2,1)S(1)}, u32[]{:S(2)}, u32[]{:S(2)}) collective-permute-start(bf16[2,128,128]{2,1,0:T(8,128)(2,1)} %get-tuple-element.51.refs_0_), channel_id=1, source_target_pairs={{0,12},{1,13},{2,14},{3,15},{4,8},{5,9},{6,10},{7,11},{8,4},{9,5},... | collective-permute-start | bytes 196616 | tf_op jit(solution)/shard_map/ppermute | solution.py:234
  68.2 13.2 %copy-start = (f32[1024,128]{1,0:T(8,128)S(1)}, f32[1024,128]{1,0:T(8,128)}, u32[]{:S(2)}) copy-start(f32[1024,128]{1,0:T(8,128)} %get-tuple-element.52) | copy-start | bytes 1572868
  68.2 13.2 %collective-permute-start.23 = (bf16[1024,128]{1,0:T(8,128)(2,1)}, bf16[1024,128]{1,0:T(8,128)(2,1)S(1)}, u32[]{:S(2)}, u32[]{:S(2)}) collective-permute-start(bf16[1024,128]{1,0:T(8,128)(2,1)} %get-tuple-element.53), channel_id=1, source_target_pairs={{0,1},{1,0},{2,3},{3,2},{4,5},{5,4},{6,7},{7,6},{8,9},{9,8},{10,11... | collective-permute-start | bytes 786440 | tf_op jit(solution)/shard_map/ppermute | solution.py:234
  68.2 5.2 %collective-permute-start.16 = (bf16[2,128,128]{2,1,0:T(8,128)(2,1)S(1)}, bf16[2,128,128]{2,1,0:T(8,128)(2,1)S(1)}, u32[]{:S(2)}, u32[]{:S(2)}) collective-permute-start(bf16[2,128,128]{2,1,0:T(8,128)(2,1)S(1)} %copy-done.6), channel_id=1, source_target_pairs={{0,4},{1,5},{2,6},{3,7},{4,0},{5,1},{6,2},{7,3},{8,12},{9,13},{10,... | collective-permute-start | bytes 196616 | tf_op jit(solution)/shard_map/ppermute | solution.py:234
  68.9 8.6 %collective-permute-start.17 = (bf16[2,128,128]{2,1,0:T(8,128)(2,1)S(1)}, bf16[2,128,128]{2,1,0:T(8,128)(2,1)S(1)}, u32[]{:S(2)}, u32[]{:S(2)}) collective-permute-start(bf16[2,128,128]{2,1,0:T(8,128)(2,1)S(1)} %copy-done.6), channel_id=1, source_target_pairs={{0,8},{1,9},{2,10},{3,11},{4,12},{5,13},{6,14},{7,15},{8,0},{9,1},... | collective-permute-start | bytes 196616 | tf_op jit(solution)/shard_map/ppermute | solution.py:234
  69.7 7.7 %collective-permute-start.18 = (bf16[2,128,128]{2,1,0:T(8,128)(2,1)S(1)}, bf16[2,128,128]{2,1,0:T(8,128)(2,1)S(1)}, u32[]{:S(2)}, u32[]{:S(2)}) collective-permute-start(bf16[2,128,128]{2,1,0:T(8,128)(2,1)S(1)} %copy-done.6), channel_id=1, source_target_pairs={{0,12},{1,13},{2,14},{3,15},{4,8},{5,9},{6,10},{7,11},{8,4},{9,5},... | collective-permute-start | bytes 196616 | tf_op jit(solution)/shard_map/ppermute | solution.py:234
  81.3 8.9 %copy-start.1 = (f32[1024,128]{1,0:T(8,128)S(1)}, f32[1024,128]{1,0:T(8,128)}, u32[]{:S(2)}) copy-start(f32[1024,128]{1,0:T(8,128)} %get-tuple-element.49) | copy-start | bytes 1572868
  81.3 1.7 %collective-permute-start.19 = (bf16[1024,128]{1,0:T(8,128)(2,1)}, bf16[1024,128]{1,0:T(8,128)(2,1)S(1)}, u32[]{:S(2)}, u32[]{:S(2)}) collective-permute-start(bf16[1024,128]{1,0:T(8,128)(2,1)} %get-tuple-element.50), channel_id=1, source_target_pairs={{0,1},{1,0},{2,3},{3,2},{4,5},{5,4},{6,7},{7,6},{8,9},{9,8},{10,11... | collective-permute-start | bytes 786440 | tf_op jit(solution)/shard_map/ppermute | solution.py:234
  81.4 8.8 %collective-permute-start.24 = (bf16[1024,128]{1,0:T(8,128)(2,1)S(1)}, bf16[1024,128]{1,0:T(8,128)(2,1)S(1)}, u32[]{:S(2)}, u32[]{:S(2)}) collective-permute-start(bf16[1024,128]{1,0:T(8,128)(2,1)S(1)} %add_convert_fusion.1), channel_id=1, source_target_pairs={{0,2},{1,3},{2,0},{3,1},{4,6},{5,7},{6,4},{7,5},{8,10},{9,11},{10,... | collective-permute-start | bytes 786440 | tf_op jit(solution)/shard_map/ppermute | solution.py:234
  90.3 17.4 %collective-permute-start.25 = (bf16[1024,128]{1,0:T(8,128)(2,1)S(1)}, bf16[1024,128]{1,0:T(8,128)(2,1)S(1)}, u32[]{:S(2)}, u32[]{:S(2)}) collective-permute-start(bf16[1024,128]{1,0:T(8,128)(2,1)S(1)} %add_convert_fusion), channel_id=1, source_target_pairs={{0,0},{1,8},{2,4},{3,12},{4,1},{5,9},{6,5},{7,13},{8,2},{9,10},{10... | collective-permute-start | bytes 786440 | tf_op jit(solution)/shard_map/ppermute | solution.py:234
  93.3 12.2 %collective-permute-start.13 = (bf16[128,128]{1,0:T(8,128)(2,1)}, bf16[128,128]{1,0:T(8,128)(2,1)S(1)}, u32[]{:S(2)}, u32[]{:S(2)}) collective-permute-start(bf16[128,128]{1,0:T(8,128)(2,1)} %get-tuple-element.44), channel_id=1, source_target_pairs={{0,4},{1,5},{2,6},{3,7},{4,0},{5,1},{6,2},{7,3},{8,12},{9,13},{10,... | collective-permute-start | bytes 98312 | tf_op jit(solution)/shard_map/ppermute | solution.py:234
  95.8 9.7 %collective-permute-start.14 = (bf16[128,128]{1,0:T(8,128)(2,1)}, bf16[128,128]{1,0:T(8,128)(2,1)S(1)}, u32[]{:S(2)}, u32[]{:S(2)}) collective-permute-start(bf16[128,128]{1,0:T(8,128)(2,1)} %get-tuple-element.45), channel_id=1, source_target_pairs={{0,8},{1,9},{2,10},{3,11},{4,12},{5,13},{6,14},{7,15},{8,0},{9,1},... | collective-permute-start | bytes 98312 | tf_op jit(solution)/shard_map/ppermute | solution.py:234
  98.1 7.4 %collective-permute-start.15 = (bf16[128,128]{1,0:T(8,128)(2,1)}, bf16[128,128]{1,0:T(8,128)(2,1)S(1)}, u32[]{:S(2)}, u32[]{:S(2)}) collective-permute-start(bf16[128,128]{1,0:T(8,128)(2,1)} %get-tuple-element.46), channel_id=1, source_target_pairs={{0,12},{1,13},{2,14},{3,15},{4,8},{5,9},{6,10},{7,11},{8,4},{9,5},... | collective-permute-start | bytes 98312 | tf_op jit(solution)/shard_map/ppermute | solution.py:234
  (20 other events, 38.8 us)

commit v2 on v1

--- a/solution.py
+++ b/solution.py
@@ -7,6 +7,7 @@
 from jax.experimental import pallas as pl
 from jax.experimental.pallas import tpu as pltpu
 from jax.sharding import PartitionSpec as P
+
 
 exact_mode = lax.Precision.HIGH
 F32 = jnp.float32
@@ -177,6 +178,19 @@
         out_ref[pl.ds(pl.multiple_of((s ^ r) * size, size), size), :] = given[r][...]
 
 
+def arrange_kernel(n, index_ref, given_ref, filters_ref, cotangent_ref, *refs):
+    weight_ref, turned_ref, blocks = refs[0], refs[1], refs[2:]
+    s = index_ref[0]
+    size = given_ref.shape[1] // n
+    for r in range(n):
+        start = pl.multiple_of((s ^ r) * size, size)
+        blocks[r][0] = filters_ref[pl.ds(start, size), :]
+        blocks[r][1] = cotangent_ref[pl.ds(start, size), :]
+        block = given_ref[:, pl.ds(start, size)]
+        weight_ref[:, r * size : (r + 1) * size] = block
+        turned_ref[r * size : (r + 1) * size, :] = block.T
+
+
 def values_kernel(n, weight_ref, *refs):
     acts, outs = refs[: n // 2], refs[n // 2 :]
     size = acts[0].shape[1]
@@ -202,6 +216,7 @@
 
 def call(kernel, outs, scratch, index, args, flops):
     sizes = sum(math.prod(a.shape) * a.dtype.itemsize for a in (*args, *outs))
+    held = sum(math.prod(a.shape) * jnp.dtype(a.dtype).itemsize for a in scratch)
     specs = [pl.BlockSpec(memory_space=pltpu.VMEM)] * len(args)
     if index is not None:
         specs = [pl.BlockSpec(memory_space=pltpu.SMEM)] + specs
@@ -213,6 +228,7 @@
         out_specs=tuple(pl.BlockSpec(memory_space=pltpu.VMEM) for _ in outs),
         scratch_shapes=scratch,
         cost_estimate=pl.CostEstimate(flops=flops, bytes_accessed=sizes, transcendentals=0),
+        compiler_params=pltpu.CompilerParams(vmem_limit_bytes=3 * (sizes + held) + (4 << 20)),
     )(*args)
 
 
@@ -239,6 +255,9 @@
     def across_ch(array, r):
         return move(array, lambda i, j: (i, j ^ r))
 
+    def spread(parts):
+        return [parts[0]] + [across_seq(parts[r], r) for r in range(1, n)]
+
     def gather_low(block):
         held = [block]
         while len(held) < half:
@@ -246,34 +265,35 @@
             held = held + [across_ch(x, step) for x in held]
         return held
 
-    own_act = move(activations, lambda i, j: (j, i))
-
-    both = jnp.stack([long_filters, cotangent]).reshape(2, n, own, size)
-    blocks = [lax.dynamic_index_in_dim(both, s ^ r, 1, False) for r in range(n)]
-    blocks = [blocks[0]] + [across_seq(blocks[r], r) for r in range(1, n)]
-
-    columns = [
-        lax.dynamic_slice_in_dim(projection, (s ^ r) * own, own, 1) for r in range(n)
-    ]
-    weight = jnp.concatenate(columns, axis=1)
-    weight, weight_t = lax.optimization_barrier((weight, weight.T))
-    table, inverse = lax.optimization_barrier(block_tables(size))
+    act = move(activations, lambda i, j: (j, i))
+    weight, weight_t, *blocks = call(
+        functools.partial(arrange_kernel, n),
+        [shape(projection.shape, BF16), shape(projection.shape[::-1], BF16)]
+        + [shape((2, own, size), BF16)] * n,
+        [],
+        index,
+        (projection, long_filters, cotangent),
+        0,
+    )
+    table, inverse = block_tables(size)
+    act, weight, weight_t, table, inverse, *blocks = lax.optimization_barrier(
+        (act, weight, weight_t, table, inverse, *blocks)
+    )
 
     def values_of(acts):
-        outs = [shape((half, own, size), BF16)] * n
-        parts = call(
+        return call(
             functools.partial(values_kernel, n),
-            outs,
+            [shape((half, own, size), BF16)] * n,
             [],
             None,
             (weight_t, *acts),
             2 * depth * n * own * half * size,
         )
-        return [parts[0]] + [across_seq(parts[r], r) for r in range(1, n)]
-
-    far_act = across_ch(own_act, half)
-    near_sums = values_of(gather_low(own_act))
-    far_sums = values_of(gather_low(far_act))
+
+    far_act = across_ch(act, half)
+    blocks = spread(blocks)
+    near_sums = spread(values_of(gather_low(act)))
+    far_sums = spread(values_of(gather_low(far_act)))
 
     spectrum = 4 * n * size * 2 * size * own
     grad_gated, filt, tap = call(
@@ -292,12 +312,8 @@
         (*near_sums, *far_sums, grad_gated, tap, table, inverse),
         8 * spectrum,
     )
-
-    def gathered(part):
-        return [part] + [across_seq(part, r) for r in range(1, n)]
-
-    far_parts = gathered(far)
-    near_parts = gathered(near)
+    far_back = spread([far] * n)
+    near_back = spread([near] * n)
 
     out_blocks = call(
         functools.partial(long_kernel, n),
@@ -307,7 +323,7 @@
         (gated, filt, table, inverse),
         4 * spectrum,
     )
-    out_blocks = [out_blocks[0]] + [across_seq(out_blocks[r], r) for r in range(1, n)]
+    out_blocks = spread(out_blocks)
 
     def input_of(parts):
         outs = [shape((depth, size), F32 if j < max(half // 2, 1) else BF16) for j in range(half)]
@@ -328,8 +344,10 @@
             sums = [a.astype(F32) + b.astype(F32) for a, b in zip(kept, sent)]
         return sums[0]
 
-    far_total = across_ch(scatter_low(list(input_of(far_parts))).astype(BF16), half)
-    total = scatter_low(list(input_of(near_parts))) + far_total.astype(F32)
+    far_total = scatter_low(list(input_of(far_back))).astype(BF16)
+    far_total = across_ch(far_total, half)
+    total = scatter_low(list(input_of(near_back)))
+    total = total + far_total.astype(F32)
     input_grad = move(total.astype(BF16), lambda i, j: (reverse_bits(j, bits), i))
     (conv_out,) = call(
         functools.partial(place_kernel, n),
@@ -501,33 +519,44 @@
     return (conv_out, input_grad)
 
 
+def fits_square(mesh, activations, projection, medium_taps):
+    seq, ch = mesh.shape["seq"], mesh.shape["ch"]
+    size = activations.shape[1] // (mesh.shape["grp"] * seq)
+    return (
+        seq == ch
+        and seq > 1
+        and seq & (seq - 1) == 0
+        and medium_taps.shape[1] == size
+        and projection.shape[1] == seq * ch * size
+        and size % 128 == 0
+        and activations.shape[0] % (2 * ch * size) == 0
+    )
+
+
 def solution(mesh):
-    seq, ch = mesh.shape["seq"], mesh.shape["ch"]
+    n = mesh.shape["seq"]
+
+    def placed(body):
+        return jax.shard_map(
+            body,
+            mesh=mesh,
+            in_specs=(
+                P("ch", ("grp", "seq")),
+                P("seq", "ch"),
+                P("ch", None),
+                P("ch", "seq"),
+                P("ch", ("grp", "seq")),
+            ),
+            out_specs=(P("ch", ("grp", "seq")), P("ch", ("grp", "seq"))),
+            check_vma=False,
+        )
+
+    def square(*args):
+        return square_plan(n, *args)
 
     def step(*args):
-        activations, projection, medium_taps = args[:3]
-        size = activations.shape[1]
-        square = (
-            seq == ch
-            and seq > 1
-            and seq & (seq - 1) == 0
-            and medium_taps.shape[1] == size
-            and projection.shape[0] == activations.shape[0]
-            and projection.shape[1] == seq * size
-            and size % 128 == 0
-        )
-        return square_plan(seq, *args) if square else on_device(*args)
-
-    return jax.shard_map(
-        step,
-        mesh=mesh,
-        in_specs=(
-            P("ch", ("grp", "seq")),
-            P("seq", "ch"),
-            P("ch", None),
-            P("ch", "seq"),
-            P("ch", ("grp", "seq")),
-        ),
-        out_specs=(P("ch", ("grp", "seq")), P("ch", ("grp", "seq"))),
-        check_vma=False,
-    )
+        return placed(square if fits_square(mesh, *args[:3]) else on_device)(*args)
+
+    if mesh.shape["seq"] != mesh.shape["ch"]:
+        return step
+    return step

time: 109 us -> 93.8 us (0.86)
  Pallas kernels: 19.1 us -> 7.48 us
  local copies, waits for them, and re-layouts: 7.77 us -> 2.78 us
  other arithmetic: 4.83 us -> 0.86 us
  waiting for transfers between devices: 30.1 us -> 33.3 us
  starting transfers between devices: 45.6 us -> 48.3 us
    pallas_call x8 -> x9, Pallas kernels: 19.1 us -> 7.48 us  [call(): pl.pallas_call(kernel, out_shape=tuple(outs), in_specs=specs, out_specs=t...]
    ppermute x26, waiting for transfers between devices: 30.1 us -> 33.3 us  [move(): return lax.ppermute(array, ('seq', 'ch'), pairs)]
    ppermute x26, starting transfers between devices: 45.6 us -> 48.3 us  [move(): return lax.ppermute(array, ('seq', 'ch'), pairs)]
    unnamed x53 -> x9, local copies, waits for them, and re-layouts: 5.16 us -> 2.78 us
    squeeze x1 -> x0, other arithmetic: 1.51 us -> none  [square_plan(): blocks = [lax.dynamic_index_in_dim(both, s ^ r, 1, False) for r in range(n)]]
    optimization_barrier x1 -> x0, local copies, waits for them, and re-layouts: 1.33 us -> none  [square_plan(): weight, weight_t = lax.optimization_barrier((weight, weight.T))]
    dynamic_slice x1 -> x0, local copies, waits for them, and re-layouts: 1.28 us -> none  [square_plan(): lax.dynamic_slice_in_dim(projection, (s ^ r) * own, own, 1)]
    transpose x1 -> x0, other arithmetic: 1.18 us -> none  [square_plan(): weight, weight_t = lax.optimization_barrier((weight, weight.T))]
  transfers between devices with their start and end apart: 26 -> 26, of which waited for: 9 -> 11; matrix products, arithmetic and copies ran while one was open for 7% -> 1% of each run, Pallas kernels for 13% -> 6%
where the time goes in v2:
time: 93.8 us; the launch traced here: 93.6 us
  starting transfers between devices  48.3 us (51%)
  waiting for transfers between devices  33.3 us (36%)
  Pallas kernels  7.48 us (8%)
  local copies, waits for them, and re-layouts  2.78 us (3%)
    ppermute x26, starting transfers between devices, move(): return lax.ppermute(array, ('seq', 'ch'), pairs)  48.3 us
    ppermute x26, waiting for transfers between devices, move(): return lax.ppermute(array, ('seq', 'ch'), pairs)  33.3 us
    pallas_call x9, Pallas kernels, call(): pl.pallas_call(kernel, out_shape=tuple(outs), in_specs=specs, out_specs=t...  7.48 us
    unnamed x9, local copies, waits for them, and re-layouts  2.78 us
  transfers between devices with their start and end apart: 26, of which 11 were waited for; matrix products, arithmetic and copies ran while one was open for 1% of the time, Pallas kernels for 6%

profile of v2, /device:TPU:0, one launch (start us, length us, event | category | flops | bytes accessed | tf_op | source)
XLA Modules:
  0.0 93.6 jit_solution(2529932819580738522)
XLA Ops:
  0.6 1.6 %collective-permute-start = (bf16[1024,128]{1,0:T(8,128)(2,1)}, bf16[1024,128]{1,0:T(8,128)(2,1)S(1)}, u32[]{:S(2)}, u32[]{:S(2)}) collective-permute-start(bf16[1024,128]{1,0:T(8,128)(2,1)} %param.5), channel_id=1, source_target_pairs={{0,0},{1,4},{2,8},{3,12},{4,1},{5,5},{6,9},{7,13},{8,2},{9,6},{10,... | collective-permute-start | bytes 786440 | tf_op jit(solution)/shard_map/ppermute | solution.py:250
  3.0 0.8 copy-done.2
  3.8 1.2 %copy-done = bf16[1024,512]{1,0:T(8,128)(2,1)S(1)} copy-done((bf16[1024,512]{1,0:T(8,128)(2,1)S(1)}, bf16[1024,512]{1,0:T(8,128)(2,1)}, u32[]{:S(2)}) %copy-start) | copy-done | bytes 1048600
  5.0 1.0 %shard_map.68 = (bf16[1024,512]{1,0:T(8,128)(2,1)S(1)}, bf16[512,1024]{1,0:T(8,128)(2,1)S(1)}, bf16[2,128,128]{2,1,0:T(8,128)(2,1)S(1)}, bf16[2,128,128]{2,1,0:T...) custom-call(s32[2]{0:T(128)S(1)} %pad_add_fusion.index_ref, ...), custom_call_target="tpu_custom_call" | custom-call | bytes 3670016 | tf_op jit(solution)/shard_map/pallas_call | solution.py:224
  6.1 15.9 %collective-permute-start.5 = (bf16[1024,128]{1,0:T(8,128)(2,1)S(1)}, bf16[1024,128]{1,0:T(8,128)(2,1)S(1)}, u32[]{:S(2)}, u32[]{:S(2)}) collective-permute-start(bf16[1024,128]{1,0:T(8,128)(2,1)S(1)} %collective-permute-done.refs_0_), channel_id=1, source_target_pairs={{0,2},{1,3},{2,0},{3,1},{4,6},{5,7},{6,4},{7,5},{8,10},{9,11},{10,... | collective-permute-start | bytes 786440 | tf_op jit(solution)/shard_map/ppermute | solution.py:250
  21.9 4.3 %collective-permute-done.5.refs_0_ = bf16[1024,128]{1,0:T(8,128)(2,1)S(1)} collective-permute-done((bf16[1024,128]{1,0:T(8,128)(2,1)S(1)}, bf16[1024,128]{1,0:T(8,128)(2,1)S(1)}, u32[]{:S(2)}, u32[]{:S(2)}) %collective-permute-start.5) | collective-permute-done | bytes 262176 | tf_op jit(solution)/shard_map/ppermute | solution.py:250
  26.3 1.0 %collective-permute-start.10 = (bf16[2,128,128]{2,1,0:T(8,128)(2,1)S(1)}, bf16[2,128,128]{2,1,0:T(8,128)(2,1)S(1)}, u32[]{:S(2)}, u32[]{:S(2)}) collective-permute-start(bf16[2,128,128]{2,1,0:T(8,128)(2,1)S(1)} %get-tuple-element.56), channel_id=1, source_target_pairs={{0,4},{1,5},{2,6},{3,7},{4,0},{5,1},{6,2},{7,3},{8,12},{9,13},{10,... | collective-permute-start | bytes 196616 | tf_op jit(solution)/shard_map/ppermute | solution.py:250
  27.3 1.8 %collective-permute-start.11 = (bf16[2,128,128]{2,1,0:T(8,128)(2,1)S(1)}, bf16[2,128,128]{2,1,0:T(8,128)(2,1)S(1)}, u32[]{:S(2)}, u32[]{:S(2)}) collective-permute-start(bf16[2,128,128]{2,1,0:T(8,128)(2,1)S(1)} %get-tuple-element.57), channel_id=1, source_target_pairs={{0,8},{1,9},{2,10},{3,11},{4,12},{5,13},{6,14},{7,15},{8,0},{9,1},... | collective-permute-start | bytes 196616 | tf_op jit(solution)/shard_map/ppermute | solution.py:250
  29.0 1.6 %collective-permute-start.12 = (bf16[2,128,128]{2,1,0:T(8,128)(2,1)S(1)}, bf16[2,128,128]{2,1,0:T(8,128)(2,1)S(1)}, u32[]{:S(2)}, u32[]{:S(2)}) collective-permute-start(bf16[2,128,128]{2,1,0:T(8,128)(2,1)S(1)} %get-tuple-element.58), channel_id=1, source_target_pairs={{0,12},{1,13},{2,14},{3,15},{4,8},{5,9},{6,10},{7,11},{8,4},{9,5},... | collective-permute-start | bytes 196616 | tf_op jit(solution)/shard_map/ppermute | solution.py:250
  31.6 2.4 %collective-permute-start.3 = (bf16[2,128,128]{2,1,0:T(8,128)(2,1)S(1)}, bf16[2,128,128]{2,1,0:T(8,128)(2,1)S(1)}, u32[]{:S(2)}, u32[]{:S(2)}) collective-permute-start(bf16[2,128,128]{2,1,0:T(8,128)(2,1)S(1)} %get-tuple-element.49), channel_id=1, source_target_pairs={{0,8},{1,9},{2,10},{3,11},{4,12},{5,13},{6,14},{7,15},{8,0},{9,1},... | collective-permute-start | bytes 196616 | tf_op jit(solution)/shard_map/ppermute | solution.py:250
  34.4 1.7 %collective-permute-start.4 = (bf16[2,128,128]{2,1,0:T(8,128)(2,1)S(1)}, bf16[2,128,128]{2,1,0:T(8,128)(2,1)S(1)}, u32[]{:S(2)}, u32[]{:S(2)}) collective-permute-start(bf16[2,128,128]{2,1,0:T(8,128)(2,1)S(1)} %get-tuple-element.50), channel_id=1, source_target_pairs={{0,12},{1,13},{2,14},{3,15},{4,8},{5,9},{6,10},{7,11},{8,4},{9,5},... | collective-permute-start | bytes 196616 | tf_op jit(solution)/shard_map/ppermute | solution.py:250
  36.3 5.2 %collective-permute-start.8 = (bf16[2,128,128]{2,1,0:T(8,128)(2,1)S(1)}, bf16[2,128,128]{2,1,0:T(8,128)(2,1)S(1)}, u32[]{:S(2)}, u32[]{:S(2)}) collective-permute-start(bf16[2,128,128]{2,1,0:T(8,128)(2,1)S(1)} %get-tuple-element.53), channel_id=1, source_target_pairs={{0,8},{1,9},{2,10},{3,11},{4,12},{5,13},{6,14},{7,15},{8,0},{9,1},... | collective-permute-start | bytes 196616 | tf_op jit(solution)/shard_map/ppermute | solution.py:250
  42.2 1.2 %shard_map.71 = (bf16[4,128,128]{2,1,0:T(8,128)(2,1)S(1)}, f32[512,256]{1,0:T(8,128)S(1)}, f32[128,256]{1,0:T(8,128)S(1)}) custom-call(s32[2]{0:T(128)S(1)} %pad_add_fusion.index_ref, bf16[2,128,128]{2,1,0:T(8,128)(2,1)S(1)} %get-tuple-element.55.refs_0_, bf16[2,128,128]{2,1,0:T(8,128)(2,1)S(1)} %collective-permute-done.10.refs_1_, ...), custom_call_target="tpu_custom_call" | custom-call | flops 402653184 | bytes 1572864 | tf_op jit(solution)/shard_map/pallas_call | solution.py:224
  43.4 2.9 %collective-permute-done.8.refs_6_ = bf16[2,128,128]{2,1,0:T(8,128)(2,1)S(1)} collective-permute-done((bf16[2,128,128]{2,1,0:T(8,128)(2,1)S(1)}, bf16[2,128,128]{2,1,0:T(8,128)(2,1)S(1)}, u32[]{:S(2)}, u32[]{:S(2)}) %collective-permute-start.8) | collective-permute-done | bytes 65568 | tf_op jit(solution)/shard_map/ppermute | solution.py:250
  46.3 1.3 %collective-permute-done.9.refs_7_ = bf16[2,128,128]{2,1,0:T(8,128)(2,1)S(1)} collective-permute-done((bf16[2,128,128]{2,1,0:T(8,128)(2,1)S(1)}, bf16[2,128,128]{2,1,0:T(8,128)(2,1)S(1)}, u32[]{:S(2)}, u32[]{:S(2)}) %collective-permute-start.9) | collective-permute-done | bytes 65568 | tf_op jit(solution)/shard_map/ppermute | solution.py:250
  47.6 1.3 %shard_map.72 = (bf16[2,128,128]{2,1,0:T(8,128)(2,1)S(1)}, bf16[2,128,128]{2,1,0:T(8,128)(2,1)S(1)}, bf16[4,128,128]{2,1,0:T(8,128)(2,1)S(1)}) custom-call(s32[2]{0:T(128)S(1)} %pad_add_fusion.index_ref, bf16[2,128,128]{2,1,0:T(8,128)(2,1)S(1)} %get-tuple-element.47.refs_0_, bf16[2,128,128]{2,1,0:T(8,128)(2,1)S(1)} %collective-permute-done.2.refs_1_, ...), custom_call_target="tpu_custom_call" | custom-call | flops 536870912 | bytes 1310720 | tf_op jit(solution)/shard_map/pallas_call | solution.py:224
  48.9 1.8 %collective-permute-start.22 = (bf16[2,128,128]{2,1,0:T(8,128)(2,1)S(1)}, bf16[2,128,128]{2,1,0:T(8,128)(2,1)S(1)}, u32[]{:S(2)}, u32[]{:S(2)}) collective-permute-start(bf16[2,128,128]{2,1,0:T(8,128)(2,1)S(1)} %get-tuple-element.73.refs_0_), channel_id=1, source_target_pairs={{0,12},{1,13},{2,14},{3,15},{4,8},{5,9},{6,10},{7,11},{8,4},{9,5},... | collective-permute-start | bytes 196616 | tf_op jit(solution)/shard_map/ppermute | solution.py:250
  51.3 2.0 %collective-permute-start.20 = (bf16[2,128,128]{2,1,0:T(8,128)(2,1)S(1)}, bf16[2,128,128]{2,1,0:T(8,128)(2,1)S(1)}, u32[]{:S(2)}, u32[]{:S(2)}) collective-permute-start(bf16[2,128,128]{2,1,0:T(8,128)(2,1)S(1)} %get-tuple-element.73.refs_0_), channel_id=1, source_target_pairs={{0,4},{1,5},{2,6},{3,7},{4,0},{5,1},{6,2},{7,3},{8,12},{9,13},{10,... | collective-permute-start | bytes 196616 | tf_op jit(solution)/shard_map/ppermute | solution.py:250
  53.3 2.4 %collective-permute-done.22.refs_3_ = bf16[2,128,128]{2,1,0:T(8,128)(2,1)S(1)} collective-permute-done((bf16[2,128,128]{2,1,0:T(8,128)(2,1)S(1)}, bf16[2,128,128]{2,1,0:T(8,128)(2,1)S(1)}, u32[]{:S(2)}, u32[]{:S(2)}) %collective-permute-start.22) | collective-permute-done | bytes 65568 | tf_op jit(solution)/shard_map/ppermute | solution.py:250
  55.7 1.6 %collective-permute-done.21.refs_2_ = bf16[2,128,128]{2,1,0:T(8,128)(2,1)S(1)} collective-permute-done((bf16[2,128,128]{2,1,0:T(8,128)(2,1)S(1)}, bf16[2,128,128]{2,1,0:T(8,128)(2,1)S(1)}, u32[]{:S(2)}, u32[]{:S(2)}) %collective-permute-start.21) | collective-permute-done | bytes 65568 | tf_op jit(solution)/shard_map/ppermute | solution.py:250
  57.9 3.0 %collective-permute-start.18 = (bf16[2,128,128]{2,1,0:T(8,128)(2,1)S(1)}, bf16[2,128,128]{2,1,0:T(8,128)(2,1)S(1)}, u32[]{:S(2)}, u32[]{:S(2)}) collective-permute-start(bf16[2,128,128]{2,1,0:T(8,128)(2,1)S(1)} %get-tuple-element.70.refs_0_), channel_id=1, source_target_pairs={{0,12},{1,13},{2,14},{3,15},{4,8},{5,9},{6,10},{7,11},{8,4},{9,5},... | collective-permute-start | bytes 196616 | tf_op jit(solution)/shard_map/ppermute | solution.py:250
  60.8 1.5 %collective-permute-start.16 = (bf16[2,128,128]{2,1,0:T(8,128)(2,1)S(1)}, bf16[2,128,128]{2,1,0:T(8,128)(2,1)S(1)}, u32[]{:S(2)}, u32[]{:S(2)}) collective-permute-start(bf16[2,128,128]{2,1,0:T(8,128)(2,1)S(1)} %get-tuple-element.70.refs_0_), channel_id=1, source_target_pairs={{0,4},{1,5},{2,6},{3,7},{4,0},{5,1},{6,2},{7,3},{8,12},{9,13},{10,... | collective-permute-start | bytes 196616 | tf_op jit(solution)/shard_map/ppermute | solution.py:250
  62.3 2.4 %collective-permute-done.18.refs_3_ = bf16[2,128,128]{2,1,0:T(8,128)(2,1)S(1)} collective-permute-done((bf16[2,128,128]{2,1,0:T(8,128)(2,1)S(1)}, bf16[2,128,128]{2,1,0:T(8,128)(2,1)S(1)}, u32[]{:S(2)}, u32[]{:S(2)}) %collective-permute-start.18) | collective-permute-done | bytes 65568 | tf_op jit(solution)/shard_map/ppermute | solution.py:250
  64.7 2.2 %collective-permute-done.17.refs_2_ = bf16[2,128,128]{2,1,0:T(8,128)(2,1)S(1)} collective-permute-done((bf16[2,128,128]{2,1,0:T(8,128)(2,1)S(1)}, bf16[2,128,128]{2,1,0:T(8,128)(2,1)S(1)}, u32[]{:S(2)}, u32[]{:S(2)}) %collective-permute-start.17) | collective-permute-done | bytes 65568 | tf_op jit(solution)/shard_map/ppermute | solution.py:250
  68.2 0.8 collective-permute-done.19
  69.0 7.3 %collective-permute-done.24 = bf16[1024,128]{1,0:T(8,128)(2,1)S(1)} collective-permute-done((bf16[1024,128]{1,0:T(8,128)(2,1)S(1)}, bf16[1024,128]{1,0:T(8,128)(2,1)S(1)}, u32[]{:S(2)}, u32[]{:S(2)}) %collective-permute-start.24) | collective-permute-done | bytes 262176 | tf_op jit(solution)/shard_map/ppermute | solution.py:250
  77.1 1.1 %shard_map.73 = (bf16[128,128]{1,0:T(8,128)(2,1)S(1)}, bf16[128,128]{1,0:T(8,128)(2,1)S(1)}, bf16[128,128]{1,0:T(8,128)(2,1)S(1)}, bf16[128,128]{1,0:T(8,128)(2,1)S(1)}) custom-call(s32[2]{0:T(128)S(1)} %pad_add_fusion.index_ref, bf16[4,128,128]{2,1,0:T(8,128)(2,1)S(1)} %get-tuple-element.63.gated_ref, f32[512,256]{1,0:T(8,128)S(1)} %get-tuple-element.64.filt_ref, ...), custom_call_target="tpu_custom_call" | custom-call | flops 268435456 | bytes 1048576 | tf_op jit(solution)/shard_map/pallas_call | solution.py:224
  78.2 2.5 %collective-permute-start.13 = (bf16[128,128]{1,0:T(8,128)(2,1)S(1)}, bf16[128,128]{1,0:T(8,128)(2,1)S(1)}, u32[]{:S(2)}, u32[]{:S(2)}) collective-permute-start(bf16[128,128]{1,0:T(8,128)(2,1)S(1)} %get-tuple-element.66), channel_id=1, source_target_pairs={{0,4},{1,5},{2,6},{3,7},{4,0},{5,1},{6,2},{7,3},{8,12},{9,13},{10,... | collective-permute-start | bytes 98312 | tf_op jit(solution)/shard_map/ppermute | solution.py:250
  80.8 2.4 %collective-permute-start.14 = (bf16[128,128]{1,0:T(8,128)(2,1)S(1)}, bf16[128,128]{1,0:T(8,128)(2,1)S(1)}, u32[]{:S(2)}, u32[]{:S(2)}) collective-permute-start(bf16[128,128]{1,0:T(8,128)(2,1)S(1)} %get-tuple-element.67), channel_id=1, source_target_pairs={{0,8},{1,9},{2,10},{3,11},{4,12},{5,13},{6,14},{7,15},{8,0},{9,1},... | collective-permute-start | bytes 98312 | tf_op jit(solution)/shard_map/ppermute | solution.py:250
  83.1 0.8 collective-permute-start.15
  83.9 7.7 %collective-permute-done.13.refs_1_ = bf16[128,128]{1,0:T(8,128)(2,1)S(1)} collective-permute-done((bf16[128,128]{1,0:T(8,128)(2,1)S(1)}, bf16[128,128]{1,0:T(8,128)(2,1)S(1)}, u32[]{:S(2)}, u32[]{:S(2)}) %collective-permute-start.13) | collective-permute-done | bytes 32800 | tf_op jit(solution)/shard_map/ppermute | solution.py:250
  91.7 1.2 %shard_map.74 = bf16[512,128]{1,0:T(8,128)(2,1)} custom-call(s32[2]{0:T(128)S(1)} %pad_add_fusion.index_ref, bf16[128,128]{1,0:T(8,128)(2,1)S(1)} %get-tuple-element.65.refs_0_, bf16[128,128]{1,0:T(8,128)(2,1)S(1)} %collective-permute-done.13.refs_1_, bf16[128,128]{1,0:T(8,128)(2,1)S(1)} %collective-permute-done.14.refs_2_, ...), custom_call_target="tpu_custom_call" | custom-call | bytes 262144 | tf_op jit(solution)/shard_map/pallas_call | solution.py:224
  (47 shorter events, 6.9 us)
Async XLA Ops:
  0.6 5.4 %collective-permute-start = (bf16[1024,128]{1,0:T(8,128)(2,1)}, bf16[1024,128]{1,0:T(8,128)(2,1)S(1)}, u32[]{:S(2)}, u32[]{:S(2)}) collective-permute-start(bf16[1024,128]{1,0:T(8,128)(2,1)} %param.5), channel_id=1, source_target_pairs={{0,0},{1,4},{2,8},{3,12},{4,1},{5,5},{6,9},{7,13},{8,2},{9,6},{10,... | collective-permute-start | bytes 786440 | tf_op jit(solution)/shard_map/ppermute | solution.py:250
  2.8 0.9 copy-start.2
  2.8 0.9 %copy-start.1 = (bf16[512,128]{1,0:T(8,128)(2,1)S(1)}, bf16[512,128]{1,0:T(8,128)(2,1)}, u32[]{:S(2)}) copy-start(bf16[512,128]{1,0:T(8,128)(2,1)} %filters_ref.1) | copy-start | bytes 393220
  3.8 1.2 %copy-start = (bf16[1024,512]{1,0:T(8,128)(2,1)S(1)}, bf16[1024,512]{1,0:T(8,128)(2,1)}, u32[]{:S(2)}) copy-start(bf16[1024,512]{1,0:T(8,128)(2,1)} %given_ref.1) | copy-start | bytes 3145732
  6.1 20.2 %collective-permute-start.5 = (bf16[1024,128]{1,0:T(8,128)(2,1)S(1)}, bf16[1024,128]{1,0:T(8,128)(2,1)S(1)}, u32[]{:S(2)}, u32[]{:S(2)}) collective-permute-start(bf16[1024,128]{1,0:T(8,128)(2,1)S(1)} %collective-permute-done.refs_0_), channel_id=1, source_target_pairs={{0,2},{1,3},{2,0},{3,1},{4,6},{5,7},{6,4},{7,5},{8,10},{9,11},{10,... | collective-permute-start | bytes 786440 | tf_op jit(solution)/shard_map/ppermute | solution.py:250
  21.9 8.7 %collective-permute-start.1 = (bf16[1024,128]{1,0:T(8,128)(2,1)S(1)}, bf16[1024,128]{1,0:T(8,128)(2,1)S(1)}, u32[]{:S(2)}, u32[]{:S(2)}) collective-permute-start(bf16[1024,128]{1,0:T(8,128)(2,1)S(1)} %collective-permute-done.refs_0_), channel_id=1, source_target_pairs={{0,1},{1,0},{2,3},{3,2},{4,5},{5,4},{6,7},{7,6},{8,9},{9,8},{10,11... | collective-permute-start | bytes 786440 | tf_op jit(solution)/shard_map/ppermute | solution.py:250
  26.3 5.3 %collective-permute-start.6 = (bf16[1024,128]{1,0:T(8,128)(2,1)S(1)}, bf16[1024,128]{1,0:T(8,128)(2,1)S(1)}, u32[]{:S(2)}, u32[]{:S(2)}) collective-permute-start(bf16[1024,128]{1,0:T(8,128)(2,1)S(1)} %collective-permute-done.5.refs_0_), channel_id=1, source_target_pairs={{0,1},{1,0},{2,3},{3,2},{4,5},{5,4},{6,7},{7,6},{8,9},{9,8},{10,11... | collective-permute-start | bytes 786440 | tf_op jit(solution)/shard_map/ppermute | solution.py:250
  26.3 8.1 %collective-permute-start.10 = (bf16[2,128,128]{2,1,0:T(8,128)(2,1)S(1)}, bf16[2,128,128]{2,1,0:T(8,128)(2,1)S(1)}, u32[]{:S(2)}, u32[]{:S(2)}) collective-permute-start(bf16[2,128,128]{2,1,0:T(8,128)(2,1)S(1)} %get-tuple-element.56), channel_id=1, source_target_pairs={{0,4},{1,5},{2,6},{3,7},{4,0},{5,1},{6,2},{7,3},{8,12},{9,13},{10,... | collective-permute-start | bytes 196616 | tf_op jit(solution)/shard_map/ppermute | solution.py:250
  27.3 8.9 %collective-permute-start.11 = (bf16[2,128,128]{2,1,0:T(8,128)(2,1)S(1)}, bf16[2,128,128]{2,1,0:T(8,128)(2,1)S(1)}, u32[]{:S(2)}, u32[]{:S(2)}) collective-permute-start(bf16[2,128,128]{2,1,0:T(8,128)(2,1)S(1)} %get-tuple-element.57), channel_id=1, source_target_pairs={{0,8},{1,9},{2,10},{3,11},{4,12},{5,13},{6,14},{7,15},{8,0},{9,1},... | collective-permute-start | bytes 196616 | tf_op jit(solution)/shard_map/ppermute | solution.py:250
  29.0 7.3 %collective-permute-start.12 = (bf16[2,128,128]{2,1,0:T(8,128)(2,1)S(1)}, bf16[2,128,128]{2,1,0:T(8,128)(2,1)S(1)}, u32[]{:S(2)}, u32[]{:S(2)}) collective-permute-start(bf16[2,128,128]{2,1,0:T(8,128)(2,1)S(1)} %get-tuple-element.58), channel_id=1, source_target_pairs={{0,12},{1,13},{2,14},{3,15},{4,8},{5,9},{6,10},{7,11},{8,4},{9,5},... | collective-permute-start | bytes 196616 | tf_op jit(solution)/shard_map/ppermute | solution.py:250
  31.1 10.3 %collective-permute-start.2 = (bf16[2,128,128]{2,1,0:T(8,128)(2,1)S(1)}, bf16[2,128,128]{2,1,0:T(8,128)(2,1)S(1)}, u32[]{:S(2)}, u32[]{:S(2)}) collective-permute-start(bf16[2,128,128]{2,1,0:T(8,128)(2,1)S(1)} %get-tuple-element.48), channel_id=1, source_target_pairs={{0,4},{1,5},{2,6},{3,7},{4,0},{5,1},{6,2},{7,3},{8,12},{9,13},{10,... | collective-permute-start | bytes 196616 | tf_op jit(solution)/shard_map/ppermute | solution.py:250
  31.6 10.6 %copy-start.3 = (f32[512,128]{1,0:T(8,128)S(1)}, f32[512,128]{1,0:T(8,128)}, u32[]{:S(2)}) copy-start(f32[512,128]{1,0:T(8,128)} %refs_4_.1) | copy-start | bytes 786436
  31.6 11.8 %collective-permute-start.3 = (bf16[2,128,128]{2,1,0:T(8,128)(2,1)S(1)}, bf16[2,128,128]{2,1,0:T(8,128)(2,1)S(1)}, u32[]{:S(2)}, u32[]{:S(2)}) collective-permute-start(bf16[2,128,128]{2,1,0:T(8,128)(2,1)S(1)} %get-tuple-element.49), channel_id=1, source_target_pairs={{0,8},{1,9},{2,10},{3,11},{4,12},{5,13},{6,14},{7,15},{8,0},{9,1},... | collective-permute-start | bytes 196616 | tf_op jit(solution)/shard_map/ppermute | solution.py:250
  34.4 8.9 %collective-permute-start.4 = (bf16[2,128,128]{2,1,0:T(8,128)(2,1)S(1)}, bf16[2,128,128]{2,1,0:T(8,128)(2,1)S(1)}, u32[]{:S(2)}, u32[]{:S(2)}) collective-permute-start(bf16[2,128,128]{2,1,0:T(8,128)(2,1)S(1)} %get-tuple-element.50), channel_id=1, source_target_pairs={{0,12},{1,13},{2,14},{3,15},{4,8},{5,9},{6,10},{7,11},{8,4},{9,5},... | collective-permute-start | bytes 196616 | tf_op jit(solution)/shard_map/ppermute | solution.py:250
  36.1 7.2 %collective-permute-start.7 = (bf16[2,128,128]{2,1,0:T(8,128)(2,1)S(1)}, bf16[2,128,128]{2,1,0:T(8,128)(2,1)S(1)}, u32[]{:S(2)}, u32[]{:S(2)}) collective-permute-start(bf16[2,128,128]{2,1,0:T(8,128)(2,1)S(1)} %get-tuple-element.52), channel_id=1, source_target_pairs={{0,4},{1,5},{2,6},{3,7},{4,0},{5,1},{6,2},{7,3},{8,12},{9,13},{10,... | collective-permute-start | bytes 196616 | tf_op jit(solution)/shard_map/ppermute | solution.py:250
  36.3 10.0 %collective-permute-start.8 = (bf16[2,128,128]{2,1,0:T(8,128)(2,1)S(1)}, bf16[2,128,128]{2,1,0:T(8,128)(2,1)S(1)}, u32[]{:S(2)}, u32[]{:S(2)}) collective-permute-start(bf16[2,128,128]{2,1,0:T(8,128)(2,1)S(1)} %get-tuple-element.53), channel_id=1, source_target_pairs={{0,8},{1,9},{2,10},{3,11},{4,12},{5,13},{6,14},{7,15},{8,0},{9,1},... | collective-permute-start | bytes 196616 | tf_op jit(solution)/shard_map/ppermute | solution.py:250
  41.4 6.2 %collective-permute-start.9 = (bf16[2,128,128]{2,1,0:T(8,128)(2,1)S(1)}, bf16[2,128,128]{2,1,0:T(8,128)(2,1)S(1)}, u32[]{:S(2)}, u32[]{:S(2)}) collective-permute-start(bf16[2,128,128]{2,1,0:T(8,128)(2,1)S(1)} %get-tuple-element.54), channel_id=1, source_target_pairs={{0,12},{1,13},{2,14},{3,15},{4,8},{5,9},{6,10},{7,11},{8,4},{9,5},... | collective-permute-start | bytes 196616 | tf_op jit(solution)/shard_map/ppermute | solution.py:250
  48.9 6.9 %collective-permute-start.22 = (bf16[2,128,128]{2,1,0:T(8,128)(2,1)S(1)}, bf16[2,128,128]{2,1,0:T(8,128)(2,1)S(1)}, u32[]{:S(2)}, u32[]{:S(2)}) collective-permute-start(bf16[2,128,128]{2,1,0:T(8,128)(2,1)S(1)} %get-tuple-element.73.refs_0_), channel_id=1, source_target_pairs={{0,12},{1,13},{2,14},{3,15},{4,8},{5,9},{6,10},{7,11},{8,4},{9,5},... | collective-permute-start | bytes 196616 | tf_op jit(solution)/shard_map/ppermute | solution.py:250
  50.7 6.7 %collective-permute-start.21 = (bf16[2,128,128]{2,1,0:T(8,128)(2,1)S(1)}, bf16[2,128,128]{2,1,0:T(8,128)(2,1)S(1)}, u32[]{:S(2)}, u32[]{:S(2)}) collective-permute-start(bf16[2,128,128]{2,1,0:T(8,128)(2,1)S(1)} %get-tuple-element.73.refs_0_), channel_id=1, source_target_pairs={{0,8},{1,9},{2,10},{3,11},{4,12},{5,13},{6,14},{7,15},{8,0},{9,1},... | collective-permute-start | bytes 196616 | tf_op jit(solution)/shard_map/ppermute | solution.py:250
  51.3 6.0 %collective-permute-start.20 = (bf16[2,128,128]{2,1,0:T(8,128)(2,1)S(1)}, bf16[2,128,128]{2,1,0:T(8,128)(2,1)S(1)}, u32[]{:S(2)}, u32[]{:S(2)}) collective-permute-start(bf16[2,128,128]{2,1,0:T(8,128)(2,1)S(1)} %get-tuple-element.73.refs_0_), channel_id=1, source_target_pairs={{0,4},{1,5},{2,6},{3,7},{4,0},{5,1},{6,2},{7,3},{8,12},{9,13},{10,... | collective-permute-start | bytes 196616 | tf_op jit(solution)/shard_map/ppermute | solution.py:250
  57.8 9.7 %collective-permute-start.23 = (bf16[1024,128]{1,0:T(8,128)(2,1)S(1)}, bf16[1024,128]{1,0:T(8,128)(2,1)S(1)}, u32[]{:S(2)}, u32[]{:S(2)}) collective-permute-start(bf16[1024,128]{1,0:T(8,128)(2,1)S(1)} %get-tuple-element.75), channel_id=1, source_target_pairs={{0,1},{1,0},{2,3},{3,2},{4,5},{5,4},{6,7},{7,6},{8,9},{9,8},{10,11... | collective-permute-start | bytes 786440 | tf_op jit(solution)/shard_map/ppermute | solution.py:250
  57.9 6.9 %collective-permute-start.18 = (bf16[2,128,128]{2,1,0:T(8,128)(2,1)S(1)}, bf16[2,128,128]{2,1,0:T(8,128)(2,1)S(1)}, u32[]{:S(2)}, u32[]{:S(2)}) collective-permute-start(bf16[2,128,128]{2,1,0:T(8,128)(2,1)S(1)} %get-tuple-element.70.refs_0_), channel_id=1, source_target_pairs={{0,12},{1,13},{2,14},{3,15},{4,8},{5,9},{6,10},{7,11},{8,4},{9,5},... | collective-permute-start | bytes 196616 | tf_op jit(solution)/shard_map/ppermute | solution.py:250
  60.8 6.1 %collective-permute-start.17 = (bf16[2,128,128]{2,1,0:T(8,128)(2,1)S(1)}, bf16[2,128,128]{2,1,0:T(8,128)(2,1)S(1)}, u32[]{:S(2)}, u32[]{:S(2)}) collective-permute-start(bf16[2,128,128]{2,1,0:T(8,128)(2,1)S(1)} %get-tuple-element.70.refs_0_), channel_id=1, source_target_pairs={{0,8},{1,9},{2,10},{3,11},{4,12},{5,13},{6,14},{7,15},{8,0},{9,1},... | collective-permute-start | bytes 196616 | tf_op jit(solution)/shard_map/ppermute | solution.py:250
  60.8 6.1 %collective-permute-start.16 = (bf16[2,128,128]{2,1,0:T(8,128)(2,1)S(1)}, bf16[2,128,128]{2,1,0:T(8,128)(2,1)S(1)}, u32[]{:S(2)}, u32[]{:S(2)}) collective-permute-start(bf16[2,128,128]{2,1,0:T(8,128)(2,1)S(1)} %get-tuple-element.70.refs_0_), channel_id=1, source_target_pairs={{0,4},{1,5},{2,6},{3,7},{4,0},{5,1},{6,2},{7,3},{8,12},{9,13},{10,... | collective-permute-start | bytes 196616 | tf_op jit(solution)/shard_map/ppermute | solution.py:250
  67.4 1.6 %collective-permute-start.19 = (bf16[1024,128]{1,0:T(8,128)(2,1)S(1)}, bf16[1024,128]{1,0:T(8,128)(2,1)S(1)}, u32[]{:S(2)}, u32[]{:S(2)}) collective-permute-start(bf16[1024,128]{1,0:T(8,128)(2,1)S(1)} %get-tuple-element.72), channel_id=1, source_target_pairs={{0,1},{1,0},{2,3},{3,2},{4,5},{5,4},{6,7},{7,6},{8,9},{9,8},{10,11... | collective-permute-start | bytes 786440 | tf_op jit(solution)/shard_map/ppermute | solution.py:250
  67.6 8.7 %collective-permute-start.24 = (bf16[1024,128]{1,0:T(8,128)(2,1)S(1)}, bf16[1024,128]{1,0:T(8,128)(2,1)S(1)}, u32[]{:S(2)}, u32[]{:S(2)}) collective-permute-start(bf16[1024,128]{1,0:T(8,128)(2,1)S(1)} %add_convert_fusion.1), channel_id=1, source_target_pairs={{0,2},{1,3},{2,0},{3,1},{4,6},{5,7},{6,4},{7,5},{8,10},{9,11},{10,... | collective-permute-start | bytes 786440 | tf_op jit(solution)/shard_map/ppermute | solution.py:250
  76.4 16.4 %collective-permute-start.25 = (bf16[1024,128]{1,0:T(8,128)(2,1)S(1)}, bf16[1024,128]{1,0:T(8,128)(2,1)S(1)}, u32[]{:S(2)}, u32[]{:S(2)}) collective-permute-start(bf16[1024,128]{1,0:T(8,128)(2,1)S(1)} %add_convert_fusion), channel_id=1, source_target_pairs={{0,0},{1,8},{2,4},{3,12},{4,1},{5,9},{6,5},{7,13},{8,2},{9,10},{10... | collective-permute-start | bytes 786440 | tf_op jit(solution)/shard_map/ppermute | solution.py:250
  78.2 13.4 %collective-permute-start.13 = (bf16[128,128]{1,0:T(8,128)(2,1)S(1)}, bf16[128,128]{1,0:T(8,128)(2,1)S(1)}, u32[]{:S(2)}, u32[]{:S(2)}) collective-permute-start(bf16[128,128]{1,0:T(8,128)(2,1)S(1)} %get-tuple-element.66), channel_id=1, source_target_pairs={{0,4},{1,5},{2,6},{3,7},{4,0},{5,1},{6,2},{7,3},{8,12},{9,13},{10,... | collective-permute-start | bytes 98312 | tf_op jit(solution)/shard_map/ppermute | solution.py:250
  80.8 10.9 %collective-permute-start.14 = (bf16[128,128]{1,0:T(8,128)(2,1)S(1)}, bf16[128,128]{1,0:T(8,128)(2,1)S(1)}, u32[]{:S(2)}, u32[]{:S(2)}) collective-permute-start(bf16[128,128]{1,0:T(8,128)(2,1)S(1)} %get-tuple-element.67), channel_id=1, source_target_pairs={{0,8},{1,9},{2,10},{3,11},{4,12},{5,13},{6,14},{7,15},{8,0},{9,1},... | collective-permute-start | bytes 98312 | tf_op jit(solution)/shard_map/ppermute | solution.py:250
  83.1 8.5 %collective-permute-start.15 = (bf16[128,128]{1,0:T(8,128)(2,1)S(1)}, bf16[128,128]{1,0:T(8,128)(2,1)S(1)}, u32[]{:S(2)}, u32[]{:S(2)}) collective-permute-start(bf16[128,128]{1,0:T(8,128)(2,1)S(1)} %get-tuple-element.68), channel_id=1, source_target_pairs={{0,12},{1,13},{2,14},{3,15},{4,8},{5,9},{6,10},{7,11},{8,4},{9,5},... | collective-permute-start | bytes 98312 | tf_op jit(solution)/shard_map/ppermute | solution.py:250

commit v3 on v2

--- a/solution.py
+++ b/solution.py
@@ -11,6 +11,7 @@
 
 exact_mode = lax.Precision.HIGH
 F32 = jnp.float32
+PIECES = 1
 BF16 = jnp.bfloat16
 
 
@@ -105,18 +106,14 @@
 
 
 def gate_kernel(n, index_ref, *refs):
-    sums = refs[: 2 * n]
-    grad_in_ref, tap_ref, table_ref, inverse_ref = refs[2 * n : 2 * n + 4]
-    far_ref, near_ref, gated_ref, held = refs[2 * n + 4 :]
+    blocks, refs = refs[:n], refs[n:]
+    grad_in_ref, tap_ref, table_ref, inverse_ref = refs[:4]
+    kept_ref, gated_ref, held, lent = refs[4], refs[5], refs[-1], refs[6:-1]
     c = index_ref[1]
     half, size = n // 2, tap_ref.shape[0]
     bits = n.bit_length() - 1
-    for part in range(2):
-        total = sums[part * n][...].astype(F32)
-        for r in range(1, n):
-            total = total + sums[part * n + r][...].astype(F32)
-        for j in range(half):
-            held[c ^ (part * half + j)] = total[j].astype(BF16)
+    for j in range(n):
+        held[c ^ j] = blocks[j][...]
     values = held[...].reshape(n * size, size)
     table, inverse = table_ref[...], inverse_ref[...]
     tr, ti = tap_ref[:, :size], tap_ref[:, size:]
@@ -141,11 +138,12 @@
     back = (through + grad * medium * gate * (1.0 - gate)).astype(BF16)
     held[...] = back.reshape(n, size, size)
     for j in range(half):
-        near_ref[j] = held[reverse_bits(c ^ j, bits)]
-        far_ref[j] = held[reverse_bits(c ^ (half + j), bits)]
-
-
-def long_kernel(n, index_ref, gated_ref, filt_ref, table_ref, inverse_ref, *refs):
+        target = lent[j - 1] if j else kept_ref
+        target[0] = held[reverse_bits(c ^ (half + j), bits)]
+        target[1] = held[reverse_bits(c ^ j, bits)]
+
+
+def long_kernel(n, index_ref, near_ref, gated_ref, filt_ref, table_ref, inverse_ref, *refs):
     outs, held = refs[:n], refs[n]
     s = index_ref[0]
     size = gated_ref.shape[2]
@@ -167,15 +165,16 @@
     out = from_spectrum(jnp.concatenate(real), jnp.concatenate(imag), inverse_ref[...])
     held[...] = out.astype(BF16).reshape(n, size, size)
     for r in range(n):
-        outs[r][...] = held[s ^ r]
+        outs[r][: n // 2] = near_ref[...]
+        outs[r][n // 2] = held[s ^ r]
 
 
 def place_kernel(n, index_ref, *refs):
     given, out_ref = refs[:n], refs[n]
     s = index_ref[0]
-    size = given[0].shape[0]
+    size = given[0].shape[1]
     for r in range(n):
-        out_ref[pl.ds(pl.multiple_of((s ^ r) * size, size), size), :] = given[r][...]
+        out_ref[pl.ds(pl.multiple_of((s ^ r) * size, size), size), :] = given[r][n // 2]
 
 
 def arrange_kernel(n, index_ref, given_ref, filters_ref, cotangent_ref, *refs):
@@ -191,33 +190,57 @@
         turned_ref[r * size : (r + 1) * size, :] = block.T
 
 
-def values_kernel(n, weight_ref, *refs):
-    acts, outs = refs[: n // 2], refs[n // 2 :]
-    size = acts[0].shape[1]
-    right = jnp.concatenate([ref[...] for ref in acts], axis=1)
-    step = weight_ref.shape[0] // n
-    for r in range(n):
-        out = matmul(weight_ref[r * step : (r + 1) * step, :], right).astype(BF16)
-        for j in range(n // 2):
-            outs[r][j] = out[:, j * size : (j + 1) * size]
-
-
-def input_kernel(n, weight_ref, *refs):
-    grads, outs = refs[:n], refs[n:]
+def values_kernel(n, *refs):
     half = n // 2
-    size = grads[0].shape[2]
-    right = jnp.concatenate(
-        [jnp.concatenate([ref[j] for j in range(half)], axis=1) for ref in grads], axis=0
-    )
-    out = matmul(weight_ref[...], right)
+    weights, (upper_ref, lower_ref), outs = refs[:half], refs[half : half + 2], refs[half + 2 :]
+    right = jnp.concatenate([upper_ref[...], lower_ref[...]], axis=0)
+    step = weights[0].shape[0] // n
     for j in range(half):
-        outs[j][...] = out[:, j * size : (j + 1) * size].astype(outs[j].dtype)
-
-
-def call(kernel, outs, scratch, index, args, flops):
+        out = matmul(weights[j][...], right).astype(BF16)
+        for r in range(n):
+            outs[r][j] = out[r * step : (r + 1) * step]
+
+
+def sum_kernel(n, *refs):
+    terms, outs = refs[: -(n // 2)], refs[-(n // 2) :]
+    for j, out_ref in enumerate(outs):
+        total = terms[0][j].astype(F32)
+        for term in terms[1:]:
+            total = total + term[j].astype(F32)
+        out_ref[...] = total.astype(BF16)
+
+
+def input_kernel(n, *refs):
+    half = n // 2
+    weights, grads, outs = refs[:half], refs[half : half + n], refs[half + n :]
+    total = 0.0
+    for j in range(half):
+        right = jnp.concatenate([ref[j] for ref in grads], axis=0)
+        total = total + matmul(weights[j][...], right)
+    rows = outs[0].shape[0]
+    for k, out_ref in enumerate(outs):
+        out_ref[...] = total[k * rows : (k + 1) * rows].astype(out_ref.dtype)
+
+
+def total_kernel(k, near_ref, far_ref, out_ref):
+    rows = far_ref.shape[0]
+    near = near_ref[k * rows : (k + 1) * rows, :]
+    out_ref[...] = (near + far_ref[...].astype(F32)).astype(BF16)
+
+
+def cut_kernel(rows, given_ref, lower_ref, upper_ref, done):
+    low = pltpu.make_async_copy(given_ref.at[rows:], lower_ref, done.at[0])
+    high = pltpu.make_async_copy(given_ref.at[:rows], upper_ref, done.at[1])
+    low.start()
+    high.start()
+    low.wait()
+    high.wait()
+
+
+def call(kernel, outs, scratch, index, args, flops, place=pltpu.VMEM):
     sizes = sum(math.prod(a.shape) * a.dtype.itemsize for a in (*args, *outs))
-    held = sum(math.prod(a.shape) * jnp.dtype(a.dtype).itemsize for a in scratch)
-    specs = [pl.BlockSpec(memory_space=pltpu.VMEM)] * len(args)
+    held = sum(math.prod(a.shape) * 4 for a in scratch)
+    specs = [pl.BlockSpec(memory_space=place)] * len(args)
     if index is not None:
         specs = [pl.BlockSpec(memory_space=pltpu.SMEM)] + specs
         args = (index, *args)
@@ -249,8 +272,8 @@
         ]
         return lax.ppermute(array, ("seq", "ch"), pairs)
 
-    def across_seq(array, r):
-        return move(array, lambda i, j: (i ^ r, j))
+    def across_seq(array, step):
+        return move(array, lambda i, j: (i ^ step, j))
 
     def across_ch(array, r):
         return move(array, lambda i, j: (i, j ^ r))
@@ -258,14 +281,30 @@
     def spread(parts):
         return [parts[0]] + [across_seq(parts[r], r) for r in range(1, n)]
 
-    def gather_low(block):
-        held = [block]
-        while len(held) < half:
-            step = len(held)
-            held = held + [across_ch(x, step) for x in held]
-        return held
-
-    act = move(activations, lambda i, j: (j, i))
+    def share_seq(part):
+        held, step = {0: part}, n // 2
+        while step:
+            for r in list(held):
+                held[r | step] = across_seq(held[r], step)
+            step //= 2
+        return [held[r] for r in range(n)]
+
+    def lend(parts):
+        return [parts[0]] + [across_ch(parts[j], j) for j in range(1, half)]
+
+    low_rows = 3 * depth // 8
+    lower, upper = call(
+        functools.partial(cut_kernel, depth - low_rows),
+        [shape((low_rows, size), BF16), shape((depth - low_rows, size), BF16)],
+        [pltpu.SemaphoreType.DMA((2,))],
+        None,
+        (activations,),
+        0,
+        place=pl.ANY,
+    )
+    moved = across_ch(lower, half)
+    upper = move(upper, lambda i, j: (j, i))
+    lower = move(moved, lambda i, j: (j ^ half, i))
     weight, weight_t, *blocks = call(
         functools.partial(arrange_kernel, n),
         [shape(projection.shape, BF16), shape(projection.shape[::-1], BF16)]
@@ -276,24 +315,36 @@
         0,
     )
     table, inverse = block_tables(size)
-    act, weight, weight_t, table, inverse, *blocks = lax.optimization_barrier(
-        (act, weight, weight_t, table, inverse, *blocks)
-    )
-
-    def values_of(acts):
-        return call(
+    weight, weight_t, table, inverse, *blocks = lax.optimization_barrier(
+        (weight, weight_t, table, inverse, *blocks)
+    )
+
+    weights, weights_t = lend([weight] * half), lend([weight_t] * half)
+
+    def values_of(upper, lower):
+        parts = call(
             functools.partial(values_kernel, n),
             [shape((half, own, size), BF16)] * n,
             [],
             None,
-            (weight_t, *acts),
+            (*weights_t, upper, lower),
             2 * depth * n * own * half * size,
         )
-
-    far_act = across_ch(act, half)
+        terms = spread(parts)
+        sums = call(
+            functools.partial(sum_kernel, n),
+            [shape((own, size), BF16)] * half,
+            [],
+            None,
+            tuple(terms),
+            n * half * own * size,
+        )
+        return lend(sums)
+
+    far_upper, far_lower = across_ch(upper, half), across_ch(lower, half)
     blocks = spread(blocks)
-    near_sums = spread(values_of(gather_low(act)))
-    far_sums = spread(values_of(gather_low(far_act)))
+    near_values = values_of(upper, lower)
+    far_values = values_of(far_upper, far_lower)
 
     spectrum = 4 * n * size * 2 * size * own
     grad_gated, filt, tap = call(
@@ -304,57 +355,60 @@
         (*blocks, medium_taps, table, inverse),
         6 * spectrum,
     )
-    far, near, gated = call(
+    kept, gated, *lent = call(
         functools.partial(gate_kernel, n),
-        [shape((half, own, size), BF16), shape((half, own, size), BF16), shape((n, own, size), BF16)],
+        [shape((2, own, size), BF16), shape((n, own, size), BF16)]
+        + [shape((2, own, size), BF16)] * (half - 1),
         [pltpu.VMEM((n, own, size), BF16)],
         index,
-        (*near_sums, *far_sums, grad_gated, tap, table, inverse),
+        (*near_values, *far_values, grad_gated, tap, table, inverse),
         8 * spectrum,
     )
-    far_back = spread([far] * n)
-    near_back = spread([near] * n)
-
-    out_blocks = call(
+    pairs = lend([kept, *lent])
+    far_back = share_seq(jnp.stack([pair[0] for pair in pairs]))
+    near = jnp.stack([pair[1] for pair in pairs])
+
+    near_back = call(
         functools.partial(long_kernel, n),
-        [shape((own, size), BF16)] * n,
+        [shape((half + 1, own, size), BF16)] * n,
         [pltpu.VMEM((n, own, size), BF16)],
         index,
-        (gated, filt, table, inverse),
+        (near, gated, filt, table, inverse),
         4 * spectrum,
     )
-    out_blocks = spread(out_blocks)
-
-    def input_of(parts):
-        outs = [shape((depth, size), F32 if j < max(half // 2, 1) else BF16) for j in range(half)]
+    near_back = spread(near_back)
+
+    def input_of(parts, kind, pieces):
         return call(
             functools.partial(input_kernel, n),
-            outs,
+            [shape((depth // pieces, size), kind)] * pieces,
             [],
             None,
-            (weight, *parts),
+            (*weights, *parts),
             2 * depth * n * own * half * size,
         )
 
-    def scatter_low(sums):
-        while len(sums) > 1:
-            step = len(sums) // 2
-            kept = sums[:step]
-            sent = [across_ch(x.astype(BF16), step) for x in sums[step:]]
-            sums = [a.astype(F32) + b.astype(F32) for a, b in zip(kept, sent)]
-        return sums[0]
-
-    far_total = scatter_low(list(input_of(far_back))).astype(BF16)
-    far_total = across_ch(far_total, half)
-    total = scatter_low(list(input_of(near_back)))
-    total = total + far_total.astype(F32)
-    input_grad = move(total.astype(BF16), lambda i, j: (reverse_bits(j, bits), i))
+    far_total = input_of(far_back, BF16, PIECES)
+    (near_total,) = input_of(near_back, F32, 1)
+    homes = []
+    for k in range(PIECES):
+        moved = across_ch(far_total[k], half)
+        (total,) = call(
+            functools.partial(total_kernel, k),
+            [shape((depth // PIECES, size), BF16)],
+            [],
+            None,
+            (near_total, moved),
+            depth // PIECES * size,
+        )
+        homes.append(move(total, lambda i, j: (reverse_bits(j, bits), i)))
+    input_grad = jnp.concatenate(homes) if PIECES > 1 else homes[0]
     (conv_out,) = call(
         functools.partial(place_kernel, n),
         [shape((n * own, size), BF16)],
         [],
         index,
-        tuple(out_blocks),
+        tuple(near_back),
         0,
     )
     return conv_out, input_grad

time: 93.8 us -> 88.7 us (0.946)
  the two profiles are of different devices: /device:TPU:0 before, /device:TPU:1 now
where the time goes in v3:
time: 88.7 us; the launch traced here: 88.5 us
  starting transfers between devices  40.3 us (45%)
  waiting for transfers between devices  33.9 us (38%)
  Pallas kernels  8.93 us (10%)
  local copies, waits for them, and re-layouts  3.71 us (4%)
  between operations  0.89 us (1%)
    ppermute x27, starting transfers between devices, move(): return lax.ppermute(array, ('seq', 'ch'), pairs)  40.3 us
    ppermute x27, waiting for transfers between devices, move(): return lax.ppermute(array, ('seq', 'ch'), pairs)  33.9 us
    pallas_call x13, Pallas kernels, call(): pl.pallas_call(kernel, out_shape=tuple(outs), in_specs=specs, out_specs=t...  8.93 us
    unnamed x11, local copies, waits for them, and re-layouts  3.7 us
  transfers between devices with their start and end apart: 27, of which 13 were waited for; matrix products, arithmetic and copies ran while one was open for 0% of the time, Pallas kernels for 8%

profile of v3, /device:TPU:1, one launch (start us, length us, event | category | flops | bytes accessed | tf_op | source)
XLA Modules:
  0.0 88.5 jit_solution(1597769216313249938)
XLA Ops:
  1.4 0.9 copy-done.2
  2.3 1.2 %copy-done = bf16[1024,512]{1,0:T(8,128)(2,1)S(1)} copy-done((bf16[1024,512]{1,0:T(8,128)(2,1)S(1)}, bf16[1024,512]{1,0:T(8,128)(2,1)}, u32[]{:S(2)}) %copy-start) | copy-done | bytes 1048600
  3.5 1.0 %shard_map.68 = (bf16[1024,512]{1,0:T(8,128)(2,1)S(1)}, bf16[512,1024]{1,0:T(8,128)(2,1)S(1)}, bf16[2,128,128]{2,1,0:T(8,128)(2,1)S(1)}, bf16[2,128,128]{2,1,0:T...) custom-call(s32[2]{0:T(128)S(1)} %pad_add_fusion.index_ref, ...), custom_call_target="tpu_custom_call" | custom-call | bytes 3670016 | tf_op jit(solution)/shard_map/pallas_call | solution.py:247
  4.6 0.8 copy-done.1
  5.8 4.6 %collective-permute-start.1 = (bf16[640,128]{1,0:T(8,128)(2,1)S(1)}, bf16[640,128]{1,0:T(8,128)(2,1)S(1)}, u32[]{:S(2)}, u32[]{:S(2)}) collective-permute-start(bf16[640,128]{1,0:T(8,128)(2,1)S(1)} %get-tuple-element.47), channel_id=1, source_target_pairs={{0,0},{1,4},{2,8},{3,12},{4,1},{5,5},{6,9},{7,13},{8,2},{9,6},{10,... | collective-permute-start | bytes 491528 | tf_op jit(solution)/shard_map/ppermute | solution.py:273
  10.4 3.3 %collective-permute-start.2 = (bf16[384,128]{1,0:T(8,128)(2,1)S(1)}, bf16[384,128]{1,0:T(8,128)(2,1)S(1)}, u32[]{:S(2)}, u32[]{:S(2)}) collective-permute-start(bf16[384,128]{1,0:T(8,128)(2,1)S(1)} %get-tuple-element.48), channel_id=1, source_target_pairs={{0,2},{1,3},{2,0},{3,1},{4,6},{5,7},{6,4},{7,5},{8,10},{9,11},{10,... | collective-permute-start | bytes 294920 | tf_op jit(solution)/shard_map/ppermute | solution.py:273
  13.6 4.9 %collective-permute-done.2 = bf16[384,128]{1,0:T(8,128)(2,1)S(1)} collective-permute-done((bf16[384,128]{1,0:T(8,128)(2,1)S(1)}, bf16[384,128]{1,0:T(8,128)(2,1)S(1)}, u32[]{:S(2)}, u32[]{:S(2)}) %collective-permute-start.2) | collective-permute-done | bytes 98336 | tf_op jit(solution)/shard_map/ppermute | solution.py:273
  18.9 2.0 %collective-permute-start.8 = (bf16[640,128]{1,0:T(8,128)(2,1)S(1)}, bf16[640,128]{1,0:T(8,128)(2,1)S(1)}, u32[]{:S(2)}, u32[]{:S(2)}) collective-permute-start(bf16[640,128]{1,0:T(8,128)(2,1)S(1)} %collective-permute-done.1.refs_2_), channel_id=1, source_target_pairs={{0,2},{1,3},{2,0},{3,1},{4,6},{5,7},{6,4},{7,5},{8,10},{9,11},{10,... | collective-permute-start | bytes 491528 | tf_op jit(solution)/shard_map/ppermute | solution.py:273
  20.9 1.7 %collective-permute-start.21 = (bf16[1024,512]{1,0:T(8,128)(2,1)S(1)}, bf16[1024,512]{1,0:T(8,128)(2,1)S(1)}, u32[]{:S(2)}, u32[]{:S(2)}) collective-permute-start(bf16[1024,512]{1,0:T(8,128)(2,1)S(1)} %get-tuple-element.77.refs_0_), channel_id=1, source_target_pairs={{0,1},{1,0},{2,3},{3,2},{4,5},{5,4},{6,7},{7,6},{8,9},{9,8},{10,11... | collective-permute-start | bytes 3145736 | tf_op jit(solution)/shard_map/ppermute | solution.py:273
  22.6 1.0 %collective-permute-done.3.refs_3_ = bf16[384,128]{1,0:T(8,128)(2,1)S(1)} collective-permute-done((bf16[384,128]{1,0:T(8,128)(2,1)S(1)}, bf16[384,128]{1,0:T(8,128)(2,1)S(1)}, u32[]{:S(2)}, u32[]{:S(2)}) %collective-permute-start.3) | collective-permute-done | bytes 98336 | tf_op jit(solution)/shard_map/ppermute | solution.py:273
  23.6 3.2 %collective-permute-start.9 = (bf16[384,128]{1,0:T(8,128)(2,1)S(1)}, bf16[384,128]{1,0:T(8,128)(2,1)S(1)}, u32[]{:S(2)}, u32[]{:S(2)}) collective-permute-start(bf16[384,128]{1,0:T(8,128)(2,1)S(1)} %collective-permute-done.3.refs_3_), channel_id=1, source_target_pairs={{0,2},{1,3},{2,0},{3,1},{4,6},{5,7},{6,4},{7,5},{8,10},{9,11},{10,... | collective-permute-start | bytes 294920 | tf_op jit(solution)/shard_map/ppermute | solution.py:273
  27.7 1.1 %collective-permute-done.9.refs_3_ = bf16[384,128]{1,0:T(8,128)(2,1)S(1)} collective-permute-done((bf16[384,128]{1,0:T(8,128)(2,1)S(1)}, bf16[384,128]{1,0:T(8,128)(2,1)S(1)}, u32[]{:S(2)}, u32[]{:S(2)}) %collective-permute-start.9) | collective-permute-done | bytes 98336 | tf_op jit(solution)/shard_map/ppermute | solution.py:273
  28.8 2.3 %collective-permute-start.6 = (bf16[2,128,128]{2,1,0:T(8,128)(2,1)S(1)}, bf16[2,128,128]{2,1,0:T(8,128)(2,1)S(1)}, u32[]{:S(2)}, u32[]{:S(2)}) collective-permute-start(bf16[2,128,128]{2,1,0:T(8,128)(2,1)S(1)} %get-tuple-element.52), channel_id=1, source_target_pairs={{0,12},{1,13},{2,14},{3,15},{4,8},{5,9},{6,10},{7,11},{8,4},{9,5},... | collective-permute-start | bytes 196616 | tf_op jit(solution)/shard_map/ppermute | solution.py:273
  31.9 1.2 %collective-permute-start.11 = (bf16[2,128,128]{2,1,0:T(8,128)(2,1)S(1)}, bf16[2,128,128]{2,1,0:T(8,128)(2,1)S(1)}, u32[]{:S(2)}, u32[]{:S(2)}) collective-permute-start(bf16[2,128,128]{2,1,0:T(8,128)(2,1)S(1)} %get-tuple-element.57), channel_id=1, source_target_pairs={{0,8},{1,9},{2,10},{3,11},{4,12},{5,13},{6,14},{7,15},{8,0},{9,1},... | collective-permute-start | bytes 196616 | tf_op jit(solution)/shard_map/ppermute | solution.py:273
  33.2 2.3 %collective-permute-start.12 = (bf16[2,128,128]{2,1,0:T(8,128)(2,1)S(1)}, bf16[2,128,128]{2,1,0:T(8,128)(2,1)S(1)}, u32[]{:S(2)}, u32[]{:S(2)}) collective-permute-start(bf16[2,128,128]{2,1,0:T(8,128)(2,1)S(1)} %get-tuple-element.58), channel_id=1, source_target_pairs={{0,12},{1,13},{2,14},{3,15},{4,8},{5,9},{6,10},{7,11},{8,4},{9,5},... | collective-permute-start | bytes 196616 | tf_op jit(solution)/shard_map/ppermute | solution.py:273
  35.7 1.0 %collective-permute-start.15 = (bf16[2,128,128]{2,1,0:T(8,128)(2,1)S(1)}, bf16[2,128,128]{2,1,0:T(8,128)(2,1)S(1)}, u32[]{:S(2)}, u32[]{:S(2)}) collective-permute-start(bf16[2,128,128]{2,1,0:T(8,128)(2,1)S(1)} %get-tuple-element.63), channel_id=1, source_target_pairs={{0,8},{1,9},{2,10},{3,11},{4,12},{5,13},{6,14},{7,15},{8,0},{9,1},... | collective-permute-start | bytes 196616 | tf_op jit(solution)/shard_map/ppermute | solution.py:273
  36.7 2.4 %collective-permute-done.11.refs_2_ = bf16[2,128,128]{2,1,0:T(8,128)(2,1)S(1)} collective-permute-done((bf16[2,128,128]{2,1,0:T(8,128)(2,1)S(1)}, bf16[2,128,128]{2,1,0:T(8,128)(2,1)S(1)}, u32[]{:S(2)}, u32[]{:S(2)}) %collective-permute-start.11) | collective-permute-done | bytes 65568 | tf_op jit(solution)/shard_map/ppermute | solution.py:273
  39.6 3.3 %collective-permute-start.7 = (bf16[128,128]{1,0:T(8,128)(2,1)S(1)}, bf16[128,128]{1,0:T(8,128)(2,1)S(1)}, u32[]{:S(2)}, u32[]{:S(2)}) collective-permute-start(bf16[128,128]{1,0:T(8,128)(2,1)S(1)} %get-tuple-element.54), channel_id=1, source_target_pairs={{0,1},{1,0},{2,3},{3,2},{4,5},{5,4},{6,7},{7,6},{8,9},{9,8},{10,11... | collective-permute-start | bytes 98312 | tf_op jit(solution)/shard_map/ppermute | solution.py:273
  43.2 2.2 %collective-permute-done.15.refs_2_ = bf16[2,128,128]{2,1,0:T(8,128)(2,1)S(1)} collective-permute-done((bf16[2,128,128]{2,1,0:T(8,128)(2,1)S(1)}, bf16[2,128,128]{2,1,0:T(8,128)(2,1)S(1)}, u32[]{:S(2)}, u32[]{:S(2)}) %collective-permute-start.15) | collective-permute-done | bytes 65568 | tf_op jit(solution)/shard_map/ppermute | solution.py:273
  45.5 1.2 %shard_map.74 = (bf16[4,128,128]{2,1,0:T(8,128)(2,1)S(1)}, f32[512,256]{1,0:T(8,128)S(1)}, f32[128,256]{1,0:T(8,128)S(1)}) custom-call(s32[2]{0:T(128)S(1)} %pad_add_fusion.index_ref, bf16[2,128,128]{2,1,0:T(8,128)(2,1)S(1)} %get-tuple-element.61.refs_0_, bf16[2,128,128]{2,1,0:T(8,128)(2,1)S(1)} %collective-permute-done.14.refs_1_, ...), custom_call_target="tpu_custom_call" | custom-call | flops 402653184 | bytes 1572864 | tf_op jit(solution)/shard_map/pallas_call | solution.py:247
  46.7 1.2 %shard_map.75 = (bf16[2,128,128]{2,1,0:T(8,128)(2,1)S(1)}, bf16[4,128,128]{2,1,0:T(8,128)(2,1)S(1)}, bf16[2,128,128]{2,1,0:T(8,128)(2,1)S(1)}) custom-call(s32[2]{0:T(128)S(1)} %pad_add_fusion.index_ref, bf16[128,128]{1,0:T(8,128)(2,1)S(1)} %get-tuple-element.53.refs_0_, bf16[128,128]{1,0:T(8,128)(2,1)S(1)} %collective-permute-done.7.refs_1_, ...), custom_call_target="tpu_custom_call" | custom-call | flops 536870912 | bytes 917504 | tf_op jit(solution)/shard_map/pallas_call | solution.py:247
  47.9 3.5 %collective-permute-start.17 = (bf16[2,128,128]{2,1,0:T(8,128)(2,1)S(1)}, bf16[2,128,128]{2,1,0:T(8,128)(2,1)S(1)}, u32[]{:S(2)}, u32[]{:S(2)}) collective-permute-start(bf16[2,128,128]{2,1,0:T(8,128)(2,1)S(1)} %get-tuple-element.70), channel_id=1, source_target_pairs={{0,1},{1,0},{2,3},{3,2},{4,5},{5,4},{6,7},{7,6},{8,9},{9,8},{10,11... | collective-permute-start | bytes 196616 | tf_op jit(solution)/shard_map/ppermute | solution.py:273
  51.4 0.9 %collective-permute-done.17 = bf16[2,128,128]{2,1,0:T(8,128)(2,1)S(1)} collective-permute-done((bf16[2,128,128]{2,1,0:T(8,128)(2,1)S(1)}, bf16[2,128,128]{2,1,0:T(8,128)(2,1)S(1)}, u32[]{:S(2)}, u32[]{:S(2)}) %collective-permute-start.17) | collective-permute-done | bytes 65568 | tf_op jit(solution)/shard_map/ppermute | solution.py:273
  52.6 5.0 %collective-permute-done.23.refs_4_ = bf16[2,128,128]{2,1,0:T(8,128)(2,1)S(1)} collective-permute-done((bf16[2,128,128]{2,1,0:T(8,128)(2,1)S(1)}, bf16[2,128,128]{2,1,0:T(8,128)(2,1)S(1)}, u32[]{:S(2)}, u32[]{:S(2)}) %collective-permute-start.23) | collective-permute-done | bytes 65568 | tf_op jit(solution)/shard_map/ppermute | solution.py:273
  57.6 3.1 %collective-permute-done.24.refs_5_ = bf16[2,128,128]{2,1,0:T(8,128)(2,1)S(1)} collective-permute-done((bf16[2,128,128]{2,1,0:T(8,128)(2,1)S(1)}, bf16[2,128,128]{2,1,0:T(8,128)(2,1)S(1)}, u32[]{:S(2)}, u32[]{:S(2)}) %collective-permute-start.24) | collective-permute-done | bytes 65568 | tf_op jit(solution)/shard_map/ppermute | solution.py:273
  61.6 1.1 %shard_map.76 = (bf16[3,128,128]{2,1,0:T(8,128)(2,1)S(1)}, bf16[3,128,128]{2,1,0:T(8,128)(2,1)S(1)}, bf16[3,128,128]{2,1,0:T(8,128)(2,1)S(1)}, bf16[3,128,128]{2,1,0:T(8,128)(2,1)S(1)}) custom-call(s32[2]{0:T(128)S(1)} %pad_add_fusion.index_ref, bf16[2,128,128]{2,1,0:T(8,128)(2,1)S(1)} %pad_maximum_fusion.3.near_ref, ...), custom_call_target="tpu_custom_call" | custom-call | flops 268435456 | bytes 1376256 | tf_op jit(solution)/shard_map/pallas_call | solution.py:247
  62.9 3.5 %collective-permute-start.20 = (bf16[3,128,128]{2,1,0:T(8,128)(2,1)S(1)}, bf16[3,128,128]{2,1,0:T(8,128)(2,1)S(1)}, u32[]{:S(2)}, u32[]{:S(2)}) collective-permute-start(bf16[3,128,128]{2,1,0:T(8,128)(2,1)S(1)} %get-tuple-element.76), channel_id=1, source_target_pairs={{0,12},{1,13},{2,14},{3,15},{4,8},{5,9},{6,10},{7,11},{8,4},{9,5},... | collective-permute-start | bytes 294920 | tf_op jit(solution)/shard_map/ppermute | solution.py:273
  66.6 0.7 collective-permute-done.19.refs_2_.refs_4_
  67.3 3.5 %collective-permute-done.20.refs_3_.refs_5_ = bf16[3,128,128]{2,1,0:T(8,128)(2,1)S(1)} collective-permute-done((bf16[3,128,128]{2,1,0:T(8,128)(2,1)S(1)}, bf16[3,128,128]{2,1,0:T(8,128)(2,1)S(1)}, u32[]{:S(2)}, u32[]{:S(2)}) %collective-permute-start.20) | collective-permute-done | bytes 98336 | tf_op jit(solution)/shard_map/ppermute | solution.py:273
  71.6 6.5 %collective-permute-start.26 = (bf16[1024,128]{1,0:T(8,128)(2,1)S(1)}, bf16[1024,128]{1,0:T(8,128)(2,1)S(1)}, u32[]{:S(2)}, u32[]{:S(2)}) collective-permute-start(bf16[1024,128]{1,0:T(8,128)(2,1)S(1)} %shard_map.80), channel_id=1, source_target_pairs={{0,0},{1,8},{2,4},{3,12},{4,1},{5,9},{6,5},{7,13},{8,2},{9,10},{10... | collective-permute-start | bytes 786440 | tf_op jit(solution)/shard_map/ppermute | solution.py:273
  78.1 1.2 %shard_map.77 = bf16[512,128]{1,0:T(8,128)(2,1)} custom-call(s32[2]{0:T(128)S(1)} %pad_add_fusion.index_ref, bf16[3,128,128]{2,1,0:T(8,128)(2,1)S(1)} %get-tuple-element.73.refs_0_.refs_2_, bf16[3,128,128]{2,1,0:T(8,128)(2,1)S(1)} %collective-permute-done.18.refs_1_.refs_3_, bf16[3,128,128]{2,1,0:T(8,128)(2,1)S(1)} %collective-permute-done.19.refs_2_.refs_4_, ...), custom_call_target="tpu_custom_call" | custom-call | bytes 524288 | tf_op jit(solution)/shard_map/pallas_call | solution.py:247
  79.3 8.5 %collective-permute-done.26 = bf16[1024,128]{1,0:T(8,128)(2,1)S(1)} collective-permute-done((bf16[1024,128]{1,0:T(8,128)(2,1)S(1)}, bf16[1024,128]{1,0:T(8,128)(2,1)S(1)}, u32[]{:S(2)}, u32[]{:S(2)}) %collective-permute-start.26) | collective-permute-done | bytes 262176 | tf_op jit(solution)/shard_map/ppermute | solution.py:273
  (57 shorter events, 7.3 us)
Async XLA Ops:
  1.3 0.9 %copy-start.2 = (bf16[512,128]{1,0:T(8,128)(2,1)S(1)}, bf16[512,128]{1,0:T(8,128)(2,1)}, u32[]{:S(2)}) copy-start(bf16[512,128]{1,0:T(8,128)(2,1)} %filters_ref.1) | copy-start | bytes 393220
  1.3 1.0 %copy-start.3 = (bf16[512,128]{1,0:T(8,128)(2,1)S(1)}, bf16[512,128]{1,0:T(8,128)(2,1)}, u32[]{:S(2)}) copy-start(bf16[512,128]{1,0:T(8,128)(2,1)} %cotangent_ref.1) | copy-start | bytes 393220
  2.3 1.2 %copy-start = (bf16[1024,512]{1,0:T(8,128)(2,1)S(1)}, bf16[1024,512]{1,0:T(8,128)(2,1)}, u32[]{:S(2)}) copy-start(bf16[1024,512]{1,0:T(8,128)(2,1)} %given_ref.2) | copy-start | bytes 3145732
  4.5 1.0 %copy-start.1 = (bf16[1024,128]{1,0:T(8,128)(2,1)S(1)}, bf16[1024,128]{1,0:T(8,128)(2,1)}, u32[]{:S(2)}) copy-start(bf16[1024,128]{1,0:T(8,128)(2,1)} %given_ref.3) | copy-start | bytes 786436
  4.5 22.3 %collective-permute-start = (bf16[512,1024]{1,0:T(8,128)(2,1)S(1)}, bf16[512,1024]{1,0:T(8,128)(2,1)S(1)}, u32[]{:S(2)}, u32[]{:S(2)}) collective-permute-start(bf16[512,1024]{1,0:T(8,128)(2,1)S(1)} %get-tuple-element.46.refs_0_), channel_id=1, source_target_pairs={{0,1},{1,0},{2,3},{3,2},{4,5},{5,4},{6,7},{7,6},{8,9},{9,8},{10,11... | collective-permute-start | bytes 3145736 | tf_op jit(solution)/shard_map/ppermute | solution.py:273
  5.8 13.1 %collective-permute-start.1 = (bf16[640,128]{1,0:T(8,128)(2,1)S(1)}, bf16[640,128]{1,0:T(8,128)(2,1)S(1)}, u32[]{:S(2)}, u32[]{:S(2)}) collective-permute-start(bf16[640,128]{1,0:T(8,128)(2,1)S(1)} %get-tuple-element.47), channel_id=1, source_target_pairs={{0,0},{1,4},{2,8},{3,12},{4,1},{5,5},{6,9},{7,13},{8,2},{9,6},{10,... | collective-permute-start | bytes 491528 | tf_op jit(solution)/shard_map/ppermute | solution.py:273
  10.4 8.2 %collective-permute-start.2 = (bf16[384,128]{1,0:T(8,128)(2,1)S(1)}, bf16[384,128]{1,0:T(8,128)(2,1)S(1)}, u32[]{:S(2)}, u32[]{:S(2)}) collective-permute-start(bf16[384,128]{1,0:T(8,128)(2,1)S(1)} %get-tuple-element.48), channel_id=1, source_target_pairs={{0,2},{1,3},{2,0},{3,1},{4,6},{5,7},{6,4},{7,5},{8,10},{9,11},{10,... | collective-permute-start | bytes 294920 | tf_op jit(solution)/shard_map/ppermute | solution.py:273
  18.5 5.0 %collective-permute-start.3 = (bf16[384,128]{1,0:T(8,128)(2,1)S(1)}, bf16[384,128]{1,0:T(8,128)(2,1)S(1)}, u32[]{:S(2)}, u32[]{:S(2)}) collective-permute-start(bf16[384,128]{1,0:T(8,128)(2,1)S(1)} %collective-permute-done.2), channel_id=1, source_target_pairs={{0,8},{1,12},{2,0},{3,4},{4,9},{5,13},{6,1},{7,5},{8,10},{9,14},{1... | collective-permute-start | bytes 294920 | tf_op jit(solution)/shard_map/ppermute | solution.py:273
  18.9 12.2 %collective-permute-start.8 = (bf16[640,128]{1,0:T(8,128)(2,1)S(1)}, bf16[640,128]{1,0:T(8,128)(2,1)S(1)}, u32[]{:S(2)}, u32[]{:S(2)}) collective-permute-start(bf16[640,128]{1,0:T(8,128)(2,1)S(1)} %collective-permute-done.1.refs_2_), channel_id=1, source_target_pairs={{0,2},{1,3},{2,0},{3,1},{4,6},{5,7},{6,4},{7,5},{8,10},{9,11},{10,... | collective-permute-start | bytes 491528 | tf_op jit(solution)/shard_map/ppermute | solution.py:273
  20.9 36.7 %collective-permute-start.21 = (bf16[1024,512]{1,0:T(8,128)(2,1)S(1)}, bf16[1024,512]{1,0:T(8,128)(2,1)S(1)}, u32[]{:S(2)}, u32[]{:S(2)}) collective-permute-start(bf16[1024,512]{1,0:T(8,128)(2,1)S(1)} %get-tuple-element.77.refs_0_), channel_id=1, source_target_pairs={{0,1},{1,0},{2,3},{3,2},{4,5},{5,4},{6,7},{7,6},{8,9},{9,8},{10,11... | collective-permute-start | bytes 3145736 | tf_op jit(solution)/shard_map/ppermute | solution.py:273
  23.6 5.2 %collective-permute-start.9 = (bf16[384,128]{1,0:T(8,128)(2,1)S(1)}, bf16[384,128]{1,0:T(8,128)(2,1)S(1)}, u32[]{:S(2)}, u32[]{:S(2)}) collective-permute-start(bf16[384,128]{1,0:T(8,128)(2,1)S(1)} %collective-permute-done.3.refs_3_), channel_id=1, source_target_pairs={{0,2},{1,3},{2,0},{3,1},{4,6},{5,7},{6,4},{7,5},{8,10},{9,11},{10,... | collective-permute-start | bytes 294920 | tf_op jit(solution)/shard_map/ppermute | solution.py:273
  27.5 4.4 %collective-permute-start.4 = (bf16[2,128,128]{2,1,0:T(8,128)(2,1)S(1)}, bf16[2,128,128]{2,1,0:T(8,128)(2,1)S(1)}, u32[]{:S(2)}, u32[]{:S(2)}) collective-permute-start(bf16[2,128,128]{2,1,0:T(8,128)(2,1)S(1)} %get-tuple-element.50), channel_id=1, source_target_pairs={{0,4},{1,5},{2,6},{3,7},{4,0},{5,1},{6,2},{7,3},{8,12},{9,13},{10,... | collective-permute-start | bytes 196616 | tf_op jit(solution)/shard_map/ppermute | solution.py:273
  27.6 5.5 %collective-permute-start.5 = (bf16[2,128,128]{2,1,0:T(8,128)(2,1)S(1)}, bf16[2,128,128]{2,1,0:T(8,128)(2,1)S(1)}, u32[]{:S(2)}, u32[]{:S(2)}) collective-permute-start(bf16[2,128,128]{2,1,0:T(8,128)(2,1)S(1)} %get-tuple-element.51), channel_id=1, source_target_pairs={{0,8},{1,9},{2,10},{3,11},{4,12},{5,13},{6,14},{7,15},{8,0},{9,1},... | collective-permute-start | bytes 196616 | tf_op jit(solution)/shard_map/ppermute | solution.py:273
  28.8 6.7 %collective-permute-start.6 = (bf16[2,128,128]{2,1,0:T(8,128)(2,1)S(1)}, bf16[2,128,128]{2,1,0:T(8,128)(2,1)S(1)}, u32[]{:S(2)}, u32[]{:S(2)}) collective-permute-start(bf16[2,128,128]{2,1,0:T(8,128)(2,1)S(1)} %get-tuple-element.52), channel_id=1, source_target_pairs={{0,12},{1,13},{2,14},{3,15},{4,8},{5,9},{6,10},{7,11},{8,4},{9,5},... | collective-permute-start | bytes 196616 | tf_op jit(solution)/shard_map/ppermute | solution.py:273
  31.9 3.8 %collective-permute-start.10 = (bf16[2,128,128]{2,1,0:T(8,128)(2,1)S(1)}, bf16[2,128,128]{2,1,0:T(8,128)(2,1)S(1)}, u32[]{:S(2)}, u32[]{:S(2)}) collective-permute-start(bf16[2,128,128]{2,1,0:T(8,128)(2,1)S(1)} %get-tuple-element.56), channel_id=1, source_target_pairs={{0,4},{1,5},{2,6},{3,7},{4,0},{5,1},{6,2},{7,3},{8,12},{9,13},{10,... | collective-permute-start | bytes 196616 | tf_op jit(solution)/shard_map/ppermute | solution.py:273
  31.9 7.2 %collective-permute-start.11 = (bf16[2,128,128]{2,1,0:T(8,128)(2,1)S(1)}, bf16[2,128,128]{2,1,0:T(8,128)(2,1)S(1)}, u32[]{:S(2)}, u32[]{:S(2)}) collective-permute-start(bf16[2,128,128]{2,1,0:T(8,128)(2,1)S(1)} %get-tuple-element.57), channel_id=1, source_target_pairs={{0,8},{1,9},{2,10},{3,11},{4,12},{5,13},{6,14},{7,15},{8,0},{9,1},... | collective-permute-start | bytes 196616 | tf_op jit(solution)/shard_map/ppermute | solution.py:273
  33.2 6.4 %collective-permute-start.12 = (bf16[2,128,128]{2,1,0:T(8,128)(2,1)S(1)}, bf16[2,128,128]{2,1,0:T(8,128)(2,1)S(1)}, u32[]{:S(2)}, u32[]{:S(2)}) collective-permute-start(bf16[2,128,128]{2,1,0:T(8,128)(2,1)S(1)} %get-tuple-element.58), channel_id=1, source_target_pairs={{0,12},{1,13},{2,14},{3,15},{4,8},{5,9},{6,10},{7,11},{8,4},{9,5},... | collective-permute-start | bytes 196616 | tf_op jit(solution)/shard_map/ppermute | solution.py:273
  35.5 7.5 %collective-permute-start.14 = (bf16[2,128,128]{2,1,0:T(8,128)(2,1)S(1)}, bf16[2,128,128]{2,1,0:T(8,128)(2,1)S(1)}, u32[]{:S(2)}, u32[]{:S(2)}) collective-permute-start(bf16[2,128,128]{2,1,0:T(8,128)(2,1)S(1)} %get-tuple-element.62), channel_id=1, source_target_pairs={{0,4},{1,5},{2,6},{3,7},{4,0},{5,1},{6,2},{7,3},{8,12},{9,13},{10,... | collective-permute-start | bytes 196616 | tf_op jit(solution)/shard_map/ppermute | solution.py:273
  35.7 9.7 %collective-permute-start.15 = (bf16[2,128,128]{2,1,0:T(8,128)(2,1)S(1)}, bf16[2,128,128]{2,1,0:T(8,128)(2,1)S(1)}, u32[]{:S(2)}, u32[]{:S(2)}) collective-permute-start(bf16[2,128,128]{2,1,0:T(8,128)(2,1)S(1)} %get-tuple-element.63), channel_id=1, source_target_pairs={{0,8},{1,9},{2,10},{3,11},{4,12},{5,13},{6,14},{7,15},{8,0},{9,1},... | collective-permute-start | bytes 196616 | tf_op jit(solution)/shard_map/ppermute | solution.py:273
  39.1 6.3 %collective-permute-start.16 = (bf16[2,128,128]{2,1,0:T(8,128)(2,1)S(1)}, bf16[2,128,128]{2,1,0:T(8,128)(2,1)S(1)}, u32[]{:S(2)}, u32[]{:S(2)}) collective-permute-start(bf16[2,128,128]{2,1,0:T(8,128)(2,1)S(1)} %get-tuple-element.64), channel_id=1, source_target_pairs={{0,12},{1,13},{2,14},{3,15},{4,8},{5,9},{6,10},{7,11},{8,4},{9,5},... | collective-permute-start | bytes 196616 | tf_op jit(solution)/shard_map/ppermute | solution.py:273
  39.5 5.9 %copy-start.4 = (f32[512,128]{1,0:T(8,128)S(1)}, f32[512,128]{1,0:T(8,128)}, u32[]{:S(2)}) copy-start(f32[512,128]{1,0:T(8,128)} %refs_4_.1) | copy-start | bytes 786436
  39.6 7.1 %collective-permute-start.7 = (bf16[128,128]{1,0:T(8,128)(2,1)S(1)}, bf16[128,128]{1,0:T(8,128)(2,1)S(1)}, u32[]{:S(2)}, u32[]{:S(2)}) collective-permute-start(bf16[128,128]{1,0:T(8,128)(2,1)S(1)} %get-tuple-element.54), channel_id=1, source_target_pairs={{0,1},{1,0},{2,3},{3,2},{4,5},{5,4},{6,7},{7,6},{8,9},{9,8},{10,11... | collective-permute-start | bytes 98312 | tf_op jit(solution)/shard_map/ppermute | solution.py:273
  43.0 3.7 %collective-permute-start.13 = (bf16[128,128]{1,0:T(8,128)(2,1)S(1)}, bf16[128,128]{1,0:T(8,128)(2,1)S(1)}, u32[]{:S(2)}, u32[]{:S(2)}) collective-permute-start(bf16[128,128]{1,0:T(8,128)(2,1)S(1)} %get-tuple-element.60), channel_id=1, source_target_pairs={{0,1},{1,0},{2,3},{3,2},{4,5},{5,4},{6,7},{7,6},{8,9},{9,8},{10,11... | collective-permute-start | bytes 98312 | tf_op jit(solution)/shard_map/ppermute | solution.py:273
  47.9 4.4 %collective-permute-start.17 = (bf16[2,128,128]{2,1,0:T(8,128)(2,1)S(1)}, bf16[2,128,128]{2,1,0:T(8,128)(2,1)S(1)}, u32[]{:S(2)}, u32[]{:S(2)}) collective-permute-start(bf16[2,128,128]{2,1,0:T(8,128)(2,1)S(1)} %get-tuple-element.70), channel_id=1, source_target_pairs={{0,1},{1,0},{2,3},{3,2},{4,5},{5,4},{6,7},{7,6},{8,9},{9,8},{10,11... | collective-permute-start | bytes 196616 | tf_op jit(solution)/shard_map/ppermute | solution.py:273
  52.3 5.3 %collective-permute-start.23 = (bf16[2,128,128]{2,1,0:T(8,128)(2,1)S(1)}, bf16[2,128,128]{2,1,0:T(8,128)(2,1)S(1)}, u32[]{:S(2)}, u32[]{:S(2)}) collective-permute-start(bf16[2,128,128]{2,1,0:T(8,128)(2,1)S(1)} %pad_maximum_fusion.4.refs_2_), channel_id=1, source_target_pairs={{0,8},{1,9},{2,10},{3,11},{4,12},{5,13},{6,14},{7,15},{8,0},{9,1},... | collective-permute-start | bytes 196616 | tf_op jit(solution)/shard_map/ppermute | solution.py:273
  52.3 5.2 %collective-permute-start.22 = (bf16[2,128,128]{2,1,0:T(8,128)(2,1)S(1)}, bf16[2,128,128]{2,1,0:T(8,128)(2,1)S(1)}, u32[]{:S(2)}, u32[]{:S(2)}) collective-permute-start(bf16[2,128,128]{2,1,0:T(8,128)(2,1)S(1)} %pad_maximum_fusion.4.refs_2_), channel_id=1, source_target_pairs={{0,4},{1,5},{2,6},{3,7},{4,0},{5,1},{6,2},{7,3},{8,12},{9,13},{10,... | collective-permute-start | bytes 196616 | tf_op jit(solution)/shard_map/ppermute | solution.py:273
  57.6 3.1 %collective-permute-start.24 = (bf16[2,128,128]{2,1,0:T(8,128)(2,1)S(1)}, bf16[2,128,128]{2,1,0:T(8,128)(2,1)S(1)}, u32[]{:S(2)}, u32[]{:S(2)}) collective-permute-start(bf16[2,128,128]{2,1,0:T(8,128)(2,1)S(1)} %collective-permute-done.23.refs_4_), channel_id=1, source_target_pairs={{0,4},{1,5},{2,6},{3,7},{4,0},{5,1},{6,2},{7,3},{8,12},{9,13},{10,... | collective-permute-start | bytes 196616 | tf_op jit(solution)/shard_map/ppermute | solution.py:273
  61.4 10.1 %collective-permute-start.25 = (bf16[1024,128]{1,0:T(8,128)(2,1)S(1)}, bf16[1024,128]{1,0:T(8,128)(2,1)S(1)}, u32[]{:S(2)}, u32[]{:S(2)}) collective-permute-start(bf16[1024,128]{1,0:T(8,128)(2,1)S(1)} %shard_map.79), channel_id=1, source_target_pairs={{0,2},{1,3},{2,0},{3,1},{4,6},{5,7},{6,4},{7,5},{8,10},{9,11},{10,... | collective-permute-start | bytes 786440 | tf_op jit(solution)/shard_map/ppermute | solution.py:273
  62.7 3.8 %collective-permute-start.18 = (bf16[3,128,128]{2,1,0:T(8,128)(2,1)S(1)}, bf16[3,128,128]{2,1,0:T(8,128)(2,1)S(1)}, u32[]{:S(2)}, u32[]{:S(2)}) collective-permute-start(bf16[3,128,128]{2,1,0:T(8,128)(2,1)S(1)} %get-tuple-element.74), channel_id=1, source_target_pairs={{0,4},{1,5},{2,6},{3,7},{4,0},{5,1},{6,2},{7,3},{8,12},{9,13},{10,... | collective-permute-start | bytes 294920 | tf_op jit(solution)/shard_map/ppermute | solution.py:273
  62.8 4.5 %collective-permute-start.19 = (bf16[3,128,128]{2,1,0:T(8,128)(2,1)S(1)}, bf16[3,128,128]{2,1,0:T(8,128)(2,1)S(1)}, u32[]{:S(2)}, u32[]{:S(2)}) collective-permute-start(bf16[3,128,128]{2,1,0:T(8,128)(2,1)S(1)} %get-tuple-element.75), channel_id=1, source_target_pairs={{0,8},{1,9},{2,10},{3,11},{4,12},{5,13},{6,14},{7,15},{8,0},{9,1},... | collective-permute-start | bytes 294920 | tf_op jit(solution)/shard_map/ppermute | solution.py:273
  62.9 7.9 %collective-permute-start.20 = (bf16[3,128,128]{2,1,0:T(8,128)(2,1)S(1)}, bf16[3,128,128]{2,1,0:T(8,128)(2,1)S(1)}, u32[]{:S(2)}, u32[]{:S(2)}) collective-permute-start(bf16[3,128,128]{2,1,0:T(8,128)(2,1)S(1)} %get-tuple-element.76), channel_id=1, source_target_pairs={{0,12},{1,13},{2,14},{3,15},{4,8},{5,9},{6,10},{7,11},{8,4},{9,5},... | collective-permute-start | bytes 294920 | tf_op jit(solution)/shard_map/ppermute | solution.py:273
  71.6 16.2 %collective-permute-start.26 = (bf16[1024,128]{1,0:T(8,128)(2,1)S(1)}, bf16[1024,128]{1,0:T(8,128)(2,1)S(1)}, u32[]{:S(2)}, u32[]{:S(2)}) collective-permute-start(bf16[1024,128]{1,0:T(8,128)(2,1)S(1)} %shard_map.80), channel_id=1, source_target_pairs={{0,0},{1,8},{2,4},{3,12},{4,1},{5,9},{6,5},{7,13},{8,2},{9,10},{10... | collective-permute-start | bytes 786440 | tf_op jit(solution)/shard_map/ppermute | solution.py:273

commit v4 on v3

--- a/solution.py
+++ b/solution.py
@@ -113,7 +113,7 @@
     half, size = n // 2, tap_ref.shape[0]
     bits = n.bit_length() - 1
     for j in range(n):
-        held[c ^ j] = blocks[j][...]
+        held[c ^ j ^ half] = blocks[j][...]
     values = held[...].reshape(n * size, size)
     table, inverse = table_ref[...], inverse_ref[...]
     tr, ti = tap_ref[:, :size], tap_ref[:, size:]
@@ -139,8 +139,8 @@
     held[...] = back.reshape(n, size, size)
     for j in range(half):
         target = lent[j - 1] if j else kept_ref
-        target[0] = held[reverse_bits(c ^ (half + j), bits)]
-        target[1] = held[reverse_bits(c ^ j, bits)]
+        target[0] = held[reverse_bits(c ^ (half + j) ^ half, bits)]
+        target[1] = held[reverse_bits(c ^ j ^ half, bits)]
 
 
 def long_kernel(n, index_ref, near_ref, gated_ref, filt_ref, table_ref, inverse_ref, *refs):
@@ -281,18 +281,10 @@
     def spread(parts):
         return [parts[0]] + [across_seq(parts[r], r) for r in range(1, n)]
 
-    def share_seq(part):
-        held, step = {0: part}, n // 2
-        while step:
-            for r in list(held):
-                held[r | step] = across_seq(held[r], step)
-            step //= 2
-        return [held[r] for r in range(n)]
-
     def lend(parts):
         return [parts[0]] + [across_ch(parts[j], j) for j in range(1, half)]
 
-    low_rows = 3 * depth // 8
+    low_rows = depth // 8
     lower, upper = call(
         functools.partial(cut_kernel, depth - low_rows),
         [shape((low_rows, size), BF16), shape((depth - low_rows, size), BF16)],
@@ -303,8 +295,8 @@
         place=pl.ANY,
     )
     moved = across_ch(lower, half)
-    upper = move(upper, lambda i, j: (j, i))
-    lower = move(moved, lambda i, j: (j ^ half, i))
+    upper = move(upper, lambda i, j: (j, i ^ half))
+    lower = move(moved, lambda i, j: (j ^ half, i ^ half))
     weight, weight_t, *blocks = call(
         functools.partial(arrange_kernel, n),
         [shape(projection.shape, BF16), shape(projection.shape[::-1], BF16)]
@@ -365,7 +357,8 @@
         8 * spectrum,
     )
     pairs = lend([kept, *lent])
-    far_back = share_seq(jnp.stack([pair[0] for pair in pairs]))
+    far = jnp.stack([pair[0] for pair in pairs])
+    far_back = spread([far] * n)
     near = jnp.stack([pair[1] for pair in pairs])
 
     near_back = call(
@@ -401,7 +394,7 @@
             (near_total, moved),
             depth // PIECES * size,
         )
-        homes.append(move(total, lambda i, j: (reverse_bits(j, bits), i)))
+        homes.append(move(total, lambda i, j: (reverse_bits(j ^ half, bits), i)))
     input_grad = jnp.concatenate(homes) if PIECES > 1 else homes[0]
     (conv_out,) = call(
         functools.partial(place_kernel, n),

time: 88.7 us -> 97.7 us (1.10)
  starting transfers between devices: 40.3 us -> 51.3 us
  waiting for transfers between devices: 33.9 us -> 32 us
    ppermute x27, starting transfers between devices: 40.3 us -> 51.3 us  [move(): return lax.ppermute(array, ('seq', 'ch'), pairs)]
    ppermute x27, waiting for transfers between devices: 33.9 us -> 32 us  [move(): return lax.ppermute(array, ('seq', 'ch'), pairs)]
  transfers between devices with their start and end apart: 27 -> 27, of which waited for: 13 -> 9; matrix products, arithmetic and copies ran while one was open for 0% -> 0% of each run, Pallas kernels for 8% -> 7%
where the time goes in v4:
time: 97.7 us; the launch traced here: 97.5 us
  starting transfers between devices  51.3 us (53%)
  waiting for transfers between devices  32 us (33%)
  Pallas kernels  8.93 us (9%)
  local copies, waits for them, and re-layouts  3.71 us (4%)
    ppermute x27, starting transfers between devices, move(): return lax.ppermute(array, ('seq', 'ch'), pairs)  51.3 us
    ppermute x27, waiting for transfers between devices, move(): return lax.ppermute(array, ('seq', 'ch'), pairs)  32 us
    pallas_call x13, Pallas kernels, call(): pl.pallas_call(kernel, out_shape=tuple(outs), in_specs=specs, out_specs=t...  8.93 us
    unnamed x11, local copies, waits for them, and re-layouts  3.7 us
  transfers between devices with their start and end apart: 27, of which 9 were waited for; matrix products, arithmetic and copies ran while one was open for 0% of the time, Pallas kernels for 7%

profile of v4, /device:TPU:1, one launch (start us, length us, event | category | flops | bytes accessed | tf_op | source)
XLA Modules:
  0.0 97.5 jit_solution(17070736803875759512)
XLA Ops:
  2.3 1.2 %copy-done = bf16[1024,512]{1,0:T(8,128)(2,1)S(1)} copy-done((bf16[1024,512]{1,0:T(8,128)(2,1)S(1)}, bf16[1024,512]{1,0:T(8,128)(2,1)}, u32[]{:S(2)}) %copy-start) | copy-done | bytes 1048600
  3.5 1.0 shard_map.68
  5.8 3.6 %collective-permute-start.1 = (bf16[896,128]{1,0:T(8,128)(2,1)S(1)}, bf16[896,128]{1,0:T(8,128)(2,1)S(1)}, u32[]{:S(2)}, u32[]{:S(2)}) collective-permute-start(bf16[896,128]{1,0:T(8,128)(2,1)S(1)} %get-tuple-element.47), channel_id=1, source_target_pairs={{0,2},{1,6},{2,10},{3,14},{4,3},{5,7},{6,11},{7,15},{8,0},{9,4},{1... | collective-permute-start | bytes 688136 | tf_op jit(solution)/shard_map/ppermute | solution.py:273
  9.4 6.6 %collective-permute-done.1.refs_2_ = bf16[896,128]{1,0:T(8,128)(2,1)S(1)} collective-permute-done((bf16[896,128]{1,0:T(8,128)(2,1)S(1)}, bf16[896,128]{1,0:T(8,128)(2,1)S(1)}, u32[]{:S(2)}, u32[]{:S(2)}) %collective-permute-start.1) | collective-permute-done | bytes 229408 | tf_op jit(solution)/shard_map/ppermute | solution.py:273
  16.8 4.4 %collective-permute-start.21 = (bf16[1024,512]{1,0:T(8,128)(2,1)S(1)}, bf16[1024,512]{1,0:T(8,128)(2,1)S(1)}, u32[]{:S(2)}, u32[]{:S(2)}) collective-permute-start(bf16[1024,512]{1,0:T(8,128)(2,1)S(1)} %get-tuple-element.77.refs_0_), channel_id=1, source_target_pairs={{0,1},{1,0},{2,3},{3,2},{4,5},{5,4},{6,7},{7,6},{8,9},{9,8},{10,11... | collective-permute-start | bytes 3145736 | tf_op jit(solution)/shard_map/ppermute | solution.py:273
  21.2 1.7 %collective-permute-start.2 = (bf16[128,128]{1,0:T(8,128)(2,1)S(1)}, bf16[128,128]{1,0:T(8,128)(2,1)S(1)}, u32[]{:S(2)}, u32[]{:S(2)}) collective-permute-start(bf16[128,128]{1,0:T(8,128)(2,1)S(1)} %get-tuple-element.48), channel_id=1, source_target_pairs={{0,2},{1,3},{2,0},{3,1},{4,6},{5,7},{6,4},{7,5},{8,10},{9,11},{10,... | collective-permute-start | bytes 98312 | tf_op jit(solution)/shard_map/ppermute | solution.py:273
  22.9 1.8 %collective-permute-done.2 = bf16[128,128]{1,0:T(8,128)(2,1)S(1)} collective-permute-done((bf16[128,128]{1,0:T(8,128)(2,1)S(1)}, bf16[128,128]{1,0:T(8,128)(2,1)S(1)}, u32[]{:S(2)}, u32[]{:S(2)}) %collective-permute-start.2) | collective-permute-done | bytes 32800 | tf_op jit(solution)/shard_map/ppermute | solution.py:273
  24.7 5.5 %collective-permute-start.3 = (bf16[128,128]{1,0:T(8,128)(2,1)S(1)}, bf16[128,128]{1,0:T(8,128)(2,1)S(1)}, u32[]{:S(2)}, u32[]{:S(2)}) collective-permute-start(bf16[128,128]{1,0:T(8,128)(2,1)S(1)} %collective-permute-done.2), channel_id=1, source_target_pairs={{0,10},{1,14},{2,2},{3,6},{4,11},{5,15},{6,3},{7,7},{8,8},{9,12},{... | collective-permute-start | bytes 98312 | tf_op jit(solution)/shard_map/ppermute | solution.py:273
  30.2 2.4 %collective-permute-done.3.refs_3_ = bf16[128,128]{1,0:T(8,128)(2,1)S(1)} collective-permute-done((bf16[128,128]{1,0:T(8,128)(2,1)S(1)}, bf16[128,128]{1,0:T(8,128)(2,1)S(1)}, u32[]{:S(2)}, u32[]{:S(2)}) %collective-permute-start.3) | collective-permute-done | bytes 32800 | tf_op jit(solution)/shard_map/ppermute | solution.py:273
  33.3 1.0 %collective-permute-start.4 = (bf16[2,128,128]{2,1,0:T(8,128)(2,1)S(1)}, bf16[2,128,128]{2,1,0:T(8,128)(2,1)S(1)}, u32[]{:S(2)}, u32[]{:S(2)}) collective-permute-start(bf16[2,128,128]{2,1,0:T(8,128)(2,1)S(1)} %get-tuple-element.50), channel_id=1, source_target_pairs={{0,4},{1,5},{2,6},{3,7},{4,0},{5,1},{6,2},{7,3},{8,12},{9,13},{10,... | collective-permute-start | bytes 196616 | tf_op jit(solution)/shard_map/ppermute | solution.py:273
  34.3 3.4 %collective-permute-start.5 = (bf16[2,128,128]{2,1,0:T(8,128)(2,1)S(1)}, bf16[2,128,128]{2,1,0:T(8,128)(2,1)S(1)}, u32[]{:S(2)}, u32[]{:S(2)}) collective-permute-start(bf16[2,128,128]{2,1,0:T(8,128)(2,1)S(1)} %get-tuple-element.51), channel_id=1, source_target_pairs={{0,8},{1,9},{2,10},{3,11},{4,12},{5,13},{6,14},{7,15},{8,0},{9,1},... | collective-permute-start | bytes 196616 | tf_op jit(solution)/shard_map/ppermute | solution.py:273
  37.8 1.2 %collective-permute-start.6 = (bf16[2,128,128]{2,1,0:T(8,128)(2,1)S(1)}, bf16[2,128,128]{2,1,0:T(8,128)(2,1)S(1)}, u32[]{:S(2)}, u32[]{:S(2)}) collective-permute-start(bf16[2,128,128]{2,1,0:T(8,128)(2,1)S(1)} %get-tuple-element.52), channel_id=1, source_target_pairs={{0,12},{1,13},{2,14},{3,15},{4,8},{5,9},{6,10},{7,11},{8,4},{9,5},... | collective-permute-start | bytes 196616 | tf_op jit(solution)/shard_map/ppermute | solution.py:273
  40.1 2.0 %collective-permute-start.11 = (bf16[2,128,128]{2,1,0:T(8,128)(2,1)S(1)}, bf16[2,128,128]{2,1,0:T(8,128)(2,1)S(1)}, u32[]{:S(2)}, u32[]{:S(2)}) collective-permute-start(bf16[2,128,128]{2,1,0:T(8,128)(2,1)S(1)} %get-tuple-element.57), channel_id=1, source_target_pairs={{0,8},{1,9},{2,10},{3,11},{4,12},{5,13},{6,14},{7,15},{8,0},{9,1},... | collective-permute-start | bytes 196616 | tf_op jit(solution)/shard_map/ppermute | solution.py:273
  42.1 1.2 %collective-permute-start.12 = (bf16[2,128,128]{2,1,0:T(8,128)(2,1)S(1)}, bf16[2,128,128]{2,1,0:T(8,128)(2,1)S(1)}, u32[]{:S(2)}, u32[]{:S(2)}) collective-permute-start(bf16[2,128,128]{2,1,0:T(8,128)(2,1)S(1)} %get-tuple-element.58), channel_id=1, source_target_pairs={{0,12},{1,13},{2,14},{3,15},{4,8},{5,9},{6,10},{7,11},{8,4},{9,5},... | collective-permute-start | bytes 196616 | tf_op jit(solution)/shard_map/ppermute | solution.py:273
  43.3 1.1 %collective-permute-done.10.refs_1_ = bf16[2,128,128]{2,1,0:T(8,128)(2,1)S(1)} collective-permute-done((bf16[2,128,128]{2,1,0:T(8,128)(2,1)S(1)}, bf16[2,128,128]{2,1,0:T(8,128)(2,1)S(1)}, u32[]{:S(2)}, u32[]{:S(2)}) %collective-permute-start.10) | collective-permute-done | bytes 65568 | tf_op jit(solution)/shard_map/ppermute | solution.py:273
  44.3 1.3 %collective-permute-start.15 = (bf16[2,128,128]{2,1,0:T(8,128)(2,1)S(1)}, bf16[2,128,128]{2,1,0:T(8,128)(2,1)S(1)}, u32[]{:S(2)}, u32[]{:S(2)}) collective-permute-start(bf16[2,128,128]{2,1,0:T(8,128)(2,1)S(1)} %get-tuple-element.63), channel_id=1, source_target_pairs={{0,8},{1,9},{2,10},{3,11},{4,12},{5,13},{6,14},{7,15},{8,0},{9,1},... | collective-permute-start | bytes 196616 | tf_op jit(solution)/shard_map/ppermute | solution.py:273
  45.7 3.3 %collective-permute-start.16 = (bf16[2,128,128]{2,1,0:T(8,128)(2,1)S(1)}, bf16[2,128,128]{2,1,0:T(8,128)(2,1)S(1)}, u32[]{:S(2)}, u32[]{:S(2)}) collective-permute-start(bf16[2,128,128]{2,1,0:T(8,128)(2,1)S(1)} %get-tuple-element.64), channel_id=1, source_target_pairs={{0,12},{1,13},{2,14},{3,15},{4,8},{5,9},{6,10},{7,11},{8,4},{9,5},... | collective-permute-start | bytes 196616 | tf_op jit(solution)/shard_map/ppermute | solution.py:273
  49.0 4.8 %collective-permute-start.7 = (bf16[128,128]{1,0:T(8,128)(2,1)S(1)}, bf16[128,128]{1,0:T(8,128)(2,1)S(1)}, u32[]{:S(2)}, u32[]{:S(2)}) collective-permute-start(bf16[128,128]{1,0:T(8,128)(2,1)S(1)} %get-tuple-element.54), channel_id=1, source_target_pairs={{0,1},{1,0},{2,3},{3,2},{4,5},{5,4},{6,7},{7,6},{8,9},{9,8},{10,11... | collective-permute-start | bytes 98312 | tf_op jit(solution)/shard_map/ppermute | solution.py:273
  54.0 1.2 %shard_map.74 = (bf16[4,128,128]{2,1,0:T(8,128)(2,1)S(1)}, f32[512,256]{1,0:T(8,128)S(1)}, f32[128,256]{1,0:T(8,128)S(1)}) custom-call(s32[2]{0:T(128)S(1)} %pad_add_fusion.index_ref, bf16[2,128,128]{2,1,0:T(8,128)(2,1)S(1)} %get-tuple-element.61.refs_0_, bf16[2,128,128]{2,1,0:T(8,128)(2,1)S(1)} %collective-permute-done.14.refs_1_, ...), custom_call_target="tpu_custom_call" | custom-call | flops 402653184 | bytes 1572864 | tf_op jit(solution)/shard_map/pallas_call | solution.py:247
  55.3 1.2 %shard_map.75 = (bf16[2,128,128]{2,1,0:T(8,128)(2,1)S(1)}, bf16[4,128,128]{2,1,0:T(8,128)(2,1)S(1)}, bf16[2,128,128]{2,1,0:T(8,128)(2,1)S(1)}) custom-call(s32[2]{0:T(128)S(1)} %pad_add_fusion.index_ref, bf16[128,128]{1,0:T(8,128)(2,1)S(1)} %get-tuple-element.53.refs_0_, bf16[128,128]{1,0:T(8,128)(2,1)S(1)} %collective-permute-done.7.refs_1_, ...), custom_call_target="tpu_custom_call" | custom-call | flops 536870912 | bytes 917504 | tf_op jit(solution)/shard_map/pallas_call | solution.py:247
  56.5 4.8 %collective-permute-start.17 = (bf16[2,128,128]{2,1,0:T(8,128)(2,1)S(1)}, bf16[2,128,128]{2,1,0:T(8,128)(2,1)S(1)}, u32[]{:S(2)}, u32[]{:S(2)}) collective-permute-start(bf16[2,128,128]{2,1,0:T(8,128)(2,1)S(1)} %get-tuple-element.70), channel_id=1, source_target_pairs={{0,1},{1,0},{2,3},{3,2},{4,5},{5,4},{6,7},{7,6},{8,9},{9,8},{10,11... | collective-permute-start | bytes 196616 | tf_op jit(solution)/shard_map/ppermute | solution.py:273
  61.3 0.9 collective-permute-done.17
  62.3 1.0 %collective-permute-start.23 = (bf16[2,128,128]{2,1,0:T(8,128)(2,1)S(1)}, bf16[2,128,128]{2,1,0:T(8,128)(2,1)S(1)}, u32[]{:S(2)}, u32[]{:S(2)}) collective-permute-start(bf16[2,128,128]{2,1,0:T(8,128)(2,1)S(1)} %pad_maximum_fusion.4.refs_2_), channel_id=1, source_target_pairs={{0,8},{1,9},{2,10},{3,11},{4,12},{5,13},{6,14},{7,15},{8,0},{9,1},... | collective-permute-start | bytes 196616 | tf_op jit(solution)/shard_map/ppermute | solution.py:273
  63.3 2.5 %collective-permute-start.24 = (bf16[2,128,128]{2,1,0:T(8,128)(2,1)S(1)}, bf16[2,128,128]{2,1,0:T(8,128)(2,1)S(1)}, u32[]{:S(2)}, u32[]{:S(2)}) collective-permute-start(bf16[2,128,128]{2,1,0:T(8,128)(2,1)S(1)} %pad_maximum_fusion.4.refs_2_), channel_id=1, source_target_pairs={{0,12},{1,13},{2,14},{3,15},{4,8},{5,9},{6,10},{7,11},{8,4},{9,5},... | collective-permute-start | bytes 196616 | tf_op jit(solution)/shard_map/ppermute | solution.py:273
  66.5 2.2 %collective-permute-done.24.refs_5_ = bf16[2,128,128]{2,1,0:T(8,128)(2,1)S(1)} collective-permute-done((bf16[2,128,128]{2,1,0:T(8,128)(2,1)S(1)}, bf16[2,128,128]{2,1,0:T(8,128)(2,1)S(1)}, u32[]{:S(2)}, u32[]{:S(2)}) %collective-permute-start.24) | collective-permute-done | bytes 65568 | tf_op jit(solution)/shard_map/ppermute | solution.py:273
  69.8 1.1 %shard_map.76 = (bf16[3,128,128]{2,1,0:T(8,128)(2,1)S(1)}, bf16[3,128,128]{2,1,0:T(8,128)(2,1)S(1)}, bf16[3,128,128]{2,1,0:T(8,128)(2,1)S(1)}, bf16[3,128,128]{2,1,0:T(8,128)(2,1)S(1)}) custom-call(s32[2]{0:T(128)S(1)} %pad_add_fusion.index_ref, bf16[2,128,128]{2,1,0:T(8,128)(2,1)S(1)} %pad_maximum_fusion.3.near_ref, ...), custom_call_target="tpu_custom_call" | custom-call | flops 268435456 | bytes 1376256 | tf_op jit(solution)/shard_map/pallas_call | solution.py:247
  70.9 1.8 %collective-permute-start.18 = (bf16[3,128,128]{2,1,0:T(8,128)(2,1)S(1)}, bf16[3,128,128]{2,1,0:T(8,128)(2,1)S(1)}, u32[]{:S(2)}, u32[]{:S(2)}) collective-permute-start(bf16[3,128,128]{2,1,0:T(8,128)(2,1)S(1)} %get-tuple-element.74), channel_id=1, source_target_pairs={{0,4},{1,5},{2,6},{3,7},{4,0},{5,1},{6,2},{7,3},{8,12},{9,13},{10,... | collective-permute-start | bytes 294920 | tf_op jit(solution)/shard_map/ppermute | solution.py:273
  73.1 1.8 %collective-permute-start.20 = (bf16[3,128,128]{2,1,0:T(8,128)(2,1)S(1)}, bf16[3,128,128]{2,1,0:T(8,128)(2,1)S(1)}, u32[]{:S(2)}, u32[]{:S(2)}) collective-permute-start(bf16[3,128,128]{2,1,0:T(8,128)(2,1)S(1)} %get-tuple-element.76), channel_id=1, source_target_pairs={{0,12},{1,13},{2,14},{3,15},{4,8},{5,9},{6,10},{7,11},{8,4},{9,5},... | collective-permute-start | bytes 294920 | tf_op jit(solution)/shard_map/ppermute | solution.py:273
  74.9 7.1 %collective-permute-done.19.refs_2_.refs_4_ = bf16[3,128,128]{2,1,0:T(8,128)(2,1)S(1)} collective-permute-done((bf16[3,128,128]{2,1,0:T(8,128)(2,1)S(1)}, bf16[3,128,128]{2,1,0:T(8,128)(2,1)S(1)}, u32[]{:S(2)}, u32[]{:S(2)}) %collective-permute-start.19) | collective-permute-done | bytes 98336 | tf_op jit(solution)/shard_map/ppermute | solution.py:273
  82.7 3.5 %collective-permute-start.26 = (bf16[1024,128]{1,0:T(8,128)(2,1)S(1)}, bf16[1024,128]{1,0:T(8,128)(2,1)S(1)}, u32[]{:S(2)}, u32[]{:S(2)}) collective-permute-start(bf16[1024,128]{1,0:T(8,128)(2,1)S(1)} %shard_map.80), channel_id=1, source_target_pairs={{0,4},{1,12},{2,0},{3,8},{4,5},{5,13},{6,1},{7,9},{8,6},{9,14},{10... | collective-permute-start | bytes 786440 | tf_op jit(solution)/shard_map/ppermute | solution.py:273
  86.2 1.2 %shard_map.77 = bf16[512,128]{1,0:T(8,128)(2,1)} custom-call(s32[2]{0:T(128)S(1)} %pad_add_fusion.index_ref, bf16[3,128,128]{2,1,0:T(8,128)(2,1)S(1)} %get-tuple-element.73.refs_0_.refs_2_, bf16[3,128,128]{2,1,0:T(8,128)(2,1)S(1)} %collective-permute-done.18.refs_1_.refs_3_, bf16[3,128,128]{2,1,0:T(8,128)(2,1)S(1)} %collective-permute-done.19.refs_2_.refs_4_, ...), custom_call_target="tpu_custom_call" | custom-call | bytes 524288 | tf_op jit(solution)/shard_map/pallas_call | solution.py:247
  87.4 9.4 %collective-permute-done.26 = bf16[1024,128]{1,0:T(8,128)(2,1)S(1)} collective-permute-done((bf16[1024,128]{1,0:T(8,128)(2,1)S(1)}, bf16[1024,128]{1,0:T(8,128)(2,1)S(1)}, u32[]{:S(2)}, u32[]{:S(2)}) %collective-permute-start.26) | collective-permute-done | bytes 262176 | tf_op jit(solution)/shard_map/ppermute | solution.py:273
  (57 shorter events, 9.5 us)
Async XLA Ops:
  1.3 0.9 copy-start.2
  1.3 1.0 copy-start.3
  2.3 1.2 %copy-start = (bf16[1024,512]{1,0:T(8,128)(2,1)S(1)}, bf16[1024,512]{1,0:T(8,128)(2,1)}, u32[]{:S(2)}) copy-start(bf16[1024,512]{1,0:T(8,128)(2,1)} %given_ref.2) | copy-start | bytes 3145732
  4.5 1.0 copy-start.1
  4.5 28.0 %collective-permute-start = (bf16[512,1024]{1,0:T(8,128)(2,1)S(1)}, bf16[512,1024]{1,0:T(8,128)(2,1)S(1)}, u32[]{:S(2)}, u32[]{:S(2)}) collective-permute-start(bf16[512,1024]{1,0:T(8,128)(2,1)S(1)} %get-tuple-element.46.refs_0_), channel_id=1, source_target_pairs={{0,1},{1,0},{2,3},{3,2},{4,5},{5,4},{6,7},{7,6},{8,9},{9,8},{10,11... | collective-permute-start | bytes 3145736 | tf_op jit(solution)/shard_map/ppermute | solution.py:273
  5.8 10.2 %collective-permute-start.1 = (bf16[896,128]{1,0:T(8,128)(2,1)S(1)}, bf16[896,128]{1,0:T(8,128)(2,1)S(1)}, u32[]{:S(2)}, u32[]{:S(2)}) collective-permute-start(bf16[896,128]{1,0:T(8,128)(2,1)S(1)} %get-tuple-element.47), channel_id=1, source_target_pairs={{0,2},{1,6},{2,10},{3,14},{4,3},{5,7},{6,11},{7,15},{8,0},{9,4},{1... | collective-permute-start | bytes 688136 | tf_op jit(solution)/shard_map/ppermute | solution.py:273
  16.0 23.0 %collective-permute-start.8 = (bf16[896,128]{1,0:T(8,128)(2,1)S(1)}, bf16[896,128]{1,0:T(8,128)(2,1)S(1)}, u32[]{:S(2)}, u32[]{:S(2)}) collective-permute-start(bf16[896,128]{1,0:T(8,128)(2,1)S(1)} %collective-permute-done.1.refs_2_), channel_id=1, source_target_pairs={{0,2},{1,3},{2,0},{3,1},{4,6},{5,7},{6,4},{7,5},{8,10},{9,11},{10,... | collective-permute-start | bytes 688136 | tf_op jit(solution)/shard_map/ppermute | solution.py:273
  16.8 49.1 %collective-permute-start.21 = (bf16[1024,512]{1,0:T(8,128)(2,1)S(1)}, bf16[1024,512]{1,0:T(8,128)(2,1)S(1)}, u32[]{:S(2)}, u32[]{:S(2)}) collective-permute-start(bf16[1024,512]{1,0:T(8,128)(2,1)S(1)} %get-tuple-element.77.refs_0_), channel_id=1, source_target_pairs={{0,1},{1,0},{2,3},{3,2},{4,5},{5,4},{6,7},{7,6},{8,9},{9,8},{10,11... | collective-permute-start | bytes 3145736 | tf_op jit(solution)/shard_map/ppermute | solution.py:273
  21.2 3.5 %collective-permute-start.2 = (bf16[128,128]{1,0:T(8,128)(2,1)S(1)}, bf16[128,128]{1,0:T(8,128)(2,1)S(1)}, u32[]{:S(2)}, u32[]{:S(2)}) collective-permute-start(bf16[128,128]{1,0:T(8,128)(2,1)S(1)} %get-tuple-element.48), channel_id=1, source_target_pairs={{0,2},{1,3},{2,0},{3,1},{4,6},{5,7},{6,4},{7,5},{8,10},{9,11},{10,... | collective-permute-start | bytes 98312 | tf_op jit(solution)/shard_map/ppermute | solution.py:273
  24.7 7.9 %collective-permute-start.3 = (bf16[128,128]{1,0:T(8,128)(2,1)S(1)}, bf16[128,128]{1,0:T(8,128)(2,1)S(1)}, u32[]{:S(2)}, u32[]{:S(2)}) collective-permute-start(bf16[128,128]{1,0:T(8,128)(2,1)S(1)} %collective-permute-done.2), channel_id=1, source_target_pairs={{0,10},{1,14},{2,2},{3,6},{4,11},{5,15},{6,3},{7,7},{8,8},{9,12},{... | collective-permute-start | bytes 98312 | tf_op jit(solution)/shard_map/ppermute | solution.py:273
  33.3 6.8 %collective-permute-start.4 = (bf16[2,128,128]{2,1,0:T(8,128)(2,1)S(1)}, bf16[2,128,128]{2,1,0:T(8,128)(2,1)S(1)}, u32[]{:S(2)}, u32[]{:S(2)}) collective-permute-start(bf16[2,128,128]{2,1,0:T(8,128)(2,1)S(1)} %get-tuple-element.50), channel_id=1, source_target_pairs={{0,4},{1,5},{2,6},{3,7},{4,0},{5,1},{6,2},{7,3},{8,12},{9,13},{10,... | collective-permute-start | bytes 196616 | tf_op jit(solution)/shard_map/ppermute | solution.py:273
  34.3 3.5 %collective-permute-start.9 = (bf16[128,128]{1,0:T(8,128)(2,1)S(1)}, bf16[128,128]{1,0:T(8,128)(2,1)S(1)}, u32[]{:S(2)}, u32[]{:S(2)}) collective-permute-start(bf16[128,128]{1,0:T(8,128)(2,1)S(1)} %collective-permute-done.3.refs_3_), channel_id=1, source_target_pairs={{0,2},{1,3},{2,0},{3,1},{4,6},{5,7},{6,4},{7,5},{8,10},{9,11},{10,... | collective-permute-start | bytes 98312 | tf_op jit(solution)/shard_map/ppermute | solution.py:273
  34.3 7.8 %collective-permute-start.5 = (bf16[2,128,128]{2,1,0:T(8,128)(2,1)S(1)}, bf16[2,128,128]{2,1,0:T(8,128)(2,1)S(1)}, u32[]{:S(2)}, u32[]{:S(2)}) collective-permute-start(bf16[2,128,128]{2,1,0:T(8,128)(2,1)S(1)} %get-tuple-element.51), channel_id=1, source_target_pairs={{0,8},{1,9},{2,10},{3,11},{4,12},{5,13},{6,14},{7,15},{8,0},{9,1},... | collective-permute-start | bytes 196616 | tf_op jit(solution)/shard_map/ppermute | solution.py:273
  37.8 5.5 %collective-permute-start.6 = (bf16[2,128,128]{2,1,0:T(8,128)(2,1)S(1)}, bf16[2,128,128]{2,1,0:T(8,128)(2,1)S(1)}, u32[]{:S(2)}, u32[]{:S(2)}) collective-permute-start(bf16[2,128,128]{2,1,0:T(8,128)(2,1)S(1)} %get-tuple-element.52), channel_id=1, source_target_pairs={{0,12},{1,13},{2,14},{3,15},{4,8},{5,9},{6,10},{7,11},{8,4},{9,5},... | collective-permute-start | bytes 196616 | tf_op jit(solution)/shard_map/ppermute | solution.py:273
  39.6 4.7 %collective-permute-start.10 = (bf16[2,128,128]{2,1,0:T(8,128)(2,1)S(1)}, bf16[2,128,128]{2,1,0:T(8,128)(2,1)S(1)}, u32[]{:S(2)}, u32[]{:S(2)}) collective-permute-start(bf16[2,128,128]{2,1,0:T(8,128)(2,1)S(1)} %get-tuple-element.56), channel_id=1, source_target_pairs={{0,4},{1,5},{2,6},{3,7},{4,0},{5,1},{6,2},{7,3},{8,12},{9,13},{10,... | collective-permute-start | bytes 196616 | tf_op jit(solution)/shard_map/ppermute | solution.py:273
  40.1 5.5 %collective-permute-start.11 = (bf16[2,128,128]{2,1,0:T(8,128)(2,1)S(1)}, bf16[2,128,128]{2,1,0:T(8,128)(2,1)S(1)}, u32[]{:S(2)}, u32[]{:S(2)}) collective-permute-start(bf16[2,128,128]{2,1,0:T(8,128)(2,1)S(1)} %get-tuple-element.57), channel_id=1, source_target_pairs={{0,8},{1,9},{2,10},{3,11},{4,12},{5,13},{6,14},{7,15},{8,0},{9,1},... | collective-permute-start | bytes 196616 | tf_op jit(solution)/shard_map/ppermute | solution.py:273
  42.1 6.9 %collective-permute-start.12 = (bf16[2,128,128]{2,1,0:T(8,128)(2,1)S(1)}, bf16[2,128,128]{2,1,0:T(8,128)(2,1)S(1)}, u32[]{:S(2)}, u32[]{:S(2)}) collective-permute-start(bf16[2,128,128]{2,1,0:T(8,128)(2,1)S(1)} %get-tuple-element.58), channel_id=1, source_target_pairs={{0,12},{1,13},{2,14},{3,15},{4,8},{5,9},{6,10},{7,11},{8,4},{9,5},... | collective-permute-start | bytes 196616 | tf_op jit(solution)/shard_map/ppermute | solution.py:273
  43.3 10.7 %collective-permute-start.14 = (bf16[2,128,128]{2,1,0:T(8,128)(2,1)S(1)}, bf16[2,128,128]{2,1,0:T(8,128)(2,1)S(1)}, u32[]{:S(2)}, u32[]{:S(2)}) collective-permute-start(bf16[2,128,128]{2,1,0:T(8,128)(2,1)S(1)} %get-tuple-element.62), channel_id=1, source_target_pairs={{0,4},{1,5},{2,6},{3,7},{4,0},{5,1},{6,2},{7,3},{8,12},{9,13},{10,... | collective-permute-start | bytes 196616 | tf_op jit(solution)/shard_map/ppermute | solution.py:273
  44.3 9.7 %collective-permute-start.15 = (bf16[2,128,128]{2,1,0:T(8,128)(2,1)S(1)}, bf16[2,128,128]{2,1,0:T(8,128)(2,1)S(1)}, u32[]{:S(2)}, u32[]{:S(2)}) collective-permute-start(bf16[2,128,128]{2,1,0:T(8,128)(2,1)S(1)} %get-tuple-element.63), channel_id=1, source_target_pairs={{0,8},{1,9},{2,10},{3,11},{4,12},{5,13},{6,14},{7,15},{8,0},{9,1},... | collective-permute-start | bytes 196616 | tf_op jit(solution)/shard_map/ppermute | solution.py:273
  45.7 8.4 %collective-permute-start.16 = (bf16[2,128,128]{2,1,0:T(8,128)(2,1)S(1)}, bf16[2,128,128]{2,1,0:T(8,128)(2,1)S(1)}, u32[]{:S(2)}, u32[]{:S(2)}) collective-permute-start(bf16[2,128,128]{2,1,0:T(8,128)(2,1)S(1)} %get-tuple-element.64), channel_id=1, source_target_pairs={{0,12},{1,13},{2,14},{3,15},{4,8},{5,9},{6,10},{7,11},{8,4},{9,5},... | collective-permute-start | bytes 196616 | tf_op jit(solution)/shard_map/ppermute | solution.py:273
  49.0 5.0 %copy-start.4 = (f32[512,128]{1,0:T(8,128)S(1)}, f32[512,128]{1,0:T(8,128)}, u32[]{:S(2)}) copy-start(f32[512,128]{1,0:T(8,128)} %refs_4_.1) | copy-start | bytes 786436
  49.0 6.2 %collective-permute-start.7 = (bf16[128,128]{1,0:T(8,128)(2,1)S(1)}, bf16[128,128]{1,0:T(8,128)(2,1)S(1)}, u32[]{:S(2)}, u32[]{:S(2)}) collective-permute-start(bf16[128,128]{1,0:T(8,128)(2,1)S(1)} %get-tuple-element.54), channel_id=1, source_target_pairs={{0,1},{1,0},{2,3},{3,2},{4,5},{5,4},{6,7},{7,6},{8,9},{9,8},{10,11... | collective-permute-start | bytes 98312 | tf_op jit(solution)/shard_map/ppermute | solution.py:273
  53.9 1.3 %collective-permute-start.13 = (bf16[128,128]{1,0:T(8,128)(2,1)S(1)}, bf16[128,128]{1,0:T(8,128)(2,1)S(1)}, u32[]{:S(2)}, u32[]{:S(2)}) collective-permute-start(bf16[128,128]{1,0:T(8,128)(2,1)S(1)} %get-tuple-element.60), channel_id=1, source_target_pairs={{0,1},{1,0},{2,3},{3,2},{4,5},{5,4},{6,7},{7,6},{8,9},{9,8},{10,11... | collective-permute-start | bytes 98312 | tf_op jit(solution)/shard_map/ppermute | solution.py:273
  56.5 5.7 %collective-permute-start.17 = (bf16[2,128,128]{2,1,0:T(8,128)(2,1)S(1)}, bf16[2,128,128]{2,1,0:T(8,128)(2,1)S(1)}, u32[]{:S(2)}, u32[]{:S(2)}) collective-permute-start(bf16[2,128,128]{2,1,0:T(8,128)(2,1)S(1)} %get-tuple-element.70), channel_id=1, source_target_pairs={{0,1},{1,0},{2,3},{3,2},{4,5},{5,4},{6,7},{7,6},{8,9},{9,8},{10,11... | collective-permute-start | bytes 196616 | tf_op jit(solution)/shard_map/ppermute | solution.py:273
  62.2 3.6 %collective-permute-start.22 = (bf16[2,128,128]{2,1,0:T(8,128)(2,1)S(1)}, bf16[2,128,128]{2,1,0:T(8,128)(2,1)S(1)}, u32[]{:S(2)}, u32[]{:S(2)}) collective-permute-start(bf16[2,128,128]{2,1,0:T(8,128)(2,1)S(1)} %pad_maximum_fusion.4.refs_2_), channel_id=1, source_target_pairs={{0,4},{1,5},{2,6},{3,7},{4,0},{5,1},{6,2},{7,3},{8,12},{9,13},{10,... | collective-permute-start | bytes 196616 | tf_op jit(solution)/shard_map/ppermute | solution.py:273
  62.3 4.2 %collective-permute-start.23 = (bf16[2,128,128]{2,1,0:T(8,128)(2,1)S(1)}, bf16[2,128,128]{2,1,0:T(8,128)(2,1)S(1)}, u32[]{:S(2)}, u32[]{:S(2)}) collective-permute-start(bf16[2,128,128]{2,1,0:T(8,128)(2,1)S(1)} %pad_maximum_fusion.4.refs_2_), channel_id=1, source_target_pairs={{0,8},{1,9},{2,10},{3,11},{4,12},{5,13},{6,14},{7,15},{8,0},{9,1},... | collective-permute-start | bytes 196616 | tf_op jit(solution)/shard_map/ppermute | solution.py:273
  63.3 5.3 %collective-permute-start.24 = (bf16[2,128,128]{2,1,0:T(8,128)(2,1)S(1)}, bf16[2,128,128]{2,1,0:T(8,128)(2,1)S(1)}, u32[]{:S(2)}, u32[]{:S(2)}) collective-permute-start(bf16[2,128,128]{2,1,0:T(8,128)(2,1)S(1)} %pad_maximum_fusion.4.refs_2_), channel_id=1, source_target_pairs={{0,12},{1,13},{2,14},{3,15},{4,8},{5,9},{6,10},{7,11},{8,4},{9,5},... | collective-permute-start | bytes 196616 | tf_op jit(solution)/shard_map/ppermute | solution.py:273
  69.4 13.3 %collective-permute-start.25 = (bf16[1024,128]{1,0:T(8,128)(2,1)S(1)}, bf16[1024,128]{1,0:T(8,128)(2,1)S(1)}, u32[]{:S(2)}, u32[]{:S(2)}) collective-permute-start(bf16[1024,128]{1,0:T(8,128)(2,1)S(1)} %shard_map.79), channel_id=1, source_target_pairs={{0,2},{1,3},{2,0},{3,1},{4,6},{5,7},{6,4},{7,5},{8,10},{9,11},{10,... | collective-permute-start | bytes 786440 | tf_op jit(solution)/shard_map/ppermute | solution.py:273
  70.9 4.0 %collective-permute-start.18 = (bf16[3,128,128]{2,1,0:T(8,128)(2,1)S(1)}, bf16[3,128,128]{2,1,0:T(8,128)(2,1)S(1)}, u32[]{:S(2)}, u32[]{:S(2)}) collective-permute-start(bf16[3,128,128]{2,1,0:T(8,128)(2,1)S(1)} %get-tuple-element.74), channel_id=1, source_target_pairs={{0,4},{1,5},{2,6},{3,7},{4,0},{5,1},{6,2},{7,3},{8,12},{9,13},{10,... | collective-permute-start | bytes 294920 | tf_op jit(solution)/shard_map/ppermute | solution.py:273
  72.7 9.2 %collective-permute-start.19 = (bf16[3,128,128]{2,1,0:T(8,128)(2,1)S(1)}, bf16[3,128,128]{2,1,0:T(8,128)(2,1)S(1)}, u32[]{:S(2)}, u32[]{:S(2)}) collective-permute-start(bf16[3,128,128]{2,1,0:T(8,128)(2,1)S(1)} %get-tuple-element.75), channel_id=1, source_target_pairs={{0,8},{1,9},{2,10},{3,11},{4,12},{5,13},{6,14},{7,15},{8,0},{9,1},... | collective-permute-start | bytes 294920 | tf_op jit(solution)/shard_map/ppermute | solution.py:273
  73.1 8.9 %collective-permute-start.20 = (bf16[3,128,128]{2,1,0:T(8,128)(2,1)S(1)}, bf16[3,128,128]{2,1,0:T(8,128)(2,1)S(1)}, u32[]{:S(2)}, u32[]{:S(2)}) collective-permute-start(bf16[3,128,128]{2,1,0:T(8,128)(2,1)S(1)} %get-tuple-element.76), channel_id=1, source_target_pairs={{0,12},{1,13},{2,14},{3,15},{4,8},{5,9},{6,10},{7,11},{8,4},{9,5},... | collective-permute-start | bytes 294920 | tf_op jit(solution)/shard_map/ppermute | solution.py:273
  82.7 14.1 %collective-permute-start.26 = (bf16[1024,128]{1,0:T(8,128)(2,1)S(1)}, bf16[1024,128]{1,0:T(8,128)(2,1)S(1)}, u32[]{:S(2)}, u32[]{:S(2)}) collective-permute-start(bf16[1024,128]{1,0:T(8,128)(2,1)S(1)} %shard_map.80), channel_id=1, source_target_pairs={{0,4},{1,12},{2,0},{3,8},{4,5},{5,13},{6,1},{7,9},{8,6},{9,14},{10... | collective-permute-start | bytes 786440 | tf_op jit(solution)/shard_map/ppermute | solution.py:273

commit v5 on v4

--- a/solution.py
+++ b/solution.py
@@ -118,7 +118,7 @@
     table, inverse = table_ref[...], inverse_ref[...]
     tr, ti = tap_ref[:, :size], tap_ref[:, size:]
     wide = values.astype(F32)
-    gate = 1.0 / (1.0 + jnp.exp(-wide))
+    gate = jax.nn.sigmoid(wide)
     grad = grad_in_ref[...].reshape(n * size, size).astype(F32)
     grad_medium = (grad * gate).astype(BF16)
     re, im = to_spectrum(values, table)
@@ -143,8 +143,21 @@
         target[1] = held[reverse_bits(c ^ j ^ half, bits)]
 
 
-def long_kernel(n, index_ref, near_ref, gated_ref, filt_ref, table_ref, inverse_ref, *refs):
-    outs, held = refs[:n], refs[n]
+def turned_side(s):
+    return (s ^ (s >> 1)) & 1
+
+
+def deal_kernel(n, index_ref, *refs):
+    pairs, outs = refs[: n // 2], refs[n // 2 :]
+    s = index_ref[0]
+    for r in range(n):
+        for j in range(n // 2):
+            outs[r][j] = pairs[j][turned_side(s ^ r)]
+
+
+def long_kernel(n, index_ref, *refs):
+    pairs, (gated_ref, filt_ref, table_ref, inverse_ref) = refs[: n // 2], refs[n // 2 : n // 2 + 4]
+    outs, held = refs[n // 2 + 4 : -1], refs[-1]
     s = index_ref[0]
     size = gated_ref.shape[2]
     re, im = to_spectrum(gated_ref[...].reshape(n * size, size), table_ref[...])
@@ -165,7 +178,8 @@
     out = from_spectrum(jnp.concatenate(real), jnp.concatenate(imag), inverse_ref[...])
     held[...] = out.astype(BF16).reshape(n, size, size)
     for r in range(n):
-        outs[r][: n // 2] = near_ref[...]
+        for j in range(n // 2):
+            outs[r][j] = pairs[j][1 - turned_side(s ^ r)]
         outs[r][n // 2] = held[s ^ r]
 
 
@@ -357,16 +371,22 @@
         8 * spectrum,
     )
     pairs = lend([kept, *lent])
-    far = jnp.stack([pair[0] for pair in pairs])
-    far_back = spread([far] * n)
-    near = jnp.stack([pair[1] for pair in pairs])
+    far_back = call(
+        functools.partial(deal_kernel, n),
+        [shape((half, own, size), BF16)] * n,
+        [],
+        index,
+        tuple(pairs),
+        0,
+    )
+    far_back = spread(far_back)
 
     near_back = call(
         functools.partial(long_kernel, n),
         [shape((half + 1, own, size), BF16)] * n,
         [pltpu.VMEM((n, own, size), BF16)],
         index,
-        (near, gated, filt, table, inverse),
+        (*pairs, gated, filt, table, inverse),
         4 * spectrum,
     )
     near_back = spread(near_back)
@@ -394,7 +414,7 @@
             (near_total, moved),
             depth // PIECES * size,
         )
-        homes.append(move(total, lambda i, j: (reverse_bits(j ^ half, bits), i)))
+        homes.append(move(total, lambda i, j: (reverse_bits(j ^ half ^ half * turned_side(i), bits), i)))
     input_grad = jnp.concatenate(homes) if PIECES > 1 else homes[0]
     (conv_out,) = call(
         functools.partial(place_kernel, n),

time: 97.7 us -> 95.1 us (0.973)
  the two profiles are of different devices: /device:TPU:1 before, /device:TPU:0 now
where the time goes in v5:
time: 95.1 us; the launch traced here: 93.7 us
  waiting for transfers between devices  47.1 us (50%)
  starting transfers between devices  32.4 us (34%)
  Pallas kernels  9.48 us (10%)
  local copies, waits for them, and re-layouts  3.15 us (3%)
    ppermute x27, waiting for transfers between devices, move(): return lax.ppermute(array, ('seq', 'ch'), pairs)  47.1 us
    ppermute x27, starting transfers between devices, move(): return lax.ppermute(array, ('seq', 'ch'), pairs)  32.4 us
    pallas_call x14, Pallas kernels, call(): pl.pallas_call(kernel, out_shape=tuple(outs), in_specs=specs, out_specs=t...  9.48 us
    unnamed x11, local copies, waits for them, and re-layouts  3.15 us
  transfers between devices with their start and end apart: 27, of which 14 were waited for; matrix products, arithmetic and copies ran while one was open for 0% of the time, Pallas kernels for 8%

profile of v5, /device:TPU:0, one launch (start us, length us, event | category | flops | bytes accessed | tf_op | source)
XLA Modules:
  0.0 93.7 jit_solution(6845894668220514758)
XLA Ops:
  2.3 1.2 %copy-done = bf16[1024,512]{1,0:T(8,128)(2,1)S(1)} copy-done((bf16[1024,512]{1,0:T(8,128)(2,1)S(1)}, bf16[1024,512]{1,0:T(8,128)(2,1)}, u32[]{:S(2)}) %copy-start) | copy-done | bytes 1048600
  3.5 1.0 %shard_map.68 = (bf16[1024,512]{1,0:T(8,128)(2,1)S(1)}, bf16[512,1024]{1,0:T(8,128)(2,1)S(1)}, bf16[2,128,128]{2,1,0:T(8,128)(2,1)S(1)}, bf16[2,128,128]{2,1,0:T...) custom-call(s32[2]{0:T(128)S(1)} %pad_add_fusion.index_ref, ...), custom_call_target="tpu_custom_call" | custom-call | bytes 3670016 | tf_op jit(solution)/shard_map/pallas_call | solution.py:261
  5.8 3.0 %collective-permute-start.1 = (bf16[896,128]{1,0:T(8,128)(2,1)S(1)}, bf16[896,128]{1,0:T(8,128)(2,1)S(1)}, u32[]{:S(2)}, u32[]{:S(2)}) collective-permute-start(bf16[896,128]{1,0:T(8,128)(2,1)S(1)} %get-tuple-element.51), channel_id=1, source_target_pairs={{0,2},{1,6},{2,10},{3,14},{4,3},{5,7},{6,11},{7,15},{8,0},{9,4},{1... | collective-permute-start | bytes 688136 | tf_op jit(solution)/shard_map/ppermute | solution.py:287
  8.8 12.3 %collective-permute-done.1.refs_2_ = bf16[896,128]{1,0:T(8,128)(2,1)S(1)} collective-permute-done((bf16[896,128]{1,0:T(8,128)(2,1)S(1)}, bf16[896,128]{1,0:T(8,128)(2,1)S(1)}, u32[]{:S(2)}, u32[]{:S(2)}) %collective-permute-start.1) | collective-permute-done | bytes 229408 | tf_op jit(solution)/shard_map/ppermute | solution.py:287
  21.1 2.0 %collective-permute-start.2 = (bf16[128,128]{1,0:T(8,128)(2,1)S(1)}, bf16[128,128]{1,0:T(8,128)(2,1)S(1)}, u32[]{:S(2)}, u32[]{:S(2)}) collective-permute-start(bf16[128,128]{1,0:T(8,128)(2,1)S(1)} %get-tuple-element.52), channel_id=1, source_target_pairs={{0,2},{1,3},{2,0},{3,1},{4,6},{5,7},{6,4},{7,5},{8,10},{9,11},{10,... | collective-permute-start | bytes 98312 | tf_op jit(solution)/shard_map/ppermute | solution.py:287
  23.2 4.3 %collective-permute-done.2 = bf16[128,128]{1,0:T(8,128)(2,1)S(1)} collective-permute-done((bf16[128,128]{1,0:T(8,128)(2,1)S(1)}, bf16[128,128]{1,0:T(8,128)(2,1)S(1)}, u32[]{:S(2)}, u32[]{:S(2)}) %collective-permute-start.2) | collective-permute-done | bytes 32800 | tf_op jit(solution)/shard_map/ppermute | solution.py:287
  27.5 3.0 %collective-permute-start.3 = (bf16[128,128]{1,0:T(8,128)(2,1)S(1)}, bf16[128,128]{1,0:T(8,128)(2,1)S(1)}, u32[]{:S(2)}, u32[]{:S(2)}) collective-permute-start(bf16[128,128]{1,0:T(8,128)(2,1)S(1)} %collective-permute-done.2), channel_id=1, source_target_pairs={{0,10},{1,14},{2,2},{3,6},{4,11},{5,15},{6,3},{7,7},{8,8},{9,12},{... | collective-permute-start | bytes 98312 | tf_op jit(solution)/shard_map/ppermute | solution.py:287
  30.5 4.6 %collective-permute-done.3.refs_3_ = bf16[128,128]{1,0:T(8,128)(2,1)S(1)} collective-permute-done((bf16[128,128]{1,0:T(8,128)(2,1)S(1)}, bf16[128,128]{1,0:T(8,128)(2,1)S(1)}, u32[]{:S(2)}, u32[]{:S(2)}) %collective-permute-start.3) | collective-permute-done | bytes 32800 | tf_op jit(solution)/shard_map/ppermute | solution.py:287
  36.6 1.4 %collective-permute-start.5 = (bf16[2,128,128]{2,1,0:T(8,128)(2,1)S(1)}, bf16[2,128,128]{2,1,0:T(8,128)(2,1)S(1)}, u32[]{:S(2)}, u32[]{:S(2)}) collective-permute-start(bf16[2,128,128]{2,1,0:T(8,128)(2,1)S(1)} %get-tuple-element.55), channel_id=1, source_target_pairs={{0,8},{1,9},{2,10},{3,11},{4,12},{5,13},{6,14},{7,15},{8,0},{9,1},... | collective-permute-start | bytes 196616 | tf_op jit(solution)/shard_map/ppermute | solution.py:287
  38.0 1.9 %collective-permute-done.9.refs_3_ = bf16[128,128]{1,0:T(8,128)(2,1)S(1)} collective-permute-done((bf16[128,128]{1,0:T(8,128)(2,1)S(1)}, bf16[128,128]{1,0:T(8,128)(2,1)S(1)}, u32[]{:S(2)}, u32[]{:S(2)}) %collective-permute-start.9) | collective-permute-done | bytes 32800 | tf_op jit(solution)/shard_map/ppermute | solution.py:287
  39.9 1.1 %collective-permute-start.6 = (bf16[2,128,128]{2,1,0:T(8,128)(2,1)S(1)}, bf16[2,128,128]{2,1,0:T(8,128)(2,1)S(1)}, u32[]{:S(2)}, u32[]{:S(2)}) collective-permute-start(bf16[2,128,128]{2,1,0:T(8,128)(2,1)S(1)} %get-tuple-element.56), channel_id=1, source_target_pairs={{0,12},{1,13},{2,14},{3,15},{4,8},{5,9},{6,10},{7,11},{8,4},{9,5},... | collective-permute-start | bytes 196616 | tf_op jit(solution)/shard_map/ppermute | solution.py:287
  42.6 2.4 %collective-permute-start.11 = (bf16[2,128,128]{2,1,0:T(8,128)(2,1)S(1)}, bf16[2,128,128]{2,1,0:T(8,128)(2,1)S(1)}, u32[]{:S(2)}, u32[]{:S(2)}) collective-permute-start(bf16[2,128,128]{2,1,0:T(8,128)(2,1)S(1)} %get-tuple-element.61), channel_id=1, source_target_pairs={{0,8},{1,9},{2,10},{3,11},{4,12},{5,13},{6,14},{7,15},{8,0},{9,1},... | collective-permute-start | bytes 196616 | tf_op jit(solution)/shard_map/ppermute | solution.py:287
  45.0 1.1 %collective-permute-start.12 = (bf16[2,128,128]{2,1,0:T(8,128)(2,1)S(1)}, bf16[2,128,128]{2,1,0:T(8,128)(2,1)S(1)}, u32[]{:S(2)}, u32[]{:S(2)}) collective-permute-start(bf16[2,128,128]{2,1,0:T(8,128)(2,1)S(1)} %get-tuple-element.62), channel_id=1, source_target_pairs={{0,12},{1,13},{2,14},{3,15},{4,8},{5,9},{6,10},{7,11},{8,4},{9,5},... | collective-permute-start | bytes 196616 | tf_op jit(solution)/shard_map/ppermute | solution.py:287
  46.5 2.4 %collective-permute-start.14 = (bf16[2,128,128]{2,1,0:T(8,128)(2,1)S(1)}, bf16[2,128,128]{2,1,0:T(8,128)(2,1)S(1)}, u32[]{:S(2)}, u32[]{:S(2)}) collective-permute-start(bf16[2,128,128]{2,1,0:T(8,128)(2,1)S(1)} %get-tuple-element.66), channel_id=1, source_target_pairs={{0,4},{1,5},{2,6},{3,7},{4,0},{5,1},{6,2},{7,3},{8,12},{9,13},{10,... | collective-permute-start | bytes 196616 | tf_op jit(solution)/shard_map/ppermute | solution.py:287
  49.4 3.1 %collective-permute-done.11.refs_2_ = bf16[2,128,128]{2,1,0:T(8,128)(2,1)S(1)} collective-permute-done((bf16[2,128,128]{2,1,0:T(8,128)(2,1)S(1)}, bf16[2,128,128]{2,1,0:T(8,128)(2,1)S(1)}, u32[]{:S(2)}, u32[]{:S(2)}) %collective-permute-start.11) | collective-permute-done | bytes 65568 | tf_op jit(solution)/shard_map/ppermute | solution.py:287
  52.5 1.6 %collective-permute-start.16 = (bf16[2,128,128]{2,1,0:T(8,128)(2,1)S(1)}, bf16[2,128,128]{2,1,0:T(8,128)(2,1)S(1)}, u32[]{:S(2)}, u32[]{:S(2)}) collective-permute-start(bf16[2,128,128]{2,1,0:T(8,128)(2,1)S(1)} %get-tuple-element.68), channel_id=1, source_target_pairs={{0,12},{1,13},{2,14},{3,15},{4,8},{5,9},{6,10},{7,11},{8,4},{9,5},... | collective-permute-start | bytes 196616 | tf_op jit(solution)/shard_map/ppermute | solution.py:287
  55.0 3.6 %collective-permute-done.16.refs_3_ = bf16[2,128,128]{2,1,0:T(8,128)(2,1)S(1)} collective-permute-done((bf16[2,128,128]{2,1,0:T(8,128)(2,1)S(1)}, bf16[2,128,128]{2,1,0:T(8,128)(2,1)S(1)}, u32[]{:S(2)}, u32[]{:S(2)}) %collective-permute-start.16) | collective-permute-done | bytes 65568 | tf_op jit(solution)/shard_map/ppermute | solution.py:287
  58.6 1.2 %shard_map.74 = (bf16[4,128,128]{2,1,0:T(8,128)(2,1)S(1)}, f32[512,256]{1,0:T(8,128)S(1)}, f32[128,256]{1,0:T(8,128)S(1)}) custom-call(s32[2]{0:T(128)S(1)} %pad_add_fusion.index_ref, bf16[2,128,128]{2,1,0:T(8,128)(2,1)S(1)} %get-tuple-element.65.refs_0_, bf16[2,128,128]{2,1,0:T(8,128)(2,1)S(1)} %collective-permute-done.14.refs_1_, ...), custom_call_target="tpu_custom_call" | custom-call | flops 402653184 | bytes 1572864 | tf_op jit(solution)/shard_map/pallas_call | solution.py:261
  59.8 1.2 %shard_map.75 = (bf16[2,128,128]{2,1,0:T(8,128)(2,1)S(1)}, bf16[4,128,128]{2,1,0:T(8,128)(2,1)S(1)}, bf16[2,128,128]{2,1,0:T(8,128)(2,1)S(1)}) custom-call(s32[2]{0:T(128)S(1)} %pad_add_fusion.index_ref, bf16[128,128]{1,0:T(8,128)(2,1)S(1)} %get-tuple-element.57.refs_0_, bf16[128,128]{1,0:T(8,128)(2,1)S(1)} %collective-permute-done.7.refs_1_, ...), custom_call_target="tpu_custom_call" | custom-call | flops 536870912 | bytes 917504 | tf_op jit(solution)/shard_map/pallas_call | solution.py:261
  61.1 1.2 %collective-permute-done.17.refs_1_ = bf16[2,128,128]{2,1,0:T(8,128)(2,1)S(1)} collective-permute-done((bf16[2,128,128]{2,1,0:T(8,128)(2,1)S(1)}, bf16[2,128,128]{2,1,0:T(8,128)(2,1)S(1)}, u32[]{:S(2)}, u32[]{:S(2)}) %collective-permute-start.17) | collective-permute-done | bytes 65568 | tf_op jit(solution)/shard_map/ppermute | solution.py:287
  63.0 2.2 %collective-permute-start.23 = (bf16[2,128,128]{2,1,0:T(8,128)(2,1)S(1)}, bf16[2,128,128]{2,1,0:T(8,128)(2,1)S(1)}, u32[]{:S(2)}, u32[]{:S(2)}) collective-permute-start(bf16[2,128,128]{2,1,0:T(8,128)(2,1)S(1)} %get-tuple-element.84), channel_id=1, source_target_pairs={{0,8},{1,9},{2,10},{3,11},{4,12},{5,13},{6,14},{7,15},{8,0},{9,1},... | collective-permute-start | bytes 196616 | tf_op jit(solution)/shard_map/ppermute | solution.py:287
  65.2 2.2 %collective-permute-start.24 = (bf16[2,128,128]{2,1,0:T(8,128)(2,1)S(1)}, bf16[2,128,128]{2,1,0:T(8,128)(2,1)S(1)}, u32[]{:S(2)}, u32[]{:S(2)}) collective-permute-start(bf16[2,128,128]{2,1,0:T(8,128)(2,1)S(1)} %get-tuple-element.85), channel_id=1, source_target_pairs={{0,12},{1,13},{2,14},{3,15},{4,8},{5,9},{6,10},{7,11},{8,4},{9,5},... | collective-permute-start | bytes 196616 | tf_op jit(solution)/shard_map/ppermute | solution.py:287
  68.2 3.5 %collective-permute-done.23.refs_4_ = bf16[2,128,128]{2,1,0:T(8,128)(2,1)S(1)} collective-permute-done((bf16[2,128,128]{2,1,0:T(8,128)(2,1)S(1)}, bf16[2,128,128]{2,1,0:T(8,128)(2,1)S(1)}, u32[]{:S(2)}, u32[]{:S(2)}) %collective-permute-start.23) | collective-permute-done | bytes 65568 | tf_op jit(solution)/shard_map/ppermute | solution.py:287
  72.4 1.1 %shard_map.76 = (bf16[3,128,128]{2,1,0:T(8,128)(2,1)S(1)}, bf16[3,128,128]{2,1,0:T(8,128)(2,1)S(1)}, bf16[3,128,128]{2,1,0:T(8,128)(2,1)S(1)}, bf16[3,128,128]{2,1,0:T(8,128)(2,1)S(1)}) custom-call(s32[2]{0:T(128)S(1)} %pad_add_fusion.index_ref, bf16[2,128,128]{2,1,0:T(8,128)(2,1)S(1)} %get-tuple-element.73.refs_0_, ...), custom_call_target="tpu_custom_call" | custom-call | flops 268435456 | bytes 1441792 | tf_op jit(solution)/shard_map/pallas_call | solution.py:261
  73.5 1.3 %collective-permute-start.18 = (bf16[3,128,128]{2,1,0:T(8,128)(2,1)S(1)}, bf16[3,128,128]{2,1,0:T(8,128)(2,1)S(1)}, u32[]{:S(2)}, u32[]{:S(2)}) collective-permute-start(bf16[3,128,128]{2,1,0:T(8,128)(2,1)S(1)} %get-tuple-element.78), channel_id=1, source_target_pairs={{0,4},{1,5},{2,6},{3,7},{4,0},{5,1},{6,2},{7,3},{8,12},{9,13},{10,... | collective-permute-start | bytes 294920 | tf_op jit(solution)/shard_map/ppermute | solution.py:287
  74.8 1.2 %collective-permute-start.19 = (bf16[3,128,128]{2,1,0:T(8,128)(2,1)S(1)}, bf16[3,128,128]{2,1,0:T(8,128)(2,1)S(1)}, u32[]{:S(2)}, u32[]{:S(2)}) collective-permute-start(bf16[3,128,128]{2,1,0:T(8,128)(2,1)S(1)} %get-tuple-element.79), channel_id=1, source_target_pairs={{0,8},{1,9},{2,10},{3,11},{4,12},{5,13},{6,14},{7,15},{8,0},{9,1},... | collective-permute-start | bytes 294920 | tf_op jit(solution)/shard_map/ppermute | solution.py:287
  76.1 1.9 %collective-permute-start.20 = (bf16[3,128,128]{2,1,0:T(8,128)(2,1)S(1)}, bf16[3,128,128]{2,1,0:T(8,128)(2,1)S(1)}, u32[]{:S(2)}, u32[]{:S(2)}) collective-permute-start(bf16[3,128,128]{2,1,0:T(8,128)(2,1)S(1)} %get-tuple-element.80), channel_id=1, source_target_pairs={{0,12},{1,13},{2,14},{3,15},{4,8},{5,9},{6,10},{7,11},{8,4},{9,5},... | collective-permute-start | bytes 294920 | tf_op jit(solution)/shard_map/ppermute | solution.py:287
  78.0 1.2 %collective-permute-done.18.refs_1_.refs_3_ = bf16[3,128,128]{2,1,0:T(8,128)(2,1)S(1)} collective-permute-done((bf16[3,128,128]{2,1,0:T(8,128)(2,1)S(1)}, bf16[3,128,128]{2,1,0:T(8,128)(2,1)S(1)}, u32[]{:S(2)}, u32[]{:S(2)}) %collective-permute-start.18) | collective-permute-done | bytes 98336 | tf_op jit(solution)/shard_map/ppermute | solution.py:287
  79.2 5.3 %collective-permute-done.19.refs_2_.refs_4_ = bf16[3,128,128]{2,1,0:T(8,128)(2,1)S(1)} collective-permute-done((bf16[3,128,128]{2,1,0:T(8,128)(2,1)S(1)}, bf16[3,128,128]{2,1,0:T(8,128)(2,1)S(1)}, u32[]{:S(2)}, u32[]{:S(2)}) %collective-permute-start.19) | collective-permute-done | bytes 98336 | tf_op jit(solution)/shard_map/ppermute | solution.py:287
  85.2 1.7 %collective-permute-start.26 = (bf16[1024,128]{1,0:T(8,128)(2,1)S(1)}, bf16[1024,128]{1,0:T(8,128)(2,1)S(1)}, u32[]{:S(2)}, u32[]{:S(2)}) collective-permute-start(bf16[1024,128]{1,0:T(8,128)(2,1)S(1)} %shard_map.81), channel_id=1, source_target_pairs={{0,4},{1,12},{2,0},{3,8},{4,1},{5,9},{6,5},{7,13},{8,2},{9,10},{10... | collective-permute-start | bytes 786440 | tf_op jit(solution)/shard_map/ppermute | solution.py:287
  86.9 1.2 %shard_map.77 = bf16[512,128]{1,0:T(8,128)(2,1)} custom-call(s32[2]{0:T(128)S(1)} %pad_add_fusion.index_ref, bf16[3,128,128]{2,1,0:T(8,128)(2,1)S(1)} %get-tuple-element.77.refs_0_.refs_2_, bf16[3,128,128]{2,1,0:T(8,128)(2,1)S(1)} %collective-permute-done.18.refs_1_.refs_3_, bf16[3,128,128]{2,1,0:T(8,128)(2,1)S(1)} %collective-permute-done.19.refs_2_.refs_4_, ...), custom_call_target="tpu_custom_call" | custom-call | bytes 524288 | tf_op jit(solution)/shard_map/pallas_call | solution.py:261
  88.1 4.9 %collective-permute-done.26 = bf16[1024,128]{1,0:T(8,128)(2,1)S(1)} collective-permute-done((bf16[1024,128]{1,0:T(8,128)(2,1)S(1)}, bf16[1024,128]{1,0:T(8,128)(2,1)S(1)}, u32[]{:S(2)}, u32[]{:S(2)}) %collective-permute-start.26) | collective-permute-done | bytes 262176 | tf_op jit(solution)/shard_map/ppermute | solution.py:287
  (54 shorter events, 11.5 us)
Async XLA Ops:
  1.3 0.9 copy-start.2
  1.3 1.0 %copy-start.3 = (bf16[512,128]{1,0:T(8,128)(2,1)S(1)}, bf16[512,128]{1,0:T(8,128)(2,1)}, u32[]{:S(2)}) copy-start(bf16[512,128]{1,0:T(8,128)(2,1)} %cotangent_ref.1) | copy-start | bytes 393220
  2.3 1.2 %copy-start = (bf16[1024,512]{1,0:T(8,128)(2,1)S(1)}, bf16[1024,512]{1,0:T(8,128)(2,1)}, u32[]{:S(2)}) copy-start(bf16[1024,512]{1,0:T(8,128)(2,1)} %given_ref.2) | copy-start | bytes 3145732
  4.5 1.0 %copy-start.1 = (bf16[1024,128]{1,0:T(8,128)(2,1)S(1)}, bf16[1024,128]{1,0:T(8,128)(2,1)}, u32[]{:S(2)}) copy-start(bf16[1024,128]{1,0:T(8,128)(2,1)} %given_ref.3) | copy-start | bytes 786436
  4.5 30.6 %collective-permute-start = (bf16[512,1024]{1,0:T(8,128)(2,1)S(1)}, bf16[512,1024]{1,0:T(8,128)(2,1)S(1)}, u32[]{:S(2)}, u32[]{:S(2)}) collective-permute-start(bf16[512,1024]{1,0:T(8,128)(2,1)S(1)} %get-tuple-element.50.refs_0_), channel_id=1, source_target_pairs={{0,1},{1,0},{2,3},{3,2},{4,5},{5,4},{6,7},{7,6},{8,9},{9,8},{10,11... | collective-permute-start | bytes 3145736 | tf_op jit(solution)/shard_map/ppermute | solution.py:287
  5.1 62.3 %collective-permute-start.21 = (bf16[1024,512]{1,0:T(8,128)(2,1)S(1)}, bf16[1024,512]{1,0:T(8,128)(2,1)S(1)}, u32[]{:S(2)}, u32[]{:S(2)}) collective-permute-start(bf16[1024,512]{1,0:T(8,128)(2,1)S(1)} %get-tuple-element.81.refs_0_), channel_id=1, source_target_pairs={{0,1},{1,0},{2,3},{3,2},{4,5},{5,4},{6,7},{7,6},{8,9},{9,8},{10,11... | collective-permute-start | bytes 3145736 | tf_op jit(solution)/shard_map/ppermute | solution.py:287
  5.8 15.3 %collective-permute-start.1 = (bf16[896,128]{1,0:T(8,128)(2,1)S(1)}, bf16[896,128]{1,0:T(8,128)(2,1)S(1)}, u32[]{:S(2)}, u32[]{:S(2)}) collective-permute-start(bf16[896,128]{1,0:T(8,128)(2,1)S(1)} %get-tuple-element.51), channel_id=1, source_target_pairs={{0,2},{1,6},{2,10},{3,14},{4,3},{5,7},{6,11},{7,15},{8,0},{9,4},{1... | collective-permute-start | bytes 688136 | tf_op jit(solution)/shard_map/ppermute | solution.py:287
  21.1 19.8 %collective-permute-start.8 = (bf16[896,128]{1,0:T(8,128)(2,1)S(1)}, bf16[896,128]{1,0:T(8,128)(2,1)S(1)}, u32[]{:S(2)}, u32[]{:S(2)}) collective-permute-start(bf16[896,128]{1,0:T(8,128)(2,1)S(1)} %collective-permute-done.1.refs_2_), channel_id=1, source_target_pairs={{0,2},{1,3},{2,0},{3,1},{4,6},{5,7},{6,4},{7,5},{8,10},{9,11},{10,... | collective-permute-start | bytes 688136 | tf_op jit(solution)/shard_map/ppermute | solution.py:287
  21.1 6.4 %collective-permute-start.2 = (bf16[128,128]{1,0:T(8,128)(2,1)S(1)}, bf16[128,128]{1,0:T(8,128)(2,1)S(1)}, u32[]{:S(2)}, u32[]{:S(2)}) collective-permute-start(bf16[128,128]{1,0:T(8,128)(2,1)S(1)} %get-tuple-element.52), channel_id=1, source_target_pairs={{0,2},{1,3},{2,0},{3,1},{4,6},{5,7},{6,4},{7,5},{8,10},{9,11},{10,... | collective-permute-start | bytes 98312 | tf_op jit(solution)/shard_map/ppermute | solution.py:287
  27.5 7.6 %collective-permute-start.3 = (bf16[128,128]{1,0:T(8,128)(2,1)S(1)}, bf16[128,128]{1,0:T(8,128)(2,1)S(1)}, u32[]{:S(2)}, u32[]{:S(2)}) collective-permute-start(bf16[128,128]{1,0:T(8,128)(2,1)S(1)} %collective-permute-done.2), channel_id=1, source_target_pairs={{0,10},{1,14},{2,2},{3,6},{4,11},{5,15},{6,3},{7,7},{8,8},{9,12},{... | collective-permute-start | bytes 98312 | tf_op jit(solution)/shard_map/ppermute | solution.py:287
  35.8 6.8 %collective-permute-start.4 = (bf16[2,128,128]{2,1,0:T(8,128)(2,1)S(1)}, bf16[2,128,128]{2,1,0:T(8,128)(2,1)S(1)}, u32[]{:S(2)}, u32[]{:S(2)}) collective-permute-start(bf16[2,128,128]{2,1,0:T(8,128)(2,1)S(1)} %get-tuple-element.54), channel_id=1, source_target_pairs={{0,4},{1,5},{2,6},{3,7},{4,0},{5,1},{6,2},{7,3},{8,12},{9,13},{10,... | collective-permute-start | bytes 196616 | tf_op jit(solution)/shard_map/ppermute | solution.py:287
  35.9 4.0 %collective-permute-start.9 = (bf16[128,128]{1,0:T(8,128)(2,1)S(1)}, bf16[128,128]{1,0:T(8,128)(2,1)S(1)}, u32[]{:S(2)}, u32[]{:S(2)}) collective-permute-start(bf16[128,128]{1,0:T(8,128)(2,1)S(1)} %collective-permute-done.3.refs_3_), channel_id=1, source_target_pairs={{0,2},{1,3},{2,0},{3,1},{4,6},{5,7},{6,4},{7,5},{8,10},{9,11},{10,... | collective-permute-start | bytes 98312 | tf_op jit(solution)/shard_map/ppermute | solution.py:287
  36.6 8.4 %collective-permute-start.5 = (bf16[2,128,128]{2,1,0:T(8,128)(2,1)S(1)}, bf16[2,128,128]{2,1,0:T(8,128)(2,1)S(1)}, u32[]{:S(2)}, u32[]{:S(2)}) collective-permute-start(bf16[2,128,128]{2,1,0:T(8,128)(2,1)S(1)} %get-tuple-element.55), channel_id=1, source_target_pairs={{0,8},{1,9},{2,10},{3,11},{4,12},{5,13},{6,14},{7,15},{8,0},{9,1},... | collective-permute-start | bytes 196616 | tf_op jit(solution)/shard_map/ppermute | solution.py:287
  39.9 6.6 %collective-permute-start.6 = (bf16[2,128,128]{2,1,0:T(8,128)(2,1)S(1)}, bf16[2,128,128]{2,1,0:T(8,128)(2,1)S(1)}, u32[]{:S(2)}, u32[]{:S(2)}) collective-permute-start(bf16[2,128,128]{2,1,0:T(8,128)(2,1)S(1)} %get-tuple-element.56), channel_id=1, source_target_pairs={{0,12},{1,13},{2,14},{3,15},{4,8},{5,9},{6,10},{7,11},{8,4},{9,5},... | collective-permute-start | bytes 196616 | tf_op jit(solution)/shard_map/ppermute | solution.py:287
  41.7 7.2 %collective-permute-start.10 = (bf16[2,128,128]{2,1,0:T(8,128)(2,1)S(1)}, bf16[2,128,128]{2,1,0:T(8,128)(2,1)S(1)}, u32[]{:S(2)}, u32[]{:S(2)}) collective-permute-start(bf16[2,128,128]{2,1,0:T(8,128)(2,1)S(1)} %get-tuple-element.60), channel_id=1, source_target_pairs={{0,4},{1,5},{2,6},{3,7},{4,0},{5,1},{6,2},{7,3},{8,12},{9,13},{10,... | collective-permute-start | bytes 196616 | tf_op jit(solution)/shard_map/ppermute | solution.py:287
  42.6 9.9 %collective-permute-start.11 = (bf16[2,128,128]{2,1,0:T(8,128)(2,1)S(1)}, bf16[2,128,128]{2,1,0:T(8,128)(2,1)S(1)}, u32[]{:S(2)}, u32[]{:S(2)}) collective-permute-start(bf16[2,128,128]{2,1,0:T(8,128)(2,1)S(1)} %get-tuple-element.61), channel_id=1, source_target_pairs={{0,8},{1,9},{2,10},{3,11},{4,12},{5,13},{6,14},{7,15},{8,0},{9,1},... | collective-permute-start | bytes 196616 | tf_op jit(solution)/shard_map/ppermute | solution.py:287
  45.0 9.2 %collective-permute-start.12 = (bf16[2,128,128]{2,1,0:T(8,128)(2,1)S(1)}, bf16[2,128,128]{2,1,0:T(8,128)(2,1)S(1)}, u32[]{:S(2)}, u32[]{:S(2)}) collective-permute-start(bf16[2,128,128]{2,1,0:T(8,128)(2,1)S(1)} %get-tuple-element.62), channel_id=1, source_target_pairs={{0,12},{1,13},{2,14},{3,15},{4,8},{5,9},{6,10},{7,11},{8,4},{9,5},... | collective-permute-start | bytes 196616 | tf_op jit(solution)/shard_map/ppermute | solution.py:287
  46.5 7.8 %collective-permute-start.14 = (bf16[2,128,128]{2,1,0:T(8,128)(2,1)S(1)}, bf16[2,128,128]{2,1,0:T(8,128)(2,1)S(1)}, u32[]{:S(2)}, u32[]{:S(2)}) collective-permute-start(bf16[2,128,128]{2,1,0:T(8,128)(2,1)S(1)} %get-tuple-element.66), channel_id=1, source_target_pairs={{0,4},{1,5},{2,6},{3,7},{4,0},{5,1},{6,2},{7,3},{8,12},{9,13},{10,... | collective-permute-start | bytes 196616 | tf_op jit(solution)/shard_map/ppermute | solution.py:287
  48.9 6.1 %collective-permute-start.15 = (bf16[2,128,128]{2,1,0:T(8,128)(2,1)S(1)}, bf16[2,128,128]{2,1,0:T(8,128)(2,1)S(1)}, u32[]{:S(2)}, u32[]{:S(2)}) collective-permute-start(bf16[2,128,128]{2,1,0:T(8,128)(2,1)S(1)} %get-tuple-element.67), channel_id=1, source_target_pairs={{0,8},{1,9},{2,10},{3,11},{4,12},{5,13},{6,14},{7,15},{8,0},{9,1},... | collective-permute-start | bytes 196616 | tf_op jit(solution)/shard_map/ppermute | solution.py:287
  52.5 6.1 %collective-permute-start.16 = (bf16[2,128,128]{2,1,0:T(8,128)(2,1)S(1)}, bf16[2,128,128]{2,1,0:T(8,128)(2,1)S(1)}, u32[]{:S(2)}, u32[]{:S(2)}) collective-permute-start(bf16[2,128,128]{2,1,0:T(8,128)(2,1)S(1)} %get-tuple-element.68), channel_id=1, source_target_pairs={{0,12},{1,13},{2,14},{3,15},{4,8},{5,9},{6,10},{7,11},{8,4},{9,5},... | collective-permute-start | bytes 196616 | tf_op jit(solution)/shard_map/ppermute | solution.py:287
  54.2 4.4 %copy-start.4 = (f32[512,128]{1,0:T(8,128)S(1)}, f32[512,128]{1,0:T(8,128)}, u32[]{:S(2)}) copy-start(f32[512,128]{1,0:T(8,128)} %refs_4_.1) | copy-start | bytes 786436
  54.2 5.6 %collective-permute-start.7 = (bf16[128,128]{1,0:T(8,128)(2,1)S(1)}, bf16[128,128]{1,0:T(8,128)(2,1)S(1)}, u32[]{:S(2)}, u32[]{:S(2)}) collective-permute-start(bf16[128,128]{1,0:T(8,128)(2,1)S(1)} %get-tuple-element.58), channel_id=1, source_target_pairs={{0,1},{1,0},{2,3},{3,2},{4,5},{5,4},{6,7},{7,6},{8,9},{9,8},{10,11... | collective-permute-start | bytes 98312 | tf_op jit(solution)/shard_map/ppermute | solution.py:287
  54.3 5.5 %collective-permute-start.13 = (bf16[128,128]{1,0:T(8,128)(2,1)S(1)}, bf16[128,128]{1,0:T(8,128)(2,1)S(1)}, u32[]{:S(2)}, u32[]{:S(2)}) collective-permute-start(bf16[128,128]{1,0:T(8,128)(2,1)S(1)} %get-tuple-element.64), channel_id=1, source_target_pairs={{0,1},{1,0},{2,3},{3,2},{4,5},{5,4},{6,7},{7,6},{8,9},{9,8},{10,11... | collective-permute-start | bytes 98312 | tf_op jit(solution)/shard_map/ppermute | solution.py:287
  61.0 1.3 %collective-permute-start.17 = (bf16[2,128,128]{2,1,0:T(8,128)(2,1)S(1)}, bf16[2,128,128]{2,1,0:T(8,128)(2,1)S(1)}, u32[]{:S(2)}, u32[]{:S(2)}) collective-permute-start(bf16[2,128,128]{2,1,0:T(8,128)(2,1)S(1)} %get-tuple-element.74), channel_id=1, source_target_pairs={{0,1},{1,0},{2,3},{3,2},{4,5},{5,4},{6,7},{7,6},{8,9},{9,8},{10,11... | collective-permute-start | bytes 196616 | tf_op jit(solution)/shard_map/ppermute | solution.py:287
  62.9 5.2 %collective-permute-start.22 = (bf16[2,128,128]{2,1,0:T(8,128)(2,1)S(1)}, bf16[2,128,128]{2,1,0:T(8,128)(2,1)S(1)}, u32[]{:S(2)}, u32[]{:S(2)}) collective-permute-start(bf16[2,128,128]{2,1,0:T(8,128)(2,1)S(1)} %get-tuple-element.83), channel_id=1, source_target_pairs={{0,4},{1,5},{2,6},{3,7},{4,0},{5,1},{6,2},{7,3},{8,12},{9,13},{10,... | collective-permute-start | bytes 196616 | tf_op jit(solution)/shard_map/ppermute | solution.py:287
  63.0 8.6 %collective-permute-start.23 = (bf16[2,128,128]{2,1,0:T(8,128)(2,1)S(1)}, bf16[2,128,128]{2,1,0:T(8,128)(2,1)S(1)}, u32[]{:S(2)}, u32[]{:S(2)}) collective-permute-start(bf16[2,128,128]{2,1,0:T(8,128)(2,1)S(1)} %get-tuple-element.84), channel_id=1, source_target_pairs={{0,8},{1,9},{2,10},{3,11},{4,12},{5,13},{6,14},{7,15},{8,0},{9,1},... | collective-permute-start | bytes 196616 | tf_op jit(solution)/shard_map/ppermute | solution.py:287
  65.2 6.5 %collective-permute-start.24 = (bf16[2,128,128]{2,1,0:T(8,128)(2,1)S(1)}, bf16[2,128,128]{2,1,0:T(8,128)(2,1)S(1)}, u32[]{:S(2)}, u32[]{:S(2)}) collective-permute-start(bf16[2,128,128]{2,1,0:T(8,128)(2,1)S(1)} %get-tuple-element.85), channel_id=1, source_target_pairs={{0,12},{1,13},{2,14},{3,15},{4,8},{5,9},{6,10},{7,11},{8,4},{9,5},... | collective-permute-start | bytes 196616 | tf_op jit(solution)/shard_map/ppermute | solution.py:287
  72.4 12.8 %collective-permute-start.25 = (bf16[1024,128]{1,0:T(8,128)(2,1)S(1)}, bf16[1024,128]{1,0:T(8,128)(2,1)S(1)}, u32[]{:S(2)}, u32[]{:S(2)}) collective-permute-start(bf16[1024,128]{1,0:T(8,128)(2,1)S(1)} %shard_map.80), channel_id=1, source_target_pairs={{0,2},{1,3},{2,0},{3,1},{4,6},{5,7},{6,4},{7,5},{8,10},{9,11},{10,... | collective-permute-start | bytes 786440 | tf_op jit(solution)/shard_map/ppermute | solution.py:287
  73.5 5.6 %collective-permute-start.18 = (bf16[3,128,128]{2,1,0:T(8,128)(2,1)S(1)}, bf16[3,128,128]{2,1,0:T(8,128)(2,1)S(1)}, u32[]{:S(2)}, u32[]{:S(2)}) collective-permute-start(bf16[3,128,128]{2,1,0:T(8,128)(2,1)S(1)} %get-tuple-element.78), channel_id=1, source_target_pairs={{0,4},{1,5},{2,6},{3,7},{4,0},{5,1},{6,2},{7,3},{8,12},{9,13},{10,... | collective-permute-start | bytes 294920 | tf_op jit(solution)/shard_map/ppermute | solution.py:287
  74.8 9.6 %collective-permute-start.19 = (bf16[3,128,128]{2,1,0:T(8,128)(2,1)S(1)}, bf16[3,128,128]{2,1,0:T(8,128)(2,1)S(1)}, u32[]{:S(2)}, u32[]{:S(2)}) collective-permute-start(bf16[3,128,128]{2,1,0:T(8,128)(2,1)S(1)} %get-tuple-element.79), channel_id=1, source_target_pairs={{0,8},{1,9},{2,10},{3,11},{4,12},{5,13},{6,14},{7,15},{8,0},{9,1},... | collective-permute-start | bytes 294920 | tf_op jit(solution)/shard_map/ppermute | solution.py:287
  76.1 8.4 %collective-permute-start.20 = (bf16[3,128,128]{2,1,0:T(8,128)(2,1)S(1)}, bf16[3,128,128]{2,1,0:T(8,128)(2,1)S(1)}, u32[]{:S(2)}, u32[]{:S(2)}) collective-permute-start(bf16[3,128,128]{2,1,0:T(8,128)(2,1)S(1)} %get-tuple-element.80), channel_id=1, source_target_pairs={{0,12},{1,13},{2,14},{3,15},{4,8},{5,9},{6,10},{7,11},{8,4},{9,5},... | collective-permute-start | bytes 294920 | tf_op jit(solution)/shard_map/ppermute | solution.py:287
  85.2 7.8 %collective-permute-start.26 = (bf16[1024,128]{1,0:T(8,128)(2,1)S(1)}, bf16[1024,128]{1,0:T(8,128)(2,1)S(1)}, u32[]{:S(2)}, u32[]{:S(2)}) collective-permute-start(bf16[1024,128]{1,0:T(8,128)(2,1)S(1)} %shard_map.81), channel_id=1, source_target_pairs={{0,4},{1,12},{2,0},{3,8},{4,1},{5,9},{6,5},{7,13},{8,2},{9,10},{10... | collective-permute-start | bytes 786440 | tf_op jit(solution)/shard_map/ppermute | solution.py:287
